TPU v7x, 32 devices: a whole 2x2x4 slice. The times are simulated.
32 devices in a mesh: dp: 4 (over y, x), ctx: 2 (over core), tp: 4 (over z).
Axes of the slice: x: 2, y: 2, z: 4, core: 2. Of those that a mesh axis runs over, the one named last changes fastest.
Arguments:
- tokens: bfloat16 [16, 2048, 1024], P('dp', 'ctx', 'tp'), may hold values from -6 to 6
- cotangent: bfloat16 [16, 2048, 1024], P('dp', 'ctx'), may hold values from -6 to 6
- prefix: int32 [16], P('dp'), may hold values from 204 to 1024, as said below
- w_query: bfloat16 [1024, 1024], P(('dp', 'ctx'), 'tp'), may hold values from -0.1875 to 0.1875
- w_key: bfloat16 [1024, 1024], P(('dp', 'ctx'), 'tp'), may hold values from -0.1875 to 0.1875
- w_value: bfloat16 [1024, 1024], P(('dp', 'ctx'), 'tp'), may hold values from -0.1875 to 0.1875
- w_out: bfloat16 [1024, 1024], P('tp', ('dp', 'ctx')), may hold values from -1.5 to 1.5
- w_up: bfloat16 [1024, 4096], P(('dp', 'ctx'), 'tp'), may hold values from -0.1875 to 0.1875
- w_down: bfloat16 [4096, 1024], P('tp', ('dp', 'ctx')), may hold values from -0.09375 to 0.09375
- state_query: bfloat16 [512, 1024], P(('dp', 'ctx'), 'tp'), may hold values from -6 to 6
- state_init: bfloat16 [512, 1024], P(('dp', 'ctx'), 'tp'), may hold values from -6 to 6
- gain_attn: bfloat16 [8, 128], P('tp', ('dp', 'ctx')), may hold values from 0.5 to 1.5
- gain_mlp: bfloat16 [8, 128], P('tp', ('dp', 'ctx')), may hold values from 0.5 to 1.5
- bias_table: bfloat16 [8, 32], P('tp', ('dp', 'ctx')), may hold values from -3 to 3
- gate_bias: bfloat16 [8, 128], P('tp', ('dp', 'ctx')), may hold values from -2 to 4
- state_key: bfloat16 [8, 128, 128], P('tp', ('dp', 'ctx')), may hold values from -0.5 to 0.5
- state_value: bfloat16 [8, 128, 128], P('tp', ('dp', 'ctx')), may hold values from -0.5 to 0.5
Outputs:
- output: bfloat16 [16, 2048, 1024], P('dp', 'ctx', 'tp')
- grad_tokens: bfloat16 [16, 2048, 1024], P('dp', 'ctx', 'tp')
- grad_w_query: float32 [1024, 1024], P(('dp', 'ctx'), 'tp')
- grad_w_key: float32 [1024, 1024], P(('dp', 'ctx'), 'tp')
- grad_w_value: float32 [1024, 1024], P(('dp', 'ctx'), 'tp')
- grad_w_out: float32 [1024, 1024], P('tp', ('dp', 'ctx'))
- grad_w_up: float32 [1024, 4096], P(('dp', 'ctx'), 'tp')
- grad_w_down: float32 [4096, 1024], P('tp', ('dp', 'ctx'))
- grad_state_query: float32 [512, 1024], P(('dp', 'ctx'), 'tp')
- grad_state_init: float32 [512, 1024], P(('dp', 'ctx'), 'tp')
- grad_gain_attn: float32 [8, 128], P('tp', ('dp', 'ctx'))
- grad_gain_mlp: float32 [8, 128], P('tp', ('dp', 'ctx'))
- grad_bias_table: float32 [8, 32], P('tp', ('dp', 'ctx'))
- grad_gate_bias: float32 [8, 128], P('tp', ('dp', 'ctx'))
- grad_state_key: float32 [8, 128, 128], P('tp', ('dp', 'ctx'))
- grad_state_value: float32 [8, 128, 128], P('tp', ('dp', 'ctx'))
Inputs may be any that keep to these rules, and one draw needn't show every extreme that they name: `prefix`: tokens of each sequence that attend both ways within the window; some sequence has exactly the least and some exactly the most in every draw.
All inputs are finite; a program needn't handle non-finite values.
Results may differ from a plain program's by a relative error of at most 0.029.
Values may be sent and summed in bfloat16 or wider, within the bound.
No kernel may reach another device: no remote copies, remote signals or barrier semaphores. Data moves between devices by JAX's collectives and lax.ppermute only.
A program may use at most 448 MiB of HBM per device.

v0:
```python
import jax
import jax.numpy as jnp
import numpy as np
from jax import lax
from jax.sharding import PartitionSpec as P

HEAD_SIZE = 128
BLOCK = 512


EPSILON = 1e-06
MASKED = -1e30


def from_behind(value, axis, steps):
    count = lax.axis_size(axis)
    first, last = (max(0, -steps), min(count, count - steps))
    return lax.ppermute(value, axis, [(source, source + steps) for source in range(first, last)])


def prefix_2(array, axis, join, neutral, backward):
    count = lax.axis_size(axis)
    place = lax.axis_index(axis)
    ahead = count - 1 - place if backward else place
    gathered = jax.tree.map(
        lambda a, kind: lax.all_gather(a.astype(kind), axis), array, (jnp.bfloat16, jnp.bfloat16)
    )
    state = jax.tree.map(lambda a, e: jnp.zeros_like(a) + jnp.asarray(e, a.dtype), array, neutral)

    def one(hop, state):
        source = count - 1 - hop if backward else hop
        return join(
            state,
            jax.tree.map(
                lambda a, own: lax.dynamic_index_in_dim(a, source, 0, False).astype(own.dtype),
                gathered,
                array,
            ),
        )

    return lax.fori_loop(0, ahead, one, state)


def bucket_index(block_size):
    query_pos = np.arange(block_size)[:, None] + block_size
    key_pos = np.arange(2 * block_size)[None, :]
    distance = query_pos - key_pos
    upper_part = (distance < 0).astype(np.int32) * 16
    magnitude = np.abs(distance)
    scaled = np.log(np.maximum(magnitude, 1) / 8.0) / np.log(16.0) * 8.0
    far_bucket = np.minimum(8 + np.floor(np.maximum(scaled, 0.0)).astype(np.int32), 15)
    return (upper_part + np.where(magnitude < 8, magnitude, far_bucket)).astype(np.int32)


def norm_forward(features, gain_vector):
    inverse = lax.rsqrt(jnp.mean(features * features, axis=-1, keepdims=True) + EPSILON)
    normed = features * inverse
    return (normed, inverse, (normed * gain_vector).astype(jnp.bfloat16))


def norm_backward(grad_normed, normed, inverse, gain_vector):
    scaled = grad_normed * gain_vector
    grad_in = inverse * (scaled - normed * jnp.mean(scaled * normed, axis=-1, keepdims=True))
    return (grad_in, jnp.sum(grad_normed * normed, axis=0))


def compose(earlier, later_pair):
    return (earlier[0] * later_pair[0], later_pair[0] * earlier[1] + later_pair[1])


def bias_matrix(bias_rows, bucket):
    summed = jnp.zeros((bias_rows.shape[0],) + bucket.shape, jnp.float32)
    for number in range(bias_rows.shape[1]):
        summed = (
            summed
            + bias_rows[:, number][:, None, None] * (bucket == number).astype(jnp.float32)[None]
        )
    return summed


def bias_gradient(grad_matrix, bucket, bucket_count):
    columns = [
        jnp.sum(grad_matrix * (bucket == number).astype(jnp.float32)[None], axis=(1, 2))
        for number in range(bucket_count)
    ]
    return jnp.stack(columns, axis=1)


def body(
    tokens,
    cotangent,
    prefix,
    w_query,
    w_key,
    w_value,
    w_out,
    w_up,
    w_down,
    state_query,
    state_init,
    gain_attn,
    gain_mlp,
    bias_table,
    gate_bias,
    state_key,
    state_value,
):
    (
        query_full,
        key_full,
        value_full,
        out_full,
        up_full,
        down_full,
        squery_full,
        sinit_full,
        gain_one,
        gain_two,
        bias_rows,
        gate_rows,
        state_key_complete,
        svalue_full,
    ) = (
        lax.all_gather(w_query, ("dp", "ctx"), axis=0, tiled=True),
        lax.all_gather(w_key, ("dp", "ctx"), axis=0, tiled=True),
        lax.all_gather(w_value, ("dp", "ctx"), axis=0, tiled=True),
        lax.all_gather(w_out, ("dp", "ctx"), axis=1, tiled=True),
        lax.all_gather(w_up, ("dp", "ctx"), axis=0, tiled=True),
        lax.all_gather(w_down, ("dp", "ctx"), axis=1, tiled=True),
        lax.all_gather(state_query, ("dp", "ctx"), axis=0, tiled=True),
        lax.all_gather(state_init, ("dp", "ctx"), axis=0, tiled=True),
        lax.all_gather(gain_attn, ("dp", "ctx"), axis=1, tiled=True),
        lax.all_gather(gain_mlp, ("dp", "ctx"), axis=1, tiled=True),
        lax.all_gather(bias_table, ("dp", "ctx"), axis=1, tiled=True),
        lax.all_gather(gate_bias, ("dp", "ctx"), axis=1, tiled=True),
        lax.all_gather(state_key, ("dp", "ctx"), axis=1, tiled=True),
        lax.all_gather(state_value, ("dp", "ctx"), axis=1, tiled=True),
    )
    seq_count = tokens.shape[0]
    length = tokens.shape[1]
    shard_width = tokens.shape[2]
    full_width = cotangent.shape[2]
    block_count = length // BLOCK
    row_count = seq_count * length
    local_head_count = bias_rows.shape[0]
    local_width = local_head_count * HEAD_SIZE
    state_slot_count = squery_full.shape[0]
    scores_scale = HEAD_SIZE ** (-0.5)
    local_shape = (seq_count, block_count, BLOCK, local_head_count, HEAD_SIZE)
    element_count = seq_count * block_count
    token_full, gain_one_full = (
        lax.all_gather(tokens, "tp", axis=2, tiled=True),
        lax.all_gather(gain_one, "tp", axis=0, tiled=True),
    )
    gain_one_vec = gain_one_full.reshape(full_width).astype(jnp.float32)
    normed_one, inverse_one, attn_in = norm_forward(
        token_full.reshape(row_count, full_width).astype(jnp.float32), gain_one_vec
    )
    queries = (
        jnp.dot(attn_in, query_full, preferred_element_type=jnp.float32)
        .astype(jnp.bfloat16)
        .reshape(local_shape)
    )
    key_rows = (
        jnp.dot(attn_in, key_full, preferred_element_type=jnp.float32)
        .astype(jnp.bfloat16)
        .reshape(local_shape)
    )
    value_rows = (
        jnp.dot(attn_in, value_full, preferred_element_type=jnp.float32)
        .astype(jnp.bfloat16)
        .reshape(local_shape)
    )
    last_keys, last_values = from_behind((key_rows[:, -1], value_rows[:, -1]), "ctx", 1)
    window_keys = jnp.concatenate(
        [jnp.concatenate([last_keys[:, None], key_rows[:, :-1]], 1), key_rows], 2
    )
    window_values = jnp.concatenate(
        [jnp.concatenate([last_values[:, None], value_rows[:, :-1]], 1), value_rows], 2
    )
    query_heads = squery_full.reshape(state_slot_count, local_head_count, HEAD_SIZE)
    read_scores = (
        jnp.einsum("mhe,sbthe->sbhmt", query_heads, key_rows, preferred_element_type=jnp.float32)
        * scores_scale
    )
    read_peak = jnp.max(read_scores, axis=-1, keepdims=True)
    read_raised = jnp.exp(read_scores - read_peak)
    read_probs = read_raised / jnp.sum(read_raised, axis=-1, keepdims=True)
    read_low = read_probs.astype(jnp.bfloat16)
    contrib = jnp.einsum(
        "sbhmt,sbthe->sbmhe", read_low, value_rows, preferred_element_type=jnp.float32
    )
    contrib = contrib.reshape(seq_count, block_count, state_slot_count, local_width)
    gate_value = jax.nn.sigmoid(gate_rows.reshape(local_width).astype(jnp.float32))
    gate_power = jnp.ones((local_width,), jnp.float32)
    accumulated = jnp.zeros((seq_count, state_slot_count, local_width), jnp.float32)
    for block_index in range(block_count):
        accumulated = gate_value * accumulated + (1.0 - gate_value) * contrib[:, block_index]
        gate_power = gate_power * gate_value
    identity = (jnp.ones((local_width,), jnp.float32), jnp.zeros_like(accumulated))
    lead_power, lead_state = prefix_2((gate_power, accumulated), "ctx", compose, identity, False)
    entry_state = lead_power * sinit_full.astype(jnp.float32) + lead_state
    state_list = [entry_state]
    block_index = 0
    state_list.append(gate_value * state_list[-1] + (1.0 - gate_value) * contrib[:, block_index])
    stacked = jnp.stack(state_list, axis=1)
    state_reduced = stacked.astype(jnp.bfloat16).reshape(
        seq_count, block_count, state_slot_count, local_head_count, HEAD_SIZE
    )
    state_key_rows = jnp.einsum(
        "cazqr,qrx->cazqx", state_reduced, state_key_complete, preferred_element_type=jnp.float32
    ).astype(jnp.bfloat16)
    state_values = jnp.einsum(
        "cazqr,qrx->cazqx", state_reduced, svalue_full, preferred_element_type=jnp.float32
    ).astype(jnp.bfloat16)
    bucket = jnp.asarray(bucket_index(BLOCK))
    bias_full = bias_matrix(bias_rows.astype(jnp.float32), bucket)
    block_ids = lax.axis_index("ctx") * block_count + jnp.arange(block_count, dtype=jnp.int32)
    query_pos = block_ids[:, None] * BLOCK + jnp.arange(BLOCK, dtype=jnp.int32)[None, :]
    key_pos = (block_ids[:, None] - 1) * BLOCK + jnp.arange(2 * BLOCK, dtype=jnp.int32)[None, :]
    causal = (key_pos[:, None, :] >= 0) & (key_pos[:, None, :] <= query_pos[:, :, None])
    in_prefix = (key_pos[None, :, None, :] >= 0) & (
        key_pos[None, :, None, :] < prefix[:, None, None, None]
    )
    permitted_mask = (causal[None] | in_prefix).reshape(element_count, 1, BLOCK, 2 * BLOCK)
    flattened_queries = queries.reshape(element_count, BLOCK, local_head_count, HEAD_SIZE)
    flattened_window_keys = window_keys.reshape(
        element_count, 2 * BLOCK, local_head_count, HEAD_SIZE
    )
    flattened_window_values = window_values.reshape(
        element_count, 2 * BLOCK, local_head_count, HEAD_SIZE
    )
    flattened_state_keys = state_key_rows.reshape(
        element_count, state_slot_count, local_head_count, HEAD_SIZE
    )
    flattened_state_values = state_values.reshape(
        element_count, state_slot_count, local_head_count, HEAD_SIZE
    )

    def block_score_rows(
        block_query_rows, block_window_key_rows, block_state_key_rows, block_permitted_mask
    ):
        window_part = (
            jnp.einsum(
                "ihe,jhe->hij",
                block_query_rows,
                block_window_key_rows,
                preferred_element_type=jnp.float32,
            )
            * scores_scale
            + bias_full
        )
        state_part = (
            jnp.einsum(
                "yat,zat->ayz",
                block_query_rows,
                block_state_key_rows,
                preferred_element_type=jnp.float32,
            )
            * scores_scale
        )
        return (jnp.where(block_permitted_mask, window_part, MASKED), state_part)

    def attend_one_block(element_entry):
        (
            block_query_rows,
            block_window_key_rows,
            block_window_value_rows,
            block_state_key_rows,
            block_state_value_rows,
            block_permitted_mask,
        ) = element_entry
        window_scores, scores_of_state = block_score_rows(
            block_query_rows, block_window_key_rows, block_state_key_rows, block_permitted_mask
        )
        row_peak = jnp.maximum(jnp.max(window_scores, axis=-1), jnp.max(scores_of_state, axis=-1))
        window_raised = jnp.exp(window_scores - row_peak[..., None])
        state_raised = jnp.exp(scores_of_state - row_peak[..., None])
        denominator = jnp.sum(window_raised, axis=-1) + jnp.sum(state_raised, axis=-1)
        log_total = row_peak + jnp.log(denominator)
        window_probs = (window_raised / denominator[..., None]).astype(jnp.bfloat16)
        state_probs = (state_raised / denominator[..., None]).astype(jnp.bfloat16)
        block_out = jnp.einsum(
            "hij,jhe->ihe",
            window_probs,
            block_window_value_rows,
            preferred_element_type=jnp.float32,
        ) + jnp.einsum(
            "wyd,dwg->ywg", state_probs, block_state_value_rows, preferred_element_type=jnp.float32
        )
        return (block_out.astype(jnp.bfloat16), log_total)

    attended_blocks, log_totals = lax.map(
        attend_one_block,
        (
            flattened_queries,
            flattened_window_keys,
            flattened_window_values,
            flattened_state_keys,
            flattened_state_values,
            permitted_mask,
        ),
    )
    attended = attended_blocks.reshape(row_count, local_width)
    attn_part = jnp.dot(attended, out_full, preferred_element_type=jnp.float32).reshape(
        seq_count, length, full_width
    )
    attn_share = lax.psum_scatter(
        attn_part.astype(jnp.bfloat16), "tp", scatter_dimension=2, tiled=True
    ).astype(jnp.float32)
    middle = tokens.astype(jnp.float32) + attn_share
    middle_full, gain_two_full = (
        lax.all_gather(middle.astype(jnp.bfloat16), "tp", axis=2, tiled=True),
        lax.all_gather(gain_two, "tp", axis=0, tiled=True),
    )
    gain_two_vec = gain_two_full.reshape(full_width).astype(jnp.float32)
    normed_two, inverse_two, mlp_in = norm_forward(
        middle_full.reshape(row_count, full_width).astype(jnp.float32), gain_two_vec
    )
    hidden_pre = jnp.dot(mlp_in, up_full, preferred_element_type=jnp.float32)
    hidden = jax.nn.gelu(hidden_pre, approximate=False).astype(jnp.bfloat16)
    mlp_part = jnp.dot(hidden, down_full, preferred_element_type=jnp.float32).reshape(
        seq_count, length, full_width
    )
    mlp_share = lax.psum_scatter(
        mlp_part.astype(jnp.bfloat16), "tp", scatter_dimension=2, tiled=True
    ).astype(jnp.float32)
    output = (middle + mlp_share).astype(jnp.bfloat16)
    grad_out = cotangent.reshape(row_count, full_width)
    grad_hidden = jnp.dot(grad_out, down_full.T, preferred_element_type=jnp.float32)
    grad_down = jnp.dot(hidden.T, grad_out, preferred_element_type=jnp.float32)

    def gelu_exact(pre_values):
        return jax.nn.gelu(pre_values, approximate=False)

    gelu_value, gelu_back = jax.vjp(gelu_exact, hidden_pre)
    grad_pre = gelu_back(grad_hidden)[0].astype(jnp.bfloat16)
    grad_up = jnp.dot(mlp_in.T, grad_pre, preferred_element_type=jnp.float32)
    grad_mlp_in = jnp.dot(grad_pre, up_full.T, preferred_element_type=jnp.float32)
    part_middle, part_gain_two = norm_backward(grad_mlp_in, normed_two, inverse_two, gain_two_vec)
    tp_index = lax.axis_index("tp")
    head_total = full_width // HEAD_SIZE
    summed, gain_two_sum = (
        lax.psum(
            part_middle.reshape(seq_count, length, full_width).astype(jnp.bfloat16), "tp"
        ).astype(jnp.float32),
        lax.psum(part_gain_two.reshape(head_total, HEAD_SIZE).astype(jnp.bfloat16), "tp").astype(
            jnp.float32
        ),
    )
    middle_grad_full = cotangent.astype(jnp.float32) + summed
    middle_grad = lax.dynamic_slice_in_dim(middle_grad_full, tp_index * shard_width, shard_width, 2)
    grad_gain_two = lax.dynamic_slice_in_dim(
        gain_two_sum, tp_index * local_head_count, local_head_count, 0
    )
    middle_grad_low = middle_grad_full.astype(jnp.bfloat16)
    middle_grad_rows = middle_grad_low.reshape(row_count, full_width)
    grad_attended = jnp.dot(
        middle_grad_rows, out_full.T, preferred_element_type=jnp.float32
    ).astype(jnp.bfloat16)
    grad_attended = grad_attended.reshape(element_count, BLOCK, local_head_count, HEAD_SIZE)
    grad_wout = jnp.dot(attended.T, middle_grad_rows, preferred_element_type=jnp.float32)

    def attend_back(bias_sum, element_entry):
        (
            block_query_rows,
            block_window_key_rows,
            block_window_value_rows,
            block_state_key_rows,
            block_state_value_rows,
            block_permitted_mask,
            block_lse,
            block_grad,
        ) = element_entry
        window_again, state_again = block_score_rows(
            block_query_rows, block_window_key_rows, block_state_key_rows, block_permitted_mask
        )
        window_exact = jnp.exp(window_again - block_lse[..., None])
        state_exact = jnp.exp(state_again - block_lse[..., None])
        grad_wprob = jnp.einsum(
            "ihe,jhe->hij", block_grad, block_window_value_rows, preferred_element_type=jnp.float32
        )
        grad_sprob = jnp.einsum(
            "yat,zat->ayz", block_grad, block_state_value_rows, preferred_element_type=jnp.float32
        )
        row_delta = jnp.sum(window_exact * grad_wprob, axis=-1) + jnp.sum(
            state_exact * grad_sprob, axis=-1
        )
        grad_wscore = (window_exact * (grad_wprob - row_delta[..., None])).astype(jnp.bfloat16)
        state_score_gradient = (state_exact * (grad_sprob - row_delta[..., None])).astype(
            jnp.bfloat16
        )
        block_grad_q = scores_scale * (
            jnp.einsum(
                "hij,jhe->ihe",
                grad_wscore,
                block_window_key_rows,
                preferred_element_type=jnp.float32,
            )
            + jnp.einsum(
                "wyd,dwg->ywg",
                state_score_gradient,
                block_state_key_rows,
                preferred_element_type=jnp.float32,
            )
        )
        block_grad_wk = scores_scale * jnp.einsum(
            "hij,ihe->jhe", grad_wscore, block_query_rows, preferred_element_type=jnp.float32
        )
        block_grad_wv = jnp.einsum(
            "hij,ihe->jhe",
            window_exact.astype(jnp.bfloat16),
            block_grad,
            preferred_element_type=jnp.float32,
        )
        block_grad_sk = (
            scores_scale
            * jnp.einsum(
                "him,ihe->mhe",
                state_score_gradient,
                block_query_rows,
                preferred_element_type=jnp.float32,
            )
        ).astype(jnp.bfloat16)
        block_grad_sv = jnp.einsum(
            "him,ihe->mhe",
            state_exact.astype(jnp.bfloat16),
            block_grad,
            preferred_element_type=jnp.float32,
        ).astype(jnp.bfloat16)
        return (
            bias_sum + grad_wscore.astype(jnp.float32),
            (block_grad_q, block_grad_wk, block_grad_wv, block_grad_sk, block_grad_sv),
        )

    bias_start = jnp.zeros((local_head_count, BLOCK, 2 * BLOCK), jnp.float32)
    bias_sum, back_items = lax.scan(
        attend_back,
        bias_start,
        (
            flattened_queries,
            flattened_window_keys,
            flattened_window_values,
            flattened_state_keys,
            flattened_state_values,
            permitted_mask,
            log_totals,
            grad_attended,
        ),
    )
    grad_bias = bias_gradient(bias_sum, bucket, bias_rows.shape[1])
    grad_queries = back_items[0].reshape(local_shape)
    grad_window_keys = back_items[1].reshape(
        seq_count, block_count, 2 * BLOCK, local_head_count, HEAD_SIZE
    )
    grad_window_values = back_items[2].reshape(
        seq_count, block_count, 2 * BLOCK, local_head_count, HEAD_SIZE
    )
    state_keys_gradient = back_items[3].reshape(
        seq_count, block_count, state_slot_count, local_head_count, HEAD_SIZE
    )
    grad_state_values = back_items[4].reshape(
        seq_count, block_count, state_slot_count, local_head_count, HEAD_SIZE
    )
    back_keys, back_values = (
        from_behind(grad_window_keys[:, 0, :BLOCK].astype(jnp.bfloat16), "ctx", -1).astype(
            jnp.float32
        ),
        from_behind(grad_window_values[:, 0, :BLOCK].astype(jnp.bfloat16), "ctx", -1).astype(
            jnp.float32
        ),
    )
    key_grad = grad_window_keys[:, :, BLOCK:] + jnp.concatenate(
        [grad_window_keys[:, 1:, :BLOCK], back_keys[:, None]], 1
    )
    value_grad = grad_window_values[:, :, BLOCK:] + jnp.concatenate(
        [grad_window_values[:, 1:, :BLOCK], back_values[:, None]], 1
    )
    state_key_gradient = jnp.einsum(
        "sbmhe,sbmhf->hef", state_reduced, state_keys_gradient, preferred_element_type=jnp.float32
    )
    grad_svalue = jnp.einsum(
        "sbmhe,sbmhf->hef", state_reduced, grad_state_values, preferred_element_type=jnp.float32
    )
    direct = jnp.einsum(
        "palcq,crq->palcr",
        state_keys_gradient,
        state_key_complete,
        preferred_element_type=jnp.float32,
    ) + jnp.einsum(
        "palcq,crq->palcr", grad_state_values, svalue_full, preferred_element_type=jnp.float32
    )
    direct = direct.reshape(seq_count, block_count, state_slot_count, local_width)
    back_accum = jnp.zeros((seq_count, state_slot_count, local_width), jnp.float32)
    for block_index in reversed(range(block_count)):
        back_accum = direct[:, block_index] + gate_value * back_accum
    back_identity = (jnp.ones((local_width,), jnp.float32), jnp.zeros_like(back_accum))
    unused_power, incoming = prefix_2((gate_power, back_accum), "ctx", compose, back_identity, True)
    carried = incoming
    contrib_grads = [None] * block_count
    gate_grad = jnp.zeros((local_width,), jnp.float32)
    for block_index in reversed(range(block_count)):
        contrib_grads[block_index] = ((1.0 - gate_value) * carried).astype(jnp.bfloat16)
        gate_grad = gate_grad + jnp.sum(
            carried * (stacked[:, block_index] - contrib[:, block_index]), axis=(0, 1)
        )
        carried = direct[:, block_index] + gate_value * carried
    first_device = (lax.axis_index("ctx") == 0).astype(jnp.float32)
    grad_sinit = first_device * jnp.sum(carried, axis=0)
    grad_gate = (gate_grad * gate_value * (1.0 - gate_value)).reshape(local_head_count, HEAD_SIZE)
    grad_contrib = jnp.stack(contrib_grads, axis=1).reshape(
        seq_count, block_count, state_slot_count, local_head_count, HEAD_SIZE
    )
    grad_read = jnp.einsum(
        "sbmhe,sbthe->sbhmt", grad_contrib, value_rows, preferred_element_type=jnp.float32
    )
    extra_values = jnp.einsum(
        "sbhmt,sbmhe->sbthe", read_low, grad_contrib, preferred_element_type=jnp.float32
    )
    read_delta = jnp.sum(read_probs * grad_read, axis=-1, keepdims=True)
    grad_read_score = (read_probs * (grad_read - read_delta)).astype(jnp.bfloat16)
    grad_squery = (
        scores_scale
        * jnp.einsum(
            "sbhmt,sbthe->mhe", grad_read_score, key_rows, preferred_element_type=jnp.float32
        )
    ).reshape(state_slot_count, local_width)
    extra_keys = scores_scale * jnp.einsum(
        "sbhmt,mhe->sbthe", grad_read_score, query_heads, preferred_element_type=jnp.float32
    )
    grad_q_rows = grad_queries.astype(jnp.bfloat16).reshape(row_count, local_width)
    grad_k_rows = (key_grad + extra_keys).astype(jnp.bfloat16).reshape(row_count, local_width)
    grad_v_rows = (value_grad + extra_values).astype(jnp.bfloat16).reshape(row_count, local_width)
    grad_wq = jnp.dot(attn_in.T, grad_q_rows, preferred_element_type=jnp.float32)
    grad_wk = jnp.dot(attn_in.T, grad_k_rows, preferred_element_type=jnp.float32)
    grad_wv = jnp.dot(attn_in.T, grad_v_rows, preferred_element_type=jnp.float32)
    grad_attn_in = (
        jnp.dot(grad_q_rows, query_full.T, preferred_element_type=jnp.float32)
        + jnp.dot(grad_k_rows, key_full.T, preferred_element_type=jnp.float32)
        + jnp.dot(grad_v_rows, value_full.T, preferred_element_type=jnp.float32)
    )
    part_tokens, part_gain_one = norm_backward(grad_attn_in, normed_one, inverse_one, gain_one_vec)
    token_share, grad_gain_one = (
        lax.psum_scatter(
            part_tokens.reshape(seq_count, length, full_width).astype(jnp.bfloat16),
            "tp",
            scatter_dimension=2,
            tiled=True,
        ).astype(jnp.float32),
        lax.psum_scatter(
            part_gain_one.reshape(head_total, HEAD_SIZE).astype(jnp.bfloat16),
            "tp",
            scatter_dimension=0,
            tiled=True,
        ).astype(jnp.float32),
    )
    grad_tokens = (middle_grad + token_share).astype(jnp.bfloat16)
    grads = (
        lax.psum_scatter(
            grad_wq.astype(jnp.bfloat16), ("dp", "ctx"), scatter_dimension=0, tiled=True
        ).astype(jnp.float32),
        lax.psum_scatter(
            grad_wk.astype(jnp.bfloat16), ("dp", "ctx"), scatter_dimension=0, tiled=True
        ).astype(jnp.float32),
        lax.psum_scatter(
            grad_wv.astype(jnp.bfloat16), ("dp", "ctx"), scatter_dimension=0, tiled=True
        ).astype(jnp.float32),
        lax.psum_scatter(
            grad_wout.astype(jnp.bfloat16), ("dp", "ctx"), scatter_dimension=1, tiled=True
        ).astype(jnp.float32),
        lax.psum_scatter(
            grad_up.astype(jnp.bfloat16), ("dp", "ctx"), scatter_dimension=0, tiled=True
        ).astype(jnp.float32),
        lax.psum_scatter(
            grad_down.astype(jnp.bfloat16), ("dp", "ctx"), scatter_dimension=1, tiled=True
        ).astype(jnp.float32),
        lax.psum_scatter(
            grad_squery.astype(jnp.bfloat16), ("dp", "ctx"), scatter_dimension=0, tiled=True
        ).astype(jnp.float32),
        lax.psum_scatter(
            grad_sinit.astype(jnp.bfloat16), ("dp", "ctx"), scatter_dimension=0, tiled=True
        ).astype(jnp.float32),
        lax.psum_scatter(
            grad_gain_one.astype(jnp.bfloat16), ("dp", "ctx"), scatter_dimension=1, tiled=True
        ).astype(jnp.float32),
        lax.psum_scatter(
            grad_gain_two.astype(jnp.bfloat16), ("dp", "ctx"), scatter_dimension=1, tiled=True
        ).astype(jnp.float32),
        lax.psum_scatter(
            grad_bias.astype(jnp.bfloat16), ("dp", "ctx"), scatter_dimension=1, tiled=True
        ).astype(jnp.float32),
        lax.psum_scatter(
            grad_gate.astype(jnp.bfloat16), ("dp", "ctx"), scatter_dimension=1, tiled=True
        ).astype(jnp.float32),
        lax.psum_scatter(
            state_key_gradient.astype(jnp.bfloat16), ("dp", "ctx"), scatter_dimension=1, tiled=True
        ).astype(jnp.float32),
        lax.psum_scatter(
            grad_svalue.astype(jnp.bfloat16), ("dp", "ctx"), scatter_dimension=1, tiled=True
        ).astype(jnp.float32),
    )
    return (
        output,
        grad_tokens,
        grads[0],
        grads[1],
        grads[2],
        grads[3],
        grads[4],
        grads[5],
        grads[6],
        grads[7],
        grads[8],
        grads[9],
        grads[10],
        grads[11],
        grads[12],
        grads[13],
    )


def solution(mesh):
    in_specs = (
        P("dp", "ctx", "tp"),
        P("dp", "ctx", None),
        P("dp"),
        P(("dp", "ctx"), "tp"),
        P(("dp", "ctx"), "tp"),
        P(("dp", "ctx"), "tp"),
        P("tp", ("dp", "ctx")),
        P(("dp", "ctx"), "tp"),
        P("tp", ("dp", "ctx")),
        P(("dp", "ctx"), "tp"),
        P(("dp", "ctx"), "tp"),
        P("tp", ("dp", "ctx")),
        P("tp", ("dp", "ctx")),
        P("tp", ("dp", "ctx")),
        P("tp", ("dp", "ctx")),
        P("tp", ("dp", "ctx"), None),
        P("tp", ("dp", "ctx"), None),
    )
    out_specs = (
        P("dp", "ctx", "tp"),
        P("dp", "ctx", "tp"),
        P(("dp", "ctx"), "tp"),
        P(("dp", "ctx"), "tp"),
        P(("dp", "ctx"), "tp"),
        P("tp", ("dp", "ctx")),
        P(("dp", "ctx"), "tp"),
        P("tp", ("dp", "ctx")),
        P(("dp", "ctx"), "tp"),
        P(("dp", "ctx"), "tp"),
        P("tp", ("dp", "ctx")),
        P("tp", ("dp", "ctx")),
        P("tp", ("dp", "ctx")),
        P("tp", ("dp", "ctx")),
        P("tp", ("dp", "ctx"), None),
        P("tp", ("dp", "ctx"), None),
    )
    return jax.shard_map(body, mesh=mesh, in_specs=in_specs, out_specs=out_specs, check_vma=False)
```

profile of v0, /device:TPU:0, one launch (start us, length us, event | category | flops | bytes accessed | tf_op | source)
XLA Modules:
  0.0 2680.5 jit_solution(5130386284348677934)
XLA Ops:
  136.4 25.1 all-gather.14.cloned.1.call-done
  220.0 18.8 fusion.207
  298.6 308.3 %while.62 = (s32[]{:T(128)}, bf16[8,512,2,128]{1,3,2,0:T(8,128)(2,1)}, f32[8,2,512]{2,1,0:T(2,128)}, bf16[8,1024,2,128]{3,1,2,0:T(8,128)(2,1)}, pred[8,1,512,102...) while((s32[]{:T(128)}, ...), condition=%wide.region_10.11_spmd.clone, body=%wide.region_5.10_spmd.clone.sunk | while | flops 884734976 | bytes 114110376 | solution.py:293
  302.5 24.2 fusion.278
  341.1 24.2 fusion.278
  379.6 24.2 fusion.278
  418.1 24.2 fusion.278
  456.7 24.2 fusion.278
  495.2 24.2 fusion.278
  533.8 24.2 fusion.278
  572.3 24.2 fusion.278
  622.1 150.3 %reduce-scatter.29.cloned.1.call-done = bf16[4,1024,256]{2,1,0:T(8,128)(2,1)} async-done(((bf16[4,1024,1024]{2,1,0:T(8,128)(2,1)}), bf16[4,1024,256]{2,1,0:T(8,128)(2,1)}) %reduce-scatter.29.cloned.1.call-update) | async-done | bytes 2097168 | tf_op jit(solution)/shard_map/reduce_scatter | solution.py:308
  796.7 129.0 %all-gather.18.cloned.1.call-done = bf16[4,1024,1024]{2,1,0:T(8,128)(2,1)} async-done(((bf16[4,1024,256]{2,1,0:T(8,128)(2,1)}), bf16[4,1024,1024]{2,1,0:T(8,128)(2,1)}) %all-gather.18.cloned.1.call-update) | async-done | bytes 8388624 | tf_op jit(solution)/shard_map/all_gather | solution.py:313
  983.3 50.8 %add_convert_fusion = (bf16[4096,1024]{1,0:T(8,128)(2,1)}, f32[4096,1024]{1,0:T(8,128)}) fusion(f32[4096,1024]{1,0:T(8,128)} %fusion.208, bf16[4096,1024]{1,0:T(8,128)(2,1)} %bitcast.648, bf16[1024,1024]{1,0:T(8,128)(2,1)} %all-gather.22.cloned.1.call-done), kind=kOutput, calls=%fused_computation.126 | convolution fusion | flops 8891924480 | bytes 52428800 | tf_op jit(solution)/shard_map/dot_general | solution.py:330
  1062.0 290.9 %all-reduce.5.cloned.1.call-done = bf16[4,1024,1024]{2,1,0:T(8,128)(2,1)} async-done(((bf16[4,1024,1024]{2,1,0:T(8,128)(2,1)}), bf16[4,1024,1024]{2,1,0:T(8,128)(2,1)}) %all-reduce.5.cloned.1.call-update) | async-done | bytes 8388624 | tf_op jit(solution)/shard_map/psum | solution.py:344
  1380.8 474.2 %while.63 = (s32[]{:T(128)}, f32[2,512,1024]{2,1,0:T(8,128)}, bf16[8,512,2,128]{1,3,2,0:T(8,128)(2,1)}, f32[8,1024,2,128]{1,3,2,0:T(8,128)}, f32[8,1024,2,128]{1...) while((s32[]{:T(128)}, f32[2,512,1024]{2,1,0:T(8,128)}, ...), condition=%wide.region_19.20_spmd.clone, body=%wide.region_16.19_spmd.clone.sunk | while | flops 2097019904 | bytes 181717040 | solution.py:437
  1394.4 26.2 multiply_reduce_fusion.47
  1452.5 26.2 multiply_reduce_fusion.47
  1512.0 26.2 multiply_reduce_fusion.47
  1571.4 26.2 multiply_reduce_fusion.47
  1630.8 26.2 multiply_reduce_fusion.47
  1690.2 26.2 multiply_reduce_fusion.47
  1749.6 26.2 multiply_reduce_fusion.47
  1809.1 26.2 multiply_reduce_fusion.47
  2057.6 22.9 multiply_reduce_fusion.4
  2196.8 29.4 %reduce-scatter.55.cloned.1.call-done = bf16[16,2]{1,0:T(8,128)(2,1)} async-done(((bf16[128,2]{1,0:T(8,128)(2,1)}), bf16[16,2]{1,0:T(8,128)(2,1)}) %reduce-scatter.55.cloned.1.call-update) | async-done | bytes 80
  2227.5 35.3 %reduce-scatter.53.cloned.1.call-done = bf16[64,256]{1,0:T(8,128)(2,1)} async-done(((bf16[512,256]{1,0:T(8,128)(2,1)}), bf16[64,256]{1,0:T(8,128)(2,1)}) %reduce-scatter.53.cloned.1.call-update) | async-done | bytes 32784
  2264.4 35.2 %reduce-scatter.43.cloned.1.call-done = bf16[64,256]{1,0:T(8,128)(2,1)} async-done(((bf16[512,256]{1,0:T(8,128)(2,1)}), bf16[64,256]{1,0:T(8,128)(2,1)}) %reduce-scatter.43.cloned.1.call-update) | async-done | bytes 32784 | tf_op jit(solution)/shard_map/reduce_scatter | solution.py:577
  2301.0 35.7 %reduce-scatter.39.cloned.1.call-done = bf16[128,256]{1,0:T(8,128)(2,1)} async-done(((bf16[1024,256]{1,0:T(8,128)(2,1)}), bf16[128,256]{1,0:T(8,128)(2,1)}) %reduce-scatter.39.cloned.1.call-update) | async-done | bytes 65552 | tf_op jit(solution)/shard_map/reduce_scatter | solution.py:565
  2338.1 36.3 %reduce-scatter.37.cloned.1.call-done = bf16[128,256]{1,0:T(8,128)(2,1)} async-done(((bf16[1024,256]{1,0:T(8,128)(2,1)}), bf16[128,256]{1,0:T(8,128)(2,1)}) %reduce-scatter.37.cloned.1.call-update) | async-done | bytes 65552 | tf_op jit(solution)/shard_map/reduce_scatter | solution.py:562
  2376.0 145.5 %reduce-scatter.31.cloned.1.call-done = bf16[4,1024,256]{2,1,0:T(8,128)(2,1)} async-done(((bf16[4,1024,1024]{2,1,0:T(8,128)(2,1)}), bf16[4,1024,256]{2,1,0:T(8,128)(2,1)}) %reduce-scatter.31.cloned.1.call-update) | async-done | bytes 2097168 | tf_op jit(solution)/shard_map/reduce_scatter | solution.py:325
  2525.8 143.3 %reduce-scatter.33.cloned.1.call-done = bf16[4,1024,256]{2,1,0:T(8,128)(2,1)} async-done(((bf16[4,1024,1024]{2,1,0:T(8,128)(2,1)}), bf16[4,1024,256]{2,1,0:T(8,128)(2,1)}) %reduce-scatter.33.cloned.1.call-update) | async-done | bytes 2097168 | tf_op jit(solution)/shard_map/reduce_scatter | solution.py:544
  (875 shorter events, 1112.2 us)
Async XLA Ops:
  7.2 154.3 %all-gather.14.cloned.1.call-start = ((), (), s32[]{:S(2)}) async-start(), calls=%async_computation.16 | async-start | bytes 10485760 | tf_op jit(solution)/shard_map/all_gather | solution.py:152
  7.9 274.2 %all-gather.16.cloned.1.call-start = ((), (), s32[]{:S(2)}) async-start(), calls=%async_computation.17 | async-start | bytes 3145728 | tf_op jit(solution)/shard_map/all_gather | solution.py:26
  68.6 222.1 %copy-start.76 = (bf16[2,128,128]{2,1,0:T(8,128)(2,1)}, bf16[2,128,128]{2,1,0:T(8,128)(2,1)S(1)}, u32[]{:S(2)}) copy-start(bf16[2,128,128]{2,1,0:T(8,128)(2,1)S(1)} %all_gather.80) | copy-start | bytes 196612
  77.5 215.7 %copy-start.74 = (bf16[2,128,128]{2,1,0:T(8,128)(2,1)}, bf16[2,128,128]{2,1,0:T(8,128)(2,1)S(1)}, u32[]{:S(2)}) copy-start(bf16[2,128,128]{2,1,0:T(8,128)(2,1)S(1)} %all_gather.81) | copy-start | bytes 196612
  205.1 63.9 %collective-permute-start = (bf16[4,512,2,128]{3,2,1,0:T(2,128)(2,1)}, bf16[4,512,2,128]{3,2,1,0:T(2,128)(2,1)}, u32[]{:S(2)}, u32[]{:S(2)}) collective-permute-start(bf16[4,512,2,128]{3,2,1,0:T(2,128)(2,1)} %get-tuple-element.2388), channel_id=1, source_target_pairs={{0,4},{1,5},{2,6},{3,7},{8,12},{9,13},{10,14},{11,15},{16,20},{17,... | collective-permute-start | bytes 3145736 | tf_op jit(solution)/shard_map/ppermute | solution.py:18
  209.7 64.0 %collective-permute-start.1 = (bf16[4,512,2,128]{3,2,1,0:T(2,128)(2,1)}, bf16[4,512,2,128]{3,2,1,0:T(2,128)(2,1)}, u32[]{:S(2)}, u32[]{:S(2)}) collective-permute-start(bf16[4,512,2,128]{3,2,1,0:T(2,128)(2,1)} %get-tuple-element.2386), channel_id=1, source_target_pairs={{0,4},{1,5},{2,6},{3,7},{8,12},{9,13},{10,14},{11,15},{16,20},{17,... | collective-permute-start | bytes 3145736 | tf_op jit(solution)/shard_map/ppermute | solution.py:18
  253.0 519.4 %reduce-scatter.29.cloned.1.call-start = ((), (), s32[]{:S(2)}) async-start(), calls=%async_computation.18 | async-start | bytes 10485760 | tf_op jit(solution)/shard_map/reduce_scatter | solution.py:308
  622.0 303.6 %all-gather.18.cloned.1.call-start = ((), (), s32[]{:S(2)}) async-start(), calls=%async_computation.19 | async-start | bytes 10485760 | tf_op jit(solution)/shard_map/all_gather | solution.py:313
  775.8 177.6 %all-gather.20.cloned.1.call-start = ((), (), s32[]{:S(2)}) async-start(), calls=%async_computation.20 | async-start | bytes 2359296 | tf_op jit(solution)/shard_map/all_gather | solution.py:128
  776.4 206.9 %all-gather.22.cloned.1.call-start = ((), (), s32[]{:S(2)}) async-start(), calls=%async_computation.21 | async-start | bytes 2359296 | tf_op jit(solution)/shard_map/all_gather | solution.py:129
  777.0 576.0 %all-reduce.5.cloned.1.call-start = ((), (), s32[]{:S(2)}) async-start(), calls=%async_computation.23 | async-start | bytes 16777216 | tf_op jit(solution)/shard_map/psum | solution.py:344
  1061.9 922.9 %all-gather.24.cloned.1.call-start = ((), (), s32[]{:S(2)}) async-start(), calls=%async_computation.24 | async-start | bytes 3145728 | tf_op jit(solution)/shard_map/all_gather | solution.py:26
  1062.0 307.0 %copy-start.67 = (bf16[256,1024]{1,0:T(8,128)(2,1)S(1)}, bf16[256,1024]{1,0:T(8,128)(2,1)}, u32[]{:S(2)}) copy-start(bf16[256,1024]{1,0:T(8,128)(2,1)} %all_gather.82) | copy-start | bytes 1572868
  1380.8 474.3 %copy-start.77 = (bf16[2,128,128]{2,1,0:T(8,128)(2,1)S(1)}, bf16[2,128,128]{2,1,0:T(8,128)(2,1)}, u32[]{:S(2)}) copy-start(bf16[2,128,128]{2,1,0:T(8,128)(2,1)} %copy-done.76) | copy-start | bytes 196612
  1863.2 278.8 %reduce-scatter.51.cloned.1.call-start = ((), (), s32[]{:S(2)}) async-start(), calls=%async_computation.34 | async-start | bytes 2359296
  1893.7 250.2 %reduce-scatter.41.cloned.1.call-start = ((), (), s32[]{:S(2)}) async-start(), calls=%async_computation.29 | async-start | bytes 2359296 | tf_op jit(solution)/shard_map/reduce_scatter | solution.py:571
  1908.7 279.7 %reduce-scatter.47.cloned.1.call-start = ((), (), s32[]{:S(2)}) async-start(), calls=%async_computation.32 | async-start | bytes 73728 | tf_op jit(solution)/shard_map/reduce_scatter | solution.py:598
  1923.2 266.4 %reduce-scatter.45.cloned.1.call-start = ((), (), s32[]{:S(2)}) async-start(), calls=%async_computation.31 | async-start | bytes 73728 | tf_op jit(solution)/shard_map/reduce_scatter | solution.py:595
  1926.4 264.5 %reduce-scatter.49.cloned.1.call-start = ((), (), s32[]{:S(2)}) async-start(), calls=%async_computation.33 | async-start | bytes 589824
  1934.1 258.5 %reduce-scatter.35.cloned.1.call-start = ((), (), s32[]{:S(2)}) async-start(), calls=%async_computation.26 | async-start | bytes 589824 | tf_op jit(solution)/shard_map/reduce_scatter | solution.py:559
  1939.9 39.3 %collective-permute-start.3 = (bf16[4,512,2,128]{1,3,2,0:T(8,128)(2,1)}, bf16[4,512,2,128]{1,3,2,0:T(8,128)(2,1)}, u32[]{:S(2)}, u32[]{:S(2)}) collective-permute-start(bf16[4,512,2,128]{1,3,2,0:T(8,128)(2,1)} %fusion.191), channel_id=1, source_target_pairs={{4,0},{5,1},{6,2},{7,3},{12,8},{13,9},{14,10},{15,11},{20,16},{21,... | collective-permute-start | bytes 3145736 | tf_op jit(solution)/shard_map/ppermute | solution.py:18
  1941.2 40.9 %collective-permute-start.2 = (bf16[4,512,2,128]{3,1,0,2:T(8,128)(2,1)}, bf16[4,512,2,128]{3,1,0,2:T(8,128)(2,1)}, u32[]{:S(2)}, u32[]{:S(2)}) collective-permute-start(bf16[4,512,2,128]{3,1,0,2:T(8,128)(2,1)} %bitcast.683), channel_id=1, source_target_pairs={{4,0},{5,1},{6,2},{7,3},{12,8},{13,9},{14,10},{15,11},{20,16},{21,... | collective-permute-start | bytes 3145736 | tf_op jit(solution)/shard_map/ppermute | solution.py:18
  1971.1 223.0 %reduce-scatter.59.cloned.1.call-start = ((), (), s32[]{:S(2)}) async-start(), calls=%async_computation.38 | async-start | bytes 36864
  2057.5 138.0 %reduce-scatter.57.cloned.1.call-start = ((), (), s32[]{:S(2)}) async-start(), calls=%async_computation.37 | async-start | bytes 36864
  2090.7 135.5 %reduce-scatter.55.cloned.1.call-start = ((), (), s32[]{:S(2)}) async-start(), calls=%async_computation.36 | async-start | bytes 36864
  2091.5 171.3 %reduce-scatter.53.cloned.1.call-start = ((), (), s32[]{:S(2)}) async-start(), calls=%async_computation.35 | async-start | bytes 294912
  2092.4 207.1 %reduce-scatter.43.cloned.1.call-start = ((), (), s32[]{:S(2)}) async-start(), calls=%async_computation.30 | async-start | bytes 294912 | tf_op jit(solution)/shard_map/reduce_scatter | solution.py:577
  2098.3 238.4 %reduce-scatter.39.cloned.1.call-start = ((), (), s32[]{:S(2)}) async-start(), calls=%async_computation.28 | async-start | bytes 589824 | tf_op jit(solution)/shard_map/reduce_scatter | solution.py:565
  2105.7 268.8 %reduce-scatter.37.cloned.1.call-start = ((), (), s32[]{:S(2)}) async-start(), calls=%async_computation.27 | async-start | bytes 589824 | tf_op jit(solution)/shard_map/reduce_scatter | solution.py:562
  2112.6 408.8 %reduce-scatter.31.cloned.1.call-start = ((), (), s32[]{:S(2)}) async-start(), calls=%async_computation.22 | async-start | bytes 10485760 | tf_op jit(solution)/shard_map/reduce_scatter | solution.py:325
  2127.6 541.5 %reduce-scatter.33.cloned.1.call-start = ((), (), s32[]{:S(2)}) async-start(), calls=%async_computation.25 | async-start | bytes 10485760 | tf_op jit(solution)/shard_map/reduce_scatter | solution.py:544
  2163.7 357.8 %copy-start.36 = (bf16[4,1024,256]{2,1,0:T(8,128)(2,1)S(1)}, bf16[4,1024,256]{2,1,0:T(8,128)(2,1)}, u32[]{:S(2)}) copy-start(bf16[4,1024,256]{2,1,0:T(8,128)(2,1)} %param.26) | copy-start | bytes 6291460
  (207 other events, 2724.5 us)
Sparse Core Ops, SparseCore 0:
  9.6 151.8 all-gather.13
  253.2 16.1 all-gather.15
  622.2 150.2 reduce-scatter.28
  775.9 149.7 all-gather.17
  927.4 25.9 all-gather.19
  955.1 28.0 all-gather.21
  1062.1 290.8 all-reduce.4
  1863.3 9.5 all-gather.23
  1893.8 40.0 reduce-scatter.50
  1937.1 41.1 reduce-scatter.40
  1981.8 31.3 reduce-scatter.46
  2016.6 31.3 reduce-scatter.44
  2051.1 34.0 reduce-scatter.48
  2088.1 34.1 reduce-scatter.34
  2125.1 31.3 reduce-scatter.58
  2160.0 31.3 reduce-scatter.56
  2194.8 31.3 reduce-scatter.54
  2229.1 33.6 reduce-scatter.52
  2265.8 33.7 reduce-scatter.42
  2302.5 34.0 reduce-scatter.38
  2340.3 34.1 reduce-scatter.36
  2376.8 144.6 reduce-scatter.30
  2523.9 145.2 reduce-scatter.32
where the time goes:
time: 2690 us; the launch traced here: 2680 us
  waiting for transfers between devices  1090 us (41%)
  matrix products  877 us (33%)
  other arithmetic  322 us (12%)
  local copies, waits for them, and re-layouts  206 us (8%)
  blocking collectives  159 us (6%)
    dot_general x16, matrix products, block_score_rows(): jnp.einsum('ihe,jhe->hij', block_query_rows, block_window_key_rows, prefe...  403 us
    psum x1, waiting for transfers between devices, body(): lax.psum(part_middle.reshape(seq_count, length, full_width).astype(jnp.bf...  291 us
    reduce_scatter x1, waiting for transfers between devices, body(): lax.psum_scatter(attn_part.astype(jnp.bfloat16), 'tp', scatter_dimension=...  150 us
    reduce_scatter x1, waiting for transfers between devices, body(): lax.psum_scatter(mlp_part.astype(jnp.bfloat16), 'tp', scatter_dimension=2...  146 us
    reduce_scatter x1, waiting for transfers between devices, body(): lax.psum_scatter(part_tokens.reshape(seq_count, length, full_width).astyp...  143 us
    all_gather x1, waiting for transfers between devices, body(): lax.all_gather(middle.astype(jnp.bfloat16), 'tp', axis=2, tiled=True)  129 us
    unnamed x29, waiting for transfers between devices  66.8 us
    unnamed x358, local copies, waits for them, and re-layouts  57.5 us
  transfers between devices with their start and end apart: 27, of which 13 were waited for; matrix products, arithmetic and copies ran while one was open for 15% of the time, Pallas kernels for 0%

commit v1 on v0

--- a/solution.py
+++ b/solution.py
@@ -1,7 +1,11 @@
+import functools
+
 import jax
 import jax.numpy as jnp
 import numpy as np
 from jax import lax
+from jax.experimental import pallas as pl
+from jax.experimental.pallas import tpu as pltpu
 from jax.sharding import PartitionSpec as P
 
 HEAD_SIZE = 128
@@ -10,6 +14,8 @@
 
 EPSILON = 1e-06
 MASKED = -1e30
+ROWS_FORWARD = 128
+KEYS_BACKWARD = 256
 
 
 def from_behind(value, axis, steps):
@@ -619,6 +625,946 @@
     )
 
 
+LOG2E = 1.4426950408889634
+VMEM_BYTES = 58 * 1024 * 1024
+BF = jnp.bfloat16
+F32 = jnp.float32
+
+
+def nn(left, right):
+    return jnp.dot(left, right, preferred_element_type=F32)
+
+
+def nt(left, right):
+    return lax.dot_general(left, right, (((1,), (1,)), ((), ())), preferred_element_type=F32)
+
+
+def tn(left, right):
+    return lax.dot_general(left, right, (((0,), (0,)), ((), ())), preferred_element_type=F32)
+
+
+def flat(ref):
+    block = ref[0]
+    return block.reshape(block.shape[0] * block.shape[1], block.shape[2])
+
+
+def merged(place_ref, own_ref, other_ref):
+    own = own_ref[0, :, 0]
+    other = other_ref[0, :, 0]
+    is_first = place_ref[0] == 0
+    pair = [jnp.where(is_first, own, other), jnp.where(is_first, other, own)]
+    block = jnp.stack(pair, axis=1)
+    return block.reshape(-1, block.shape[-1])
+
+
+def inverse_rms(x):
+    return lax.rsqrt(jnp.mean(x * x, axis=-1, keepdims=True) + EPSILON)
+
+
+def params():
+    return pltpu.CompilerParams(vmem_limit_bytes=VMEM_BYTES)
+
+
+def project_kernel(
+    place_ref, tok_ref, gain_ref, wq_ref, wqo_ref, wk_ref, wko_ref, wv_ref, wvo_ref,
+    q_ref, k_ref, v_ref, ain_ref,
+):
+    @pl.when(pl.program_id(0) == 0)
+    def _():
+        x = tok_ref[...].astype(F32)
+        ain_ref[...] = (x * inverse_rms(x) * gain_ref[...]).astype(BF)
+
+    a = ain_ref[...]
+    for w_ref, w_other, o_ref in (
+        (wq_ref, wqo_ref, q_ref), (wk_ref, wko_ref, k_ref), (wv_ref, wvo_ref, v_ref)
+    ):
+        o_ref[...] = nn(a, merged(place_ref, w_ref, w_other)).astype(BF)
+
+
+def read_kernel(
+    place_ref, sq_ref, sqo_ref, k_ref, v_ref, gate_ref, o_ref, sum_ref, state_ref, *, blocks
+):
+    n = pl.program_id(1)
+    sq = merged(place_ref, sq_ref, sqo_ref)
+    k = k_ref[...]
+    v = v_ref[...]
+    scale = HEAD_SIZE ** (-0.5) * LOG2E
+    step = 256
+    gate = jnp.where(lax.rem(n, blocks) == 0, 0.0, gate_ref[...])
+    fresh = 1.0 - gate_ref[...]
+
+    @pl.when(n == 0)
+    def _():
+        state_ref[...] = jnp.zeros_like(state_ref)
+
+    for start in range(0, sq.shape[0], step):
+        rows = slice(start, start + step)
+        s = nt(sq[rows], k) * scale
+        p = jnp.exp2(s - jnp.max(s, axis=-1, keepdims=True))
+        total = jnp.sum(p, axis=-1, keepdims=True)
+        contrib = nn(p.astype(BF), v) / total
+        o_ref[rows, :] = contrib
+        state = gate * state_ref[rows, :] + fresh * contrib
+        state_ref[rows, :] = state
+        sum_ref[rows, :] = state.astype(BF)
+
+
+def attend_kernel(
+    place_ref, info_ref, q_ref, k_ref, v_ref, kp_ref, vp_ref, hk_ref, hv_ref,
+    wk_ref, wko_ref, wv_ref, wvo_ref, contrib_ref, init_ref, inito_ref, lead_ref, power_ref,
+    gate_ref, u_ref, o_ref, lse_ref, low_ref, moved_ref, bias_ref, state_ref, *, blocks,
+):
+    n = pl.program_id(1)
+    first = lax.rem(n, blocks) == 0
+    scale = HEAD_SIZE ** (-0.5) * LOG2E
+
+    @pl.when(n == 0)
+    def _():
+        row = jnp.broadcast_to(u_ref[0], (BLOCK, u_ref.shape[-1]))
+        bias_ref[...] = pltpu.roll(row, 0, 1, stride=1, stride_axis=0)[:, : 2 * BLOCK]
+
+    has_previous = info_ref[n, 0] > 0
+    reach = info_ref[n, 1]
+    k = k_ref[...]
+    v = v_ref[...]
+    kp = jnp.where(first, hk_ref[...], kp_ref[...])
+    vp = jnp.where(first, hv_ref[...], vp_ref[...])
+
+    @pl.when(first)
+    def _():
+        init = merged(place_ref, init_ref, inito_ref).astype(F32)
+        state_ref[...] = power_ref[...] * init + lead_ref[...].astype(F32)
+
+    state = state_ref[...]
+    contrib = contrib_ref[...]
+    st = state.astype(BF)
+    low_ref[...] = st
+    moved_ref[...] = (state - contrib).astype(BF)
+    state_ref[...] = contrib + gate_ref[...] * (state - contrib)
+    sk = nn(st, merged(place_ref, wk_ref, wko_ref)).astype(BF)
+    sv = nn(st, merged(place_ref, wv_ref, wvo_ref)).astype(BF)
+    step = ROWS_FORWARD
+
+    def run(with_previous):
+        for start in range(0, BLOCK, step):
+            q = q_ref[start : start + step, :]
+            sc = nt(q, k) * scale + bias_ref[start : start + step, BLOCK:]
+            row = lax.broadcasted_iota(jnp.int32, (step, 1), 0) + start
+            column = lax.broadcasted_iota(jnp.int32, (step, BLOCK), 1)
+            sc = jnp.where(column <= jnp.maximum(row, reach - 1), sc, MASKED)
+            ss = nt(q, sk) * scale
+            peak = jnp.maximum(
+                jnp.max(sc, axis=-1, keepdims=True), jnp.max(ss, axis=-1, keepdims=True)
+            )
+            if with_previous:
+                sp = nt(q, kp) * scale + bias_ref[start : start + step, :BLOCK]
+                peak = jnp.maximum(peak, jnp.max(sp, axis=-1, keepdims=True))
+            pc = jnp.exp2(sc - peak)
+            ps = jnp.exp2(ss - peak)
+            total = jnp.sum(pc, axis=-1, keepdims=True) + jnp.sum(ps, axis=-1, keepdims=True)
+            out = nn(pc.astype(BF), v) + nn(ps.astype(BF), sv)
+            if with_previous:
+                pp = jnp.exp2(sp - peak)
+                total = total + jnp.sum(pp, axis=-1, keepdims=True)
+                out = out + nn(pp.astype(BF), vp)
+            o_ref[start : start + step, :] = (out / total).astype(BF)
+            lse = jnp.broadcast_to(peak + jnp.log2(total), (step, 128))
+            lse_ref[0, 0, :, start : start + step] = lse.T[:1]
+
+    @pl.when(has_previous)
+    def _():
+        run(True)
+
+    @pl.when(jnp.logical_not(has_previous))
+    def _():
+        run(False)
+
+
+def attend_back_kernel(
+    place_ref, info_ref, q_ref, k_ref, v_ref, kp_ref, vp_ref, hk_ref, hv_ref,
+    wk_ref, wko_ref, wv_ref, wvo_ref, st_ref, gate_ref, u_ref, do_ref, o_ref, lse_ref,
+    dq_ref, dk_ref, dv_ref, dkp_ref, dvp_ref, direct_ref, gwk_ref, gwv_ref, gb_ref, total_ref,
+    bias_ref, sum_ref, dq_acc, state_acc, *, blocks,
+):
+    step_at = pl.program_id(1)
+    n = pl.num_programs(1) - 1 - step_at
+    first = lax.rem(n, blocks) == 0
+    gate = jnp.where(lax.rem(n, blocks) == blocks - 1, 0.0, gate_ref[...])
+    factor = HEAD_SIZE ** (-0.5)
+    scale = factor * LOG2E
+    window = 2 * BLOCK
+    width = BLOCK + window
+
+    @pl.when(step_at == 0)
+    def _():
+        state_acc[...] = jnp.zeros_like(state_acc)
+        row = jnp.broadcast_to(u_ref[0], (window, u_ref.shape[-1]))
+        bias_ref[...] = pltpu.roll(row, 0, 1, stride=1, stride_axis=0)[:, :BLOCK]
+        sum_ref[...] = jnp.zeros_like(sum_ref)
+        gwk_ref[...] = jnp.zeros_like(gwk_ref)
+        gwv_ref[...] = jnp.zeros_like(gwv_ref)
+
+    has_previous = info_ref[n, 0] > 0
+    reach = info_ref[n, 1]
+    q = q_ref[...]
+    do = do_ref[...]
+    lse = lse_ref[0, 0]
+    delta = jnp.sum((do.astype(F32) * o_ref[...].astype(F32)).T, axis=0, keepdims=True)
+    step = KEYS_BACKWARD
+
+    def part(key, value, start, bias_start, masked):
+        s = nt(key, q) * scale
+        if bias_start is not None:
+            s = s + bias_ref[bias_start : bias_start + step, :]
+        if masked:
+            key_at = lax.broadcasted_iota(jnp.int32, (step, BLOCK), 0) + start
+            query_at = lax.broadcasted_iota(jnp.int32, (1, BLOCK), 1)
+            s = jnp.where(key_at <= jnp.maximum(query_at, reach - 1), s, MASKED)
+        p = jnp.exp2(s - lse)
+        dp = nt(value, do)
+        ds = (p * (dp - delta)).astype(BF)
+        if bias_start is not None:
+            for block in range(0, step, 128):
+                at = window - bias_start - block
+                sum_ref[:, at : at + BLOCK] += ds[block : block + 128].astype(F32)
+        dq_acc[...] += tn(ds, key)
+        return nn(ds, q) * factor, nn(p.astype(BF), do)
+
+    dq_acc[...] = jnp.zeros_like(dq_acc)
+    st = st_ref[...]
+    key_map = merged(place_ref, wk_ref, wko_ref)
+    value_map = merged(place_ref, wv_ref, wvo_ref)
+    sk = nn(st, key_map).astype(BF)
+    sv = nn(st, value_map).astype(BF)
+    for start in range(0, st.shape[0], step):
+        rows = slice(start, start + step)
+        dk, dv = part(sk[rows], sv[rows], start, None, False)
+        dk = dk.astype(BF)
+        dv = dv.astype(BF)
+        direct = nt(dk, key_map) + nt(dv, value_map)
+        direct_ref[rows, :] = direct
+        state = direct + gate * state_acc[rows, :]
+        state_acc[rows, :] = state
+        total_ref[rows, :] = state.astype(BF)
+        gwk_ref[0] += tn(st[rows], dk)
+        gwv_ref[0] += tn(st[rows], dv)
+    for start in range(0, BLOCK, step):
+        rows = slice(start, start + step)
+        dk, dv = part(k_ref[rows, :], v_ref[rows, :], start, BLOCK + start, True)
+        dk_ref[rows, :] = dk
+        dv_ref[rows, :] = dv
+
+    @pl.when(has_previous)
+    def _():
+        for start in range(0, BLOCK, step):
+            rows = slice(start, start + step)
+            key = jnp.where(first, hk_ref[rows, :], kp_ref[rows, :])
+            value = jnp.where(first, hv_ref[rows, :], vp_ref[rows, :])
+            dk, dv = part(key, value, start, start, False)
+            dkp_ref[rows, :] = dk.astype(BF)
+            dvp_ref[rows, :] = dv.astype(BF)
+
+    @pl.when(jnp.logical_not(has_previous))
+    def _():
+        dkp_ref[...] = jnp.zeros_like(dkp_ref)
+        dvp_ref[...] = jnp.zeros_like(dvp_ref)
+
+    dq_ref[...] = (dq_acc[...] * factor).astype(BF)
+
+    @pl.when(n == 0)
+    def _():
+        folded = sum_ref[...]
+        half = 64
+        while half >= 8:
+            folded = folded[:half] + pltpu.roll(folded[half:], width - half, 1)
+            half //= 2
+        total = folded[:1]
+        for row in range(1, 8):
+            total = total + pltpu.roll(folded[row : row + 1], width - row, 1)
+        gb_ref[0] = total
+
+
+def read_back_kernel(
+    place_ref, sq_ref, sqo_ref, k_ref, v_ref, direct_ref, moved_ref, later_ref, gate_ref,
+    dk_ref, dv_ref, nk_ref, nv_ref, rk_ref, rv_ref,
+    gk_ref, gv_ref, gsq_ref, ginit_ref, ggate_ref, carried_ref, *, blocks,
+):
+    step_at = pl.program_id(1)
+    n = pl.num_programs(1) - 1 - step_at
+    last = lax.rem(n, blocks) == blocks - 1
+    factor = HEAD_SIZE ** (-0.5)
+
+    @pl.when(step_at == 0)
+    def _():
+        gsq_ref[...] = jnp.zeros_like(gsq_ref)
+        ginit_ref[...] = jnp.zeros_like(ginit_ref)
+        ggate_ref[...] = jnp.zeros_like(ggate_ref)
+
+    @pl.when(last)
+    def _():
+        carried_ref[...] = later_ref[...].astype(F32)
+
+    gate = gate_ref[...]
+    carried = carried_ref[...]
+    gc = ((1.0 - gate) * carried).astype(BF)
+    change = jnp.sum(carried * moved_ref[...].astype(F32), axis=0, keepdims=True)
+    ggate_ref[0] += change * (gate * (1.0 - gate))
+    carried = direct_ref[...] + gate * carried
+    carried_ref[...] = carried
+
+    @pl.when((lax.rem(n, blocks) == 0) & (place_ref[0] == 0))
+    def _():
+        ginit_ref[...] += carried
+
+    sq = merged(place_ref, sq_ref, sqo_ref)
+    k = k_ref[...]
+    s = nt(k, sq) * (factor * LOG2E)
+    p = jnp.exp2(s - jnp.max(s, axis=0, keepdims=True))
+    p = p * (1.0 / jnp.sum(p, axis=0, keepdims=True))
+    dp = nt(v_ref[...], gc)
+    ds = (p * (dp - jnp.sum(p * dp, axis=0, keepdims=True))).astype(BF)
+    next_k = jnp.where(last, rk_ref[...], nk_ref[...]).astype(F32)
+    next_v = jnp.where(last, rv_ref[...], nv_ref[...]).astype(F32)
+    gk_ref[...] = (dk_ref[...] + next_k + nn(ds, sq) * factor).astype(BF)
+    gv_ref[...] = (dv_ref[...] + next_v + nn(p.astype(BF), gc)).astype(BF)
+    gsq_ref[...] += tn(ds, k) * factor
+
+
+def pack_kernel(up_ref, down_ref, out_ref, packed_ref):
+    hidden = up_ref.shape[1]
+    packed_ref[:, :hidden] = up_ref[...]
+    packed_ref[:, hidden : 2 * hidden] = down_ref[...].T
+    packed_ref[:, 2 * hidden :] = out_ref[...].T
+
+
+def unpack_kernel(packed_ref, up_ref, down_ref, out_ref):
+    hidden = up_ref.shape[1]
+    up_ref[...] = packed_ref[:, :hidden].astype(F32)
+    down_ref[...] = packed_ref[:, hidden : 2 * hidden].astype(F32).T
+    out_ref[...] = packed_ref[:, 2 * hidden :].astype(F32).T
+
+
+def out_kernel(att_ref, wo_ref, tok_ref, gain_ref, mid_ref, min_ref):
+    t = pl.program_id(0)
+    part = nt(att_ref[...], flat(wo_ref))
+
+    @pl.when(t == 0)
+    def _():
+        mid_ref[...] = tok_ref[...].astype(F32) + part
+
+    @pl.when(t > 0)
+    def _():
+        mid_ref[...] += part
+
+    @pl.when(t == pl.num_programs(0) - 1)
+    def _():
+        x = mid_ref[...].astype(BF).astype(F32)
+        min_ref[...] = (x * inverse_rms(x) * gain_ref[...]).astype(BF)
+
+
+def mlp_kernel(
+    place_ref, min_ref, cot_ref, mid_ref, gain_ref, wu_ref, wd_ref,
+    out_ref, gmid_ref, ggain_ref, gw_ref,
+    min_t, cot_t, out_acc, gm_acc, hidden_ref,
+):
+    tile = pl.program_id(0)
+    which = pl.program_id(1)
+
+    @pl.when((tile == 0) & (which == 0))
+    def _():
+        min_t[...] = min_ref[...].T
+        cot_t[...] = cot_ref[...].T
+        out_acc[...] = jnp.zeros_like(out_acc)
+        gm_acc[...] = jnp.zeros_like(gm_acc)
+
+    @pl.when(which == 0)
+    def _():
+        wu = flat(wu_ref)
+        wd = flat(wd_ref)
+        pre = nn(min_ref[...], wu)
+        cdf = 0.5 + 0.5 * lax.erf(pre * (0.5**0.5))
+        density = jnp.exp2(pre * pre * (-0.5 * LOG2E)) * ((2.0 * np.pi) ** -0.5)
+        hidden_ref[...] = (pre * cdf).astype(BF)
+        grad_pre = (nn(cot_ref[...], wd) * (cdf + pre * density)).astype(BF)
+        out_acc[...] += nt(hidden_ref[...], wd)
+        gm_acc[...] += nt(grad_pre, wu)
+        grad = nn(min_t[...], grad_pre).astype(BF)
+        gw_ref[...] = grad.reshape(gw_ref.shape)
+
+    @pl.when(which == 1)
+    def _():
+        grad = nn(cot_t[...], hidden_ref[...]).astype(BF)
+        gw_ref[...] = grad.reshape(gw_ref.shape)
+
+    @pl.when((tile == pl.num_programs(0) - 1) & (which == 1))
+    def _():
+        mid = mid_ref[...]
+        lanes = out_ref.shape[2]
+        for part in range(out_ref.shape[0]):
+            at = slice(part * lanes, (part + 1) * lanes)
+            out_ref[part] = (mid[:, at] + out_acc[:, at]).astype(BF)
+        x = mid.astype(BF).astype(F32)
+        inverse = inverse_rms(x)
+        normed = x * inverse
+        gm = gm_acc[...]
+        ggain_ref[...] = jnp.sum(gm * normed, axis=0, keepdims=True)
+        scaled = gm * gain_ref[...]
+        back = inverse * (scaled - normed * jnp.mean(scaled * normed, axis=-1, keepdims=True))
+        gmid_ref[...] = (cot_ref[...].astype(F32) + back).astype(BF)
+
+
+def out_back_kernel(gmid_ref, wo_ref, att_ref, late_ref, gatt_ref, gwo_ref, gmid_t):
+    @pl.when(pl.program_id(0) == 0)
+    def _():
+        gmid_t[...] = gmid_ref[...].T
+
+    gatt_ref[...] = nn(gmid_ref[...], flat(wo_ref)).astype(BF)
+    gwo_ref[...] = nn(gmid_t[...], att_ref[...]).astype(BF).reshape(gwo_ref.shape)
+
+
+def project_back_kernel(
+    place_ref, tok_ref, gmid_ref, gain_ref, gq_ref, gk_ref, gv_ref,
+    wq_ref, wqo_ref, wk_ref, wko_ref, wv_ref, wvo_ref, gsq_ref, ginit_ref, gmk_ref, gmv_ref,
+    gtok_ref, ggain_ref, gown_ref, gother_ref, ain_t, acc_ref, pack_ref,
+):
+    t = pl.program_id(0)
+
+    @pl.when(t == 0)
+    def _():
+        x = tok_ref[...].astype(F32)
+        ain_t[...] = (x * inverse_rms(x) * gain_ref[...]).astype(BF).T
+        acc_ref[...] = jnp.zeros_like(acc_ref)
+
+    groups, _, lanes = pack_ref.shape
+    at = 0
+    for g_ref, w_ref, w_other in (
+        (gq_ref, wq_ref, wqo_ref), (gk_ref, wk_ref, wko_ref), (gv_ref, wv_ref, wvo_ref)
+    ):
+        g = g_ref[...]
+        acc_ref[...] += nt(g, merged(place_ref, w_ref, w_other))
+        grad = nn(ain_t[...], g).astype(BF)
+        rows = grad.shape[0] // groups
+        pack_ref[:, at : at + rows] = grad.reshape(groups, rows, lanes)
+        at += rows
+    for g_ref in (gsq_ref, ginit_ref):
+        rows = g_ref.shape[0] // groups
+        pack_ref[:, at : at + rows] = g_ref[...].astype(BF).reshape(groups, rows, lanes)
+        at += rows
+    for g_ref in (gmk_ref, gmv_ref):
+        rows = HEAD_SIZE // groups
+        for item in range(g_ref.shape[0]):
+            where = slice(item * HEAD_SIZE, (item + 1) * HEAD_SIZE)
+            pack_ref[:, at : at + rows, where] = g_ref[item].astype(BF).reshape(groups, rows, -1)
+        at += rows
+    pack_ref[:, at:] = jnp.zeros_like(pack_ref[:, at:])
+    for index in range(groups // 2):
+        gown_ref[0, index] = pack_ref[2 * index + place_ref[0]]
+        gother_ref[0, index] = pack_ref[2 * index + 1 - place_ref[0]]
+
+    @pl.when(t == pl.num_programs(0) - 1)
+    def _():
+        x = tok_ref[...].astype(F32)
+        inverse = inverse_rms(x)
+        normed = x * inverse
+        ga = acc_ref[...]
+        ggain_ref[...] = jnp.sum(ga * normed, axis=0, keepdims=True)
+        scaled = ga * gain_ref[...]
+        back = inverse * (scaled - normed * jnp.mean(scaled * normed, axis=-1, keepdims=True))
+        grad = (gmid_ref[...].astype(F32) + back).astype(BF)
+        for part in range(gtok_ref.shape[0]):
+            gtok_ref[part] = grad[:, part * lanes : (part + 1) * lanes]
+
+
+def distance_bucket(distance):
+    magnitude = np.abs(distance)
+    scaled = np.log(np.maximum(magnitude, 1) / 8.0) / np.log(16.0) * 8.0
+    far = np.minimum(8 + np.floor(np.maximum(scaled, 0.0)).astype(np.int32), 15)
+    return (distance < 0).astype(np.int32) * 16 + np.where(magnitude < 8, magnitude, far)
+
+
+def one_hot(distance, valid, bucket_count):
+    hot = distance_bucket(distance)[:, None] == np.arange(bucket_count)[None, :]
+    return jnp.asarray((hot & valid[:, None]).astype(np.float32))
+
+
+def carry(value, power, axis, backward):
+    count = lax.axis_size(axis)
+    sign = -1 if backward else 1
+    total = from_behind(value.astype(BF), axis, sign).astype(F32)
+    step = 1
+    while step < count - 1:
+        moved = from_behind(total.astype(BF), axis, sign * step).astype(F32)
+        total = total + power**step * moved
+        step *= 2
+    return total
+
+
+def across(value, axis, bit):
+    count = lax.axis_size(axis)
+    return lax.ppermute(value, axis, [(source, source ^ bit) for source in range(count)])
+
+
+def take(value, index, dim):
+    return lax.dynamic_index_in_dim(value, index, dim, False)
+
+
+def add_low(left, right):
+    return (left.astype(F32) + right.astype(F32)).astype(BF)
+
+
+def ordered(bit, own, other, dim):
+    first = bit == 0
+    return jnp.stack([jnp.where(first, own, other), jnp.where(first, other, own)], axis=dim)
+
+
+def gather_pairs(item):
+    shards = lax.axis_size("tp")
+    half = shards // 2
+    tp = lax.axis_index("tp")
+    x_bit = lax.axis_index("dp") % 2
+    y_bit = lax.axis_index("dp") // 2
+    parts = [item] + [across(item, "tp", k) for k in range(1, shards)]
+    bit = 1
+    while bit < shards:
+        swap = (tp & bit) > 0
+        parts = [jnp.where(swap, parts[k ^ bit], parts[k]) for k in range(shards)]
+        bit *= 2
+    low = jnp.stack(parts[:half])
+    high = jnp.stack(parts[half:])
+    low_x = across(low, "dp", 1)
+    high_y = across(high, "dp", 2)
+    low = ordered(x_bit, low, low_x, 0)
+    high = ordered(y_bit, high, high_y, 0)
+    low_y = across(low, "dp", 2)
+    high_x = across(high, "dp", 1)
+    low = ordered(y_bit, low, low_y, 0)
+    high = ordered(x_bit, high, high_x, 1)
+    own = jnp.stack([low, high]).reshape((2, 4, half) + item.shape)
+    return own, across(own, "ctx", 1)
+
+
+def scatter_pairs(own, other):
+    shards = own.shape[0]
+    half = shards // 2
+    tp = lax.axis_index("tp")
+    x_bit = lax.axis_index("dp") % 2
+    y_bit = lax.axis_index("dp") // 2
+    grid = (shards, 2, 2) + own.shape[2:]
+    moved = across(other, "ctx", 1).reshape(grid)
+    own = own.reshape(grid)
+
+    def both(part, index, dim):
+        return add_low(take(own[part], index, dim), take(moved[part], index, dim))
+
+    first, second = slice(0, half), slice(half, shards)
+    low_moved = across(both(first, 1 - x_bit, 2), "dp", 1)
+    high_moved = across(both(second, 1 - y_bit, 1), "dp", 2)
+    low = add_low(both(first, x_bit, 2), low_moved)
+    high = add_low(both(second, y_bit, 1), high_moved)
+    low_moved = across(take(low, 1 - y_bit, 1), "dp", 2)
+    high_moved = across(take(high, 1 - x_bit, 1), "dp", 1)
+    low = add_low(take(low, y_bit, 1), low_moved)
+    high = add_low(take(high, x_bit, 1), high_moved)
+    kept = jnp.concatenate([low, high])
+    total = take(kept, tp, 0).astype(F32)
+    for k in range(1, shards):
+        total = total + across(take(kept, tp ^ k, 0), "tp", k).astype(F32)
+    return total
+
+
+def sequence_body(
+    tokens, cotangent, prefix, w_query, w_key, w_value, w_out, w_up, w_down,
+    state_query, state_init, gain_attn, gain_mlp, bias_table, gate_bias, state_key, state_value,
+):
+    shards = lax.axis_size("tp")
+    groups = lax.axis_size("dp") * lax.axis_size("ctx")
+    pairs = lax.axis_size("dp")
+    half = shards // 2
+    everywhere = ("tp", "dp", "ctx")
+    seq_count, length, shard_width = tokens.shape
+    width = cotangent.shape[2]
+    seqs = seq_count // shards
+    blocks = length // BLOCK
+    units = seqs * blocks
+    rows = units * BLOCK
+    local_heads = bias_table.shape[0]
+    heads = local_heads * shards
+    buckets = bias_table.shape[1] * groups
+    own_rows = w_query.shape[0]
+    own_slots = state_query.shape[0]
+    slots = own_slots * groups
+    hidden = w_up.shape[1]
+    tp_index = lax.axis_index("tp")
+    ctx_index = lax.axis_index("ctx")
+    dp_index = lax.axis_index("dp")
+    head = HEAD_SIZE
+    map_rows = state_key.shape[1]
+    place = jnp.stack([ctx_index, tp_index]).astype(jnp.int32)
+
+    def call(kernel, grid, in_specs, out_specs, out_shape, scratch=(), prefetch=1, **more):
+        return pl.pallas_call(
+            kernel,
+            grid_spec=pltpu.PrefetchScalarGridSpec(
+                num_scalar_prefetch=prefetch, grid=grid, in_specs=in_specs, out_specs=out_specs,
+                scratch_shapes=list(scratch),
+            ),
+            out_shape=out_shape,
+            compiler_params=params(),
+            **more,
+        )
+
+    vectors = (gain_attn, gain_mlp, gate_bias, bias_table)
+    sizes = [item.size for item in vectors]
+    tail = jnp.concatenate([item.reshape(-1) for item in vectors])
+    tail = jnp.pad(tail, (0, 16 * shard_width - tail.size)).reshape(16, shard_width)
+
+    def beside(item):
+        return jnp.moveaxis(item, 0, 1).reshape(map_rows, shard_width)
+
+    first_own, first_other = gather_pairs(jnp.concatenate([w_query, w_key, w_value, tail], axis=0))
+    x = lax.all_to_all(tokens, "tp", 0, 2, tiled=True).reshape(rows, width)
+    second_own, second_other = gather_pairs(
+        jnp.concatenate(
+            [state_query, state_init, beside(state_key), beside(state_value)], axis=0
+        )
+    )
+    late_width = 2 * hidden + shard_width
+    late = pl.pallas_call(
+        pack_kernel, out_shape=jax.ShapeDtypeStruct((own_rows, late_width), BF)
+    )(w_up, w_down, w_out)
+    late = lax.all_gather(late, everywhere, axis=0, tiled=True)
+    late = late.reshape(shards, groups, own_rows, late_width)
+
+    at_tail = 3 * own_rows
+    small = ordered(
+        ctx_index, first_own[:, :, :, at_tail], first_other[:, :, :, at_tail], 2
+    )
+    small = jnp.moveaxis(small, 3, 1).reshape(shards, groups, shard_width)
+    ends = np.cumsum([0] + sizes)
+
+    def spread(index):
+        item = small[:, :, ends[index] : ends[index + 1]]
+        item = item.reshape(shards, groups, local_heads, -1)
+        return jnp.moveaxis(item, 1, 2).reshape(heads, -1).astype(F32)
+
+    gain_one = spread(0).reshape(1, width)
+    gain_two = spread(1).reshape(1, width)
+    gate = jax.nn.sigmoid(spread(2)).reshape(1, width)
+    bias_rows = spread(3)
+
+    def whole(shape):
+        return pl.BlockSpec(shape, lambda *_: (0,) * len(shape))
+
+    def weight(index):
+        spec = pl.BlockSpec(
+            (1, pairs, 1, own_rows, shard_width), lambda t, *_: (t // half, 0, t % half, index, 0)
+        )
+        return [spec, spec]
+
+    def of_head(count, index):
+        def at(h, *_):
+            t = h // local_heads
+            return (t // half, 0, t % half, index, h % local_heads)
+
+        spec = pl.BlockSpec((1, pairs, 1, count, head), at)
+        return [spec, spec]
+
+    column = pl.BlockSpec((rows, shard_width), lambda t, *_: (0, t))
+    wide = jax.ShapeDtypeStruct((rows, width), BF)
+    wide32 = jax.ShapeDtypeStruct((rows, width), F32)
+    split = jax.ShapeDtypeStruct((shards, rows, shard_width), BF)
+    queries, keys, values, _ = call(
+        project_kernel,
+        (shards,),
+        [whole((rows, width)), whole((1, width))] + weight(0) + weight(1) + weight(2),
+        [column, column, column, whole((rows, width))],
+        [wide] * 4,
+    )(place, x, gain_one, *([first_own, first_other] * 3))
+
+    key_blocks = keys.reshape(seqs, blocks, BLOCK, width)
+    value_blocks = values.reshape(seqs, blocks, BLOCK, width)
+    halo_keys = from_behind(key_blocks[:, -1], "ctx", 1).reshape(seqs * BLOCK, width)
+    halo_values = from_behind(value_blocks[:, -1], "ctx", 1).reshape(seqs * BLOCK, width)
+
+    def along(rows_of, index):
+        return pl.BlockSpec((rows_of, head), lambda h, n, *_: (index(n), h))
+
+    def turned(n):
+        return units - 1 - n
+
+    query_slots = of_head(own_slots, 0)
+    init_slots = of_head(own_slots, 1)
+    key_maps = of_head(map_rows, 2 * own_slots // map_rows)
+    value_maps = of_head(map_rows, 2 * own_slots // map_rows + 1)
+    channel = pl.BlockSpec((1, head), lambda h, n, *_: (0, h))
+    slot_rows = units * slots
+    slot_f32 = jax.ShapeDtypeStruct((slot_rows, width), F32)
+    slot_low = jax.ShapeDtypeStruct((slot_rows, width), BF)
+    message = jax.ShapeDtypeStruct((seqs * slots, width), BF)
+    slot_scratch = pltpu.VMEM((slots, head), F32)
+    own = along(BLOCK, lambda n: n)
+    slot = along(slots, lambda n: n)
+    slot_of_seq = along(slots, lambda n: n // blocks)
+    contrib, accumulated = call(
+        functools.partial(read_kernel, blocks=blocks),
+        (heads, units),
+        query_slots + [own, own, channel],
+        [slot, slot_of_seq],
+        [slot_f32, message],
+        [slot_scratch],
+    )(place, second_own, second_other, keys, values, gate)
+    power = gate**blocks
+    lead = carry(accumulated, power, "ctx", False)
+    lead_power = jnp.ones_like(gate)
+    for step in range(lax.axis_size("ctx") - 1):
+        lead_power = jnp.where(ctx_index > step, lead_power * power, lead_power)
+
+    block_at = ctx_index * blocks + jnp.arange(blocks, dtype=jnp.int32)
+    own_prefix = lax.dynamic_slice_in_dim(prefix, tp_index * seqs, seqs, 0)
+    info = jnp.stack(
+        [
+            jnp.broadcast_to(block_at[None], (seqs, blocks)),
+            own_prefix[:, None] - block_at[None] * BLOCK,
+        ],
+        axis=-1,
+    ).reshape(units, 2)
+    span = 4 * BLOCK
+    offset = np.arange(span)
+    offset = np.where(offset < 2 * BLOCK, offset, offset - span)
+    forward_hot = one_hot(BLOCK - offset, offset > -BLOCK, buckets)
+    back_span = 3 * BLOCK
+    back_offset = np.arange(back_span)
+    back_offset = np.where(back_offset < BLOCK, back_offset, back_offset - back_span)
+    backward_hot = one_hot(BLOCK + back_offset, back_offset > -2 * BLOCK, buckets)
+    exact = lax.Precision.HIGHEST
+    scaled_bias = bias_rows * LOG2E
+    forward_bias = jnp.dot(scaled_bias, forward_hot.T, precision=exact)[:, None]
+    backward_bias = jnp.dot(scaled_bias, backward_hot.T, precision=exact)[:, None]
+
+    def attend_specs(index):
+        before = along(BLOCK, lambda n: jnp.maximum(index(n) - 1, 0))
+        by_seq = along(BLOCK, lambda n: index(n) // blocks)
+        here = along(BLOCK, index)
+        return [here, here, here, before, before, by_seq, by_seq] + key_maps + value_maps
+
+    def lse_spec(index):
+        return pl.BlockSpec((1, 1, 1, BLOCK), lambda h, n, *_: (index(n), h, 0, 0))
+
+    def vector(size):
+        return pl.BlockSpec((1, 1, size), lambda h, *_: (h, 0, 0))
+
+    attend_args = (
+        place, info, queries, keys, values, keys, values, halo_keys, halo_values,
+        second_own, second_other, second_own, second_other,
+    )
+    attended, lse, states, moved = call(
+        functools.partial(attend_kernel, blocks=blocks),
+        (heads, units),
+        attend_specs(lambda n: n)
+        + [slot] + init_slots + [slot_of_seq, channel, channel, vector(span)],
+        [own, lse_spec(lambda n: n), slot, slot],
+        [wide, jax.ShapeDtypeStruct((units, heads, 1, BLOCK), F32), slot_low, slot_low],
+        [pltpu.VMEM((BLOCK, 2 * BLOCK), F32), slot_scratch],
+        2,
+    )(*attend_args, contrib, second_own, second_other, lead, lead_power, gate, forward_bias)
+
+    out_weight = pl.BlockSpec(
+        (1, groups, own_rows, shard_width), lambda t, *_: (t, 0, 0, 2 * hidden // shard_width)
+    )
+    middle, mlp_in = pl.pallas_call(
+        out_kernel,
+        grid=(shards,),
+        in_specs=[column, out_weight, whole((rows, width)), whole((1, width))],
+        out_specs=[whole((rows, width)), whole((rows, width))],
+        out_shape=[wide32, wide],
+        compiler_params=params(),
+    )(attended, late, x, gain_two)
+
+    tile = 512
+    per_shard = hidden // tile
+    tile_block = (1, groups, own_rows, tile)
+    output, middle_grad, gain_two_grad, late_grad = call(
+        mlp_kernel,
+        (shards * per_shard, 2),
+        [
+            whole((rows, width)),
+            pl.BlockSpec((rows, width), lambda i, j, place_ref: (place_ref[1], 0)),
+            whole((rows, width)), whole((1, width)),
+            pl.BlockSpec(tile_block, lambda i, j, *_: (i // per_shard, 0, 0, i % per_shard)),
+            pl.BlockSpec(
+                tile_block, lambda i, j, *_: (i // per_shard, 0, 0, per_shard + i % per_shard)
+            ),
+        ],
+        [
+            whole((shards, rows, shard_width)), whole((rows, width)), whole((1, width)),
+            pl.BlockSpec(
+                tile_block, lambda i, j, *_: (i // per_shard, 0, 0, j * per_shard + i % per_shard)
+            ),
+        ],
+        [
+            split, wide, jax.ShapeDtypeStruct((1, width), F32),
+            jax.ShapeDtypeStruct((shards, groups, own_rows, late_width), BF),
+        ],
+        [
+            pltpu.VMEM((width, rows), BF), pltpu.VMEM((width, rows), BF),
+            pltpu.VMEM((rows, width), F32), pltpu.VMEM((rows, width), F32),
+            pltpu.VMEM((rows, tile), BF),
+        ],
+    )(
+        place, mlp_in, cotangent.reshape(seq_count * length, width), middle, gain_two, late, late
+    )
+    output = lax.all_to_all(output, "tp", 0, 0, tiled=True)
+
+    grad_attended, late_grad = pl.pallas_call(
+        out_back_kernel,
+        grid=(shards,),
+        in_specs=[
+            whole((rows, width)), out_weight, column, pl.BlockSpec(memory_space=pl.ANY)
+        ],
+        out_specs=[column, out_weight],
+        out_shape=[wide, jax.ShapeDtypeStruct(late_grad.shape, BF)],
+        scratch_shapes=[pltpu.VMEM((width, rows), BF)],
+        compiler_params=params(),
+        input_output_aliases={3: 1},
+    )(middle_grad, late, attended, late_grad)
+    late_grad = lax.psum_scatter(
+        late_grad.reshape(shards * groups * own_rows, late_width), everywhere,
+        scatter_dimension=0, tiled=True,
+    )
+    up_grad, down_grad, out_grad = pl.pallas_call(
+        unpack_kernel,
+        out_shape=[
+            jax.ShapeDtypeStruct(w_up.shape, F32), jax.ShapeDtypeStruct(w_down.shape, F32),
+            jax.ShapeDtypeStruct(w_out.shape, F32),
+        ],
+    )(late_grad)
+
+    head_sum = jax.ShapeDtypeStruct((heads, head, head), F32)
+    head_map = pl.BlockSpec((1, head, head), lambda h, n, *_: (h, 0, 0))
+    back_own = along(BLOCK, turned)
+    back_slot = along(slots, turned)
+    back_of_seq = along(slots, lambda n: turned(n) // blocks)
+    (
+        grad_queries, dk, dv, dk_before, dv_before, direct, key_map_grad, value_map_grad,
+        bias_sum, gathered,
+    ) = call(
+        functools.partial(attend_back_kernel, blocks=blocks),
+        (heads, units),
+        attend_specs(turned)
+        + [back_slot, channel, vector(back_span), back_own, back_own, lse_spec(turned)],
+        [back_own] * 5 + [back_slot, head_map, head_map, vector(back_span), back_of_seq],
+        [
+            wide, wide32, wide32, wide, wide, slot_f32, head_sum, head_sum,
+            jax.ShapeDtypeStruct((heads, 1, back_span), F32), message,
+        ],
+        [
+            pltpu.VMEM((2 * BLOCK, BLOCK), F32), pltpu.VMEM((128, back_span), F32),
+            pltpu.VMEM((BLOCK, head), F32), slot_scratch,
+        ],
+        2,
+    )(*attend_args, states, gate, backward_bias, grad_attended, attended, lse)
+    sum_at = np.arange(back_span) - BLOCK
+    sum_hot = one_hot(sum_at, sum_at > -BLOCK, buckets)
+    bias_grad = jnp.dot(bias_sum[:, 0], sum_hot, precision=exact)
+
+    later = carry(gathered, power, "ctx", True)
+    first_keys = dk_before.reshape(seqs, blocks, BLOCK, width)[:, 0]
+    first_values = dv_before.reshape(seqs, blocks, BLOCK, width)[:, 0]
+    back_keys = from_behind(first_keys, "ctx", -1).reshape(seqs * BLOCK, width)
+    back_values = from_behind(first_values, "ctx", -1).reshape(seqs * BLOCK, width)
+    following = along(BLOCK, lambda n: jnp.minimum(turned(n) + 1, units - 1))
+    key_of_seq = along(BLOCK, lambda n: turned(n) // blocks)
+    kept_slot = pl.BlockSpec((slots, head), lambda h, n, *_: (0, h))
+    slot_sum = jax.ShapeDtypeStruct((slots, width), F32)
+    grad_keys, grad_values, slot_query_grad, init_grad, gate_grad = call(
+        functools.partial(read_back_kernel, blocks=blocks),
+        (heads, units),
+        query_slots
+        + [back_own, back_own, back_slot, back_slot, back_of_seq, channel]
+        + [back_own, back_own, following, following, key_of_seq, key_of_seq],
+        [back_own, back_own, kept_slot, kept_slot, vector(head)],
+        [wide, wide, slot_sum, slot_sum, jax.ShapeDtypeStruct((heads, 1, head), F32)],
+        [slot_scratch],
+    )(
+        place, second_own, second_other, keys, values, direct, moved, later, gate,
+        dk, dv, dk_before, dv_before, back_keys, back_values,
+    )
+
+    at_slots = 3 * own_rows
+    at_init = at_slots + own_slots
+    at_maps = at_init + own_slots
+    at_vectors = at_maps + 2 * map_rows
+    full_rows = at_vectors + 16
+    maps_of = pl.BlockSpec((local_heads, head, head), lambda t, *_: (t, 0, 0))
+    slots_of = pl.BlockSpec((slots, shard_width), lambda t, *_: (0, t))
+    piece = pl.BlockSpec((1, pairs, full_rows, shard_width), lambda t, *_: (t, 0, 0, 0))
+    pieces = jax.ShapeDtypeStruct((shards, pairs, full_rows, shard_width), BF)
+    token_grad, gain_one_grad, grad_own, grad_other = call(
+        project_back_kernel,
+        (shards,),
+        [whole((rows, width)), whole((rows, width)), whole((1, width)), column, column, column]
+        + weight(0) + weight(1) + weight(2) + [slots_of, slots_of, maps_of, maps_of],
+        [whole((shards, rows, shard_width)), whole((1, width)), piece, piece],
+        [split, jax.ShapeDtypeStruct((1, width), F32), pieces, pieces],
+        [
+            pltpu.VMEM((width, rows), BF), pltpu.VMEM((rows, width), F32),
+            pltpu.VMEM((groups, full_rows, shard_width), BF),
+        ],
+    )(
+        place, x, middle_grad, gain_one, grad_queries, grad_keys, grad_values,
+        *([first_own, first_other] * 3), slot_query_grad, init_grad, key_map_grad, value_map_grad,
+    )
+    token_grad = lax.all_to_all(token_grad, "tp", 0, 0, tiled=True)
+
+    vector_sums = [gain_one_grad, gain_two_grad, gate_grad.reshape(1, width), bias_grad]
+    vector_rows = jnp.concatenate([item.reshape(-1) for item in vector_sums])
+    vector_rows = jnp.pad(vector_rows, (0, 16 * shard_width - vector_rows.size)).astype(BF)
+    vector_rows = jnp.broadcast_to(
+        vector_rows.reshape(1, 1, 16, shard_width), (shards, pairs, 16, shard_width)
+    )
+    grad_own = lax.dynamic_update_slice(grad_own, vector_rows, (0, 0, at_vectors, 0))
+    grad_other = lax.dynamic_update_slice(grad_other, vector_rows, (0, 0, at_vectors, 0))
+    grads = scatter_pairs(grad_own, grad_other)
+    vector_grads = grads[at_vectors:].reshape(-1)
+    group = dp_index * lax.axis_size("ctx") + ctx_index
+
+    def own_part(index, like):
+        begin = sum(item.size for item in vector_sums[:index])
+        item = vector_grads[begin : begin + vector_sums[index].size].reshape(heads, -1)
+        return lax.dynamic_slice(
+            item, (tp_index * local_heads, group * like.shape[1]), like.shape
+        )
+
+    def apart(item):
+        return jnp.moveaxis(item.reshape(map_rows, local_heads, head), 1, 0)
+
+    return (
+        output.reshape(seq_count, length, shard_width),
+        token_grad.reshape(seq_count, length, shard_width),
+        grads[:own_rows],
+        grads[own_rows : 2 * own_rows],
+        grads[2 * own_rows : at_slots],
+        out_grad,
+        up_grad,
+        down_grad,
+        grads[at_slots:at_init],
+        grads[at_init:at_maps],
+        own_part(0, gain_attn),
+        own_part(1, gain_mlp),
+        own_part(3, bias_table),
+        own_part(2, gate_bias),
+        apart(grads[at_maps : at_maps + map_rows]),
+        apart(grads[at_maps + map_rows : at_vectors]),
+    )
+
+
+def choose(tokens, *others):
+    shards = lax.axis_size("tp")
+    even = tokens.shape[0] % shards == 0 and shards % 2 == 0 and shards & (shards - 1) == 0
+    even = even and lax.axis_size("dp") == 4 and lax.axis_size("ctx") == 2
+    return (sequence_body if even else body)(tokens, *others)
+
+
 def solution(mesh):
     in_specs = (
         P("dp", "ctx", "tp"),
@@ -657,4 +1603,4 @@
         P("tp", ("dp", "ctx"), None),
         P("tp", ("dp", "ctx"), None),
     )
-    return jax.shard_map(body, mesh=mesh, in_specs=in_specs, out_specs=out_specs, check_vma=False)
+    return jax.shard_map(choose, mesh=mesh, in_specs=in_specs, out_specs=out_specs, check_vma=False)

time: 2690 us -> 713 us (0.27)
  matrix products: 877 us -> 3.36 us
  waiting for transfers between devices: 1090 us -> 263 us
  other arithmetic: 322 us -> 24 us
  Pallas kernels: 0 us -> 290 us
  blocking collectives: 159 us -> 0 us
  local copies, waits for them, and re-layouts: 206 us -> 52.9 us
  starting transfers between devices: 8.54 us -> 53.8 us
    dot_general x142 -> x3, matrix products: 877 us -> 3.36 us  [the longest x1 2.16 us: sequence_body(): forward_bias = jnp.dot(scaled_bias, forward_hot.T, precision=exact)[:, None]]
    reduce_scatter x10 -> x1, waiting for transfers between devices: 546 us -> 0.01 us  [sequence_body(): lax.psum_scatter(late_grad.reshape(shards * groups * own_rows, late_width...]
    psum x1 -> x0, waiting for transfers between devices: 291 us -> none  [body(): lax.psum(part_middle.reshape(seq_count, length, full_width).astype(jnp.bf...]
    pallas_call x0 -> x11, Pallas kernels: none -> 290 us  [the longest x1 71.8 us: sequence_body(): call(mlp_kernel, (shards * per_shard, 2), [whole((rows, width)), pl.Block...]
    ppermute x0 -> x24, waiting for transfers between devices: none -> 185 us  [across(): lax.ppermute(value, axis, [(source, source ^ bit) for source in range(cou...]
    all_gather x6 -> x1, waiting for transfers between devices: 185 us -> 0.02 us  [sequence_body(): late = lax.all_gather(late, everywhere, axis=0, tiled=True)]
    all_gather x15 -> x0, blocking collectives: 136 us -> none  [the longest x1 11.5 us: body(): lax.all_gather(gain_one, 'tp', axis=0, tiled=True)]
    convert_element_type x41 -> x9, other arithmetic: 123 us -> 11.3 us  [the longest x6 8.14 us: add_low(): return (left.astype(F32) + right.astype(F32)).astype(BF)]
  transfers between devices with their start and end apart: 27 -> 35, of which waited for: 13 -> 19; matrix products, arithmetic and copies ran while one was open for 15% -> 10% of each run, Pallas kernels for 0% -> 28%
where the time goes in v1:
time: 713 us; the launch traced here: 702 us
  Pallas kernels  290 us (41%)
  waiting for transfers between devices  263 us (37%)
  starting transfers between devices  53.8 us (8%)
  local copies, waits for them, and re-layouts  52.9 us (7%)
  other arithmetic  24 us (3%)
  between operations  15 us (2%)
    ppermute x24, waiting for transfers between devices, across(): lax.ppermute(value, axis, [(source, source ^ bit) for source in range(cou...  185 us
    pallas_call x1, Pallas kernels, sequence_body(): call(mlp_kernel, (shards * per_shard, 2), [whole((rows, width)), pl.Block...  71.8 us
    pallas_call x1, Pallas kernels, sequence_body(): call(functools.partial(attend_back_kernel, blocks=blocks), (heads, units)...  68.4 us
    all_to_all x1, waiting for transfers between devices, sequence_body(): output = lax.all_to_all(output, 'tp', 0, 0, tiled=True)  66.2 us
    pallas_call x1, Pallas kernels, sequence_body(): call(functools.partial(attend_kernel, blocks=blocks), (heads, units), att...  42.2 us
    pallas_call x1, Pallas kernels, sequence_body(): call(functools.partial(read_back_kernel, blocks=blocks), (heads, units),...  29.2 us
    ppermute x24, starting transfers between devices, across(): lax.ppermute(value, axis, [(source, source ^ bit) for source in range(cou...  27.4 us
    pallas_call x1, Pallas kernels, sequence_body(): call(project_back_kernel, (shards,), [whole((rows, width)), whole((rows,...  24.8 us
  transfers between devices with their start and end apart: 35, of which 19 were waited for; matrix products, arithmetic and copies ran while one was open for 10% of the time, Pallas kernels for 28%

profile of v1, /device:TPU:0, one launch (start us, length us, event | category | flops | bytes accessed | tf_op | source)
XLA Modules:
  0.0 702.2 jit_solution(18202678342165796622)
XLA Ops:
  14.0 5.1 collective-permute-start
  19.8 6.3 collective-permute-done
  26.1 23.1 %collective-permute-done.1 = bf16[400,256]{1,0:T(8,128)(2,1)S(1)} collective-permute-done((bf16[400,256]{1,0:T(8,128)(2,1)S(1)}, bf16[400,256]{1,0:T(8,128)(2,1)S(1)}, u32[]{:S(2)}, u32[]{:S(2)}) %collective-permute-start.1) | collective-permute-done | bytes 204832 | tf_op jit(solution)/shard_map/ppermute | solution.py:1104
  52.5 13.3 %collective-permute-done.3 = bf16[2,400,256]{2,1,0:T(8,128)(2,1)S(1)} collective-permute-done((bf16[2,400,256]{2,1,0:T(8,128)(2,1)S(1)}, bf16[2,400,256]{2,1,0:T(8,128)(2,1)S(1)}, u32[]{:S(2)}, u32[]{:S(2)}) %collective-permute-start.3) | collective-permute-done | bytes 409632 | tf_op jit(solution)/shard_map/ppermute | solution.py:1104
  65.8 3.3 collective-permute-done.5
  72.8 4.5 all-to-all-start
  77.4 17.1 %collective-permute-done.6 = bf16[2,2,400,256]{3,2,1,0:T(8,128)(2,1)} collective-permute-done((bf16[2,2,400,256]{3,2,1,0:T(8,128)(2,1)}, bf16[2,2,400,256]{3,2,1,0:T(8,128)(2,1)}, u32[]{:S(2)}, u32[]{:S(2)}) %collective-permute-start.6) | collective-permute-done | bytes 819232 | tf_op jit(solution)/shard_map/ppermute | solution.py:1104
  99.8 2.7 collective-permute-start.12
  102.5 21.2 %collective-permute-done.10 = bf16[160,256]{1,0:T(8,128)(2,1)S(1)} collective-permute-done((bf16[160,256]{1,0:T(8,128)(2,1)S(1)}, bf16[160,256]{1,0:T(8,128)(2,1)S(1)}, u32[]{:S(2)}, u32[]{:S(2)}) %collective-permute-start.10) | collective-permute-done | bytes 81952 | tf_op jit(solution)/shard_map/ppermute | solution.py:1104
  123.7 30.2 %collective-permute-done.11 = bf16[160,256]{1,0:T(8,128)(2,1)S(1)} collective-permute-done((bf16[160,256]{1,0:T(8,128)(2,1)S(1)}, bf16[160,256]{1,0:T(8,128)(2,1)S(1)}, u32[]{:S(2)}, u32[]{:S(2)}) %collective-permute-start.11) | collective-permute-done | bytes 81952 | tf_op jit(solution)/shard_map/ppermute | solution.py:1104
  156.7 6.9 collective-permute-done.13
  167.1 8.8 %collective-permute-done.16 = bf16[2,2,160,256]{3,2,1,0:T(8,128)(2,1)S(1)} collective-permute-done((bf16[2,2,160,256]{3,2,1,0:T(8,128)(2,1)S(1)}, bf16[2,2,160,256]{3,2,1,0:T(8,128)(2,1)S(1)}, u32[]{:S(2)}, u32[]{:S(2)}) %collective-permute-start.16) | collective-permute-done | bytes 327712 | tf_op jit(solution)/shard_map/ppermute | solution.py:1104
  178.0 3.2 copy.80
  187.7 12.3 %shard_map.315 = (bf16[1024,1024]{1,0:T(8,128)(2,1)}, bf16[1024,1024]{1,0:T(8,128)(2,1)}, bf16[1024,1024]{1,0:T(8,128)(2,1)}, bf16[1024,1024]{1,0:T(8,128)(2,1)}) custom-call(s32[2]{0:T(128)} %pad_add_fusion.place_ref, bf16[1024,1024]{1,0:T(8,128)(2,1)} %bitcast.173, f32[1,1024]{1,0:T(1,128)} %reshape.355.gain_ref, bf16[2,4,2,400,256]{4,3,2,1,0:T(8,128)(2,1)} %copy-done.2, ...), custom_call_target="tpu_custom_call" | custom-call | tf_op jit(solution)/shard_map/pallas_call | solution.py:1276
  200.0 18.3 %shard_map.316 = (f32[1024,1024]{1,0:T(8,128)}, bf16[512,1024]{1,0:T(8,128)(2,1)}) custom-call(s32[2]{0:T(128)} %pad_add_fusion.place_ref, bf16[2,4,2,160,256]{4,3,2,1,0:T(8,128)(2,1)} %pad_maximum_fusion.3.sq_ref.wk_ref.wv_ref.init_ref, bf16[2,4,2,160,256]{4,3,2,1,0:T(8,128)(2,1)} %collective-permute-done.17.sqo_ref.wko_ref.wvo_ref.inito_ref, ...), custom_call_target="tpu_custom_call" | custom-call | tf_op jit(solution)/shard_map/pallas_call | solution.py:1308
  218.3 2.8 collective-permute-start.18
  235.7 42.2 %shard_map.317 = (bf16[1024,1024]{1,0:T(8,128)(2,1)}, f32[2,8,1,512]{3,2,1,0:T(1,128)}, bf16[1024,1024]{1,0:T(8,128)(2,1)}, bf16[1024,1024]{1,0:T(8,128)(2,1)}) custom-call(s32[2]{0:T(128)} %pad_add_fusion.place_ref, s32[2,2]{1,0:T(2,128)} %add_bitcast_fusion.info_ref, bf16[1024,1024]{1,0:T(8,128)(2,1)} %get-tuple-element.55.q_ref, ...), custom_call_target="tpu_custom_call" | custom-call | tf_op jit(solution)/shard_map/pallas_call | solution.py:1360
  278.0 10.0 %shard_map.319 = (f32[1024,1024]{1,0:T(8,128)}, bf16[1024,1024]{1,0:T(8,128)(2,1)}) custom-call(bf16[1024,1024]{1,0:T(8,128)(2,1)} %get-tuple-element.60.att_ref.o_ref, bf16[4,8,128,2304]{3,2,1,0:T(8,128)(2,1)} %bitcast.166, bf16[1024,1024]{1,0:T(8,128)(2,1)} %bitcast.174, f32[1,1024]{1,0:T(1,128)} %reshape.359.gain_ref), custom_call_target="tpu_custom_call" | custom-call | tf_op jit(solution)/shard_map/pallas_call | solution.py:1374
  288.0 71.8 %shard_map.320 = (bf16[4,1024,256]{2,1,0:T(8,128)(2,1)}, bf16[1024,1024]{1,0:T(8,128)(2,1)}, f32[1,1024]{1,0:T(1,128)}, bf16[4,8,128,2304]{3,2,1,0:T(8,128)(2,1)}) custom-call(s32[2]{0:T(128)} %pad_add_fusion.place_ref, bf16[1024,1024]{1,0:T(8,128)(2,1)} %get-tuple-element.61.min_ref, bf16[4096,1024]{1,0:T(8,128)(2,1)} %bitcast.185, ...), custom_call_target="tpu_custom_call" | custom-call | tf_op jit(solution)/shard_map/pallas_call | solution.py:1386
  359.8 9.1 %shard_map.321 = (bf16[1024,1024]{1,0:T(8,128)(2,1)}, bf16[4,8,128,2304]{3,2,1,0:T(8,128)(2,1)}) custom-call(bf16[1024,1024]{1,0:T(8,128)(2,1)} %get-tuple-element.64.gmid_ref, bf16[4,8,128,2304]{3,2,1,0:T(8,128)(2,1)} %bitcast.169, bf16[1024,1024]{1,0:T(8,128)(2,1)} %get-tuple-element.60.att_ref.o_ref, ...), custom_call_target="tpu_custom_call", output_to_operand_aliasing={{1}: (3, {})} | custom-call | tf_op jit(solution)/shard_map/pallas_call | solution.py:1418
  371.4 68.4 %shard_map.322 = (bf16[1024,1024]{1,0:T(8,128)(2,1)}, f32[1024,1024]{1,0:T(8,128)}, f32[1024,1024]{1,0:T(8,128)}, bf16[1024,1024]{1,0:T(8,128)(2,1)}, bf16[1024,...) custom-call(s32[2]{0:T(128)} %pad_add_fusion.place_ref, ...), custom_call_target="tpu_custom_call" | custom-call | tf_op jit(solution)/shard_map/pallas_call | solution.py:1450
  447.9 6.4 collective-permute-done.19
  461.5 29.2 %shard_map.323 = (bf16[1024,1024]{1,0:T(8,128)(2,1)}, bf16[1024,1024]{1,0:T(8,128)(2,1)}, f32[512,1024]{1,0:T(8,128)}, f32[512,1024]{1,0:T(8,128)}, f32[8,1,128]{2,1,0:T(1,128)}) custom-call(s32[2]{0:T(128)} %pad_add_fusion.place_ref, bf16[2,4,2,160,256]{4,3,2,1,0:T(8,128)(2,1)} %pad_maximum_fusion.3.sq_ref.wk_ref.wv_ref.init_ref, ...), custom_call_target="tpu_custom_call" | custom-call | tf_op jit(solution)/shard_map/pallas_call | solution.py:1479
  490.7 24.8 %shard_map.324 = (bf16[4,1024,256]{2,1,0:T(8,128)(2,1)}, f32[1,1024]{1,0:T(1,128)}, bf16[4,4,560,256]{3,2,1,0:T(8,128)(2,1)}, bf16[4,4,560,256]{3,2,1,0:T(8,128)(2,1)}) custom-call(s32[2]{0:T(128)} %pad_add_fusion.place_ref, bf16[1024,1024]{1,0:T(8,128)(2,1)} %bitcast.175, bf16[1024,1024]{1,0:T(8,128)(2,1)} %get-tuple-element.64.gmid_ref, ...), custom_call_target="tpu_custom_call" | custom-call | tf_op jit(solution)/shard_map/pallas_call | solution.py:1502
  517.4 7.4 %all-to-all-start.1 = ((bf16[4,1024,256]{2,1,0:T(8,128)(2,1)}), bf16[4,1024,256]{2,1,0:T(8,128)(2,1)S(1)}, u32[]{:S(2)}, u32[]{:S(2)}) async-start(bf16[4,1024,256]{2,1,0:T(8,128)(2,1)} %get-tuple-element.63), calls=%async_computation.1 | async-start | bytes 4194304 | tf_op jit(solution)/shard_map/all_to_all | solution.py:1416
  536.5 66.2 %all-to-all-done.1 = bf16[4,1024,256]{2,1,0:T(8,128)(2,1)S(1)} async-done(((bf16[4,1024,256]{2,1,0:T(8,128)(2,1)}), bf16[4,1024,256]{2,1,0:T(8,128)(2,1)S(1)}, u32[]{:S(2)}, u32[]{:S(2)}) %all-to-all-start.1) | async-done | bytes 2097184 | tf_op jit(solution)/shard_map/all_to_all | solution.py:1416
  602.7 4.7 all-to-all-start.2
  614.3 23.4 %collective-permute-done.23 = bf16[2,2,560,256]{3,2,0,1:T(8,128)(2,1)S(1)} collective-permute-done((bf16[2,2,560,256]{3,2,0,1:T(8,128)(2,1)S(1)}, bf16[2,2,560,256]{3,2,0,1:T(8,128)(2,1)S(1)}, u32[]{:S(2)}, u32[]{:S(2)}) %collective-permute-start.23) | collective-permute-done | bytes 1146912 | tf_op jit(solution)/shard_map/ppermute | solution.py:1104
  640.5 8.3 %collective-permute-done.26 = bf16[2,560,256]{2,1,0:T(8,128)(2,1)} collective-permute-done((bf16[2,560,256]{2,1,0:T(8,128)(2,1)}, bf16[2,560,256]{2,1,0:T(8,128)(2,1)}, u32[]{:S(2)}, u32[]{:S(2)}) %collective-permute-start.26) | collective-permute-done | bytes 573472 | tf_op jit(solution)/shard_map/ppermute | solution.py:1104
  658.8 9.2 %collective-permute-done.27 = bf16[560,256]{1,0:T(8,128)(2,1)S(1)} collective-permute-done((bf16[560,256]{1,0:T(8,128)(2,1)}, bf16[560,256]{1,0:T(8,128)(2,1)S(1)}, u32[]{:S(2)}, u32[]{:S(2)}) %collective-permute-start.27) | collective-permute-done | bytes 286752 | tf_op jit(solution)/shard_map/ppermute | solution.py:1104
  668.0 9.8 %collective-permute-done.28 = bf16[560,256]{1,0:T(8,128)(2,1)} collective-permute-done((bf16[560,256]{1,0:T(8,128)(2,1)}, bf16[560,256]{1,0:T(8,128)(2,1)}, u32[]{:S(2)}, u32[]{:S(2)}) %collective-permute-start.28) | collective-permute-done | bytes 286752 | tf_op jit(solution)/shard_map/ppermute | solution.py:1104
  692.1 3.0 copy.143
  (235 shorter events, 114.2 us)
Async XLA Ops:
  7.2 270.8 %all-gather.2.cloned.1.call-start = ((), (), s32[]{:S(2)}) async-start(), calls=%async_computation.4 | async-start | bytes 19464192 | tf_op jit(solution)/shard_map/all_gather | solution.py:1235
  14.0 12.1 %collective-permute-start = (bf16[400,256]{1,0:T(8,128)(2,1)S(1)}, bf16[400,256]{1,0:T(8,128)(2,1)S(1)}, u32[]{:S(2)}, u32[]{:S(2)}) collective-permute-start(bf16[400,256]{1,0:T(8,128)(2,1)S(1)} %constant_dynamic-update-slice_fusion), channel_id=1, source_target_pairs={{0,3},{1,2},{2,1},{3,0},{4,7},{5,6},{6,5},{7,4},{8,11},{9,10},{10,... | collective-permute-start | bytes 614408 | tf_op jit(solution)/shard_map/ppermute | solution.py:1104
  19.2 30.0 %collective-permute-start.1 = (bf16[400,256]{1,0:T(8,128)(2,1)S(1)}, bf16[400,256]{1,0:T(8,128)(2,1)S(1)}, u32[]{:S(2)}, u32[]{:S(2)}) collective-permute-start(bf16[400,256]{1,0:T(8,128)(2,1)S(1)} %constant_dynamic-update-slice_fusion), channel_id=1, source_target_pairs={{0,2},{1,3},{2,0},{3,1},{4,6},{5,7},{6,4},{7,5},{8,10},{9,11},{10,... | collective-permute-start | bytes 614408 | tf_op jit(solution)/shard_map/ppermute | solution.py:1104
  19.2 30.0 %collective-permute-start.2 = (bf16[400,256]{1,0:T(8,128)(2,1)S(1)}, bf16[400,256]{1,0:T(8,128)(2,1)S(1)}, u32[]{:S(2)}, u32[]{:S(2)}) collective-permute-start(bf16[400,256]{1,0:T(8,128)(2,1)S(1)} %constant_dynamic-update-slice_fusion), channel_id=1, source_target_pairs={{0,1},{1,0},{2,3},{3,2},{4,5},{5,4},{6,7},{7,6},{8,9},{9,8},{10,11... | collective-permute-start | bytes 614408 | tf_op jit(solution)/shard_map/ppermute | solution.py:1104
  49.3 16.5 %collective-permute-start.3 = (bf16[2,400,256]{2,1,0:T(8,128)(2,1)S(1)}, bf16[2,400,256]{2,1,0:T(8,128)(2,1)S(1)}, u32[]{:S(2)}, u32[]{:S(2)}) collective-permute-start(bf16[2,400,256]{2,1,0:T(8,128)(2,1)S(1)} %pad_maximum_fusion.8), channel_id=1, source_target_pairs={{0,8},{8,0},{16,24},{24,16},{1,9},{9,1},{17,25},{25,17},{2,10},{10... | collective-permute-start | bytes 1228808 | tf_op jit(solution)/shard_map/ppermute | solution.py:1104
  50.9 18.2 %collective-permute-start.5 = (bf16[2,400,256]{2,1,0:T(8,128)(2,1)S(1)}, bf16[2,400,256]{2,1,0:T(8,128)(2,1)S(1)}, u32[]{:S(2)}, u32[]{:S(2)}) collective-permute-start(bf16[2,400,256]{2,1,0:T(8,128)(2,1)S(1)} %pad_maximum_fusion.9), channel_id=1, source_target_pairs={{0,16},{8,24},{16,0},{24,8},{1,17},{9,25},{17,1},{25,9},{2,18},{10... | collective-permute-start | bytes 1228808 | tf_op jit(solution)/shard_map/ppermute | solution.py:1104
  70.2 24.2 %collective-permute-start.6 = (bf16[2,2,400,256]{3,2,1,0:T(8,128)(2,1)}, bf16[2,2,400,256]{3,2,1,0:T(8,128)(2,1)}, u32[]{:S(2)}, u32[]{:S(2)}) collective-permute-start(bf16[2,2,400,256]{3,2,1,0:T(8,128)(2,1)} %pad_maximum_fusion.5), channel_id=1, source_target_pairs={{0,8},{8,0},{16,24},{24,16},{1,9},{9,1},{17,25},{25,17},{2,10},{10... | collective-permute-start | bytes 2457608 | tf_op jit(solution)/shard_map/ppermute | solution.py:1104
  70.3 25.8 %collective-permute-start.4 = (bf16[2,2,400,256]{3,2,1,0:T(8,128)(2,1)S(1)}, bf16[2,2,400,256]{3,2,1,0:T(8,128)(2,1)S(1)}, u32[]{:S(2)}, u32[]{:S(2)}) collective-permute-start(bf16[2,2,400,256]{3,2,1,0:T(8,128)(2,1)S(1)} %pad_maximum_fusion.4), channel_id=1, source_target_pairs={{0,16},{8,24},{16,0},{24,8},{1,17},{9,25},{17,1},{25,9},{2,18},{10... | collective-permute-start | bytes 2457608 | tf_op jit(solution)/shard_map/ppermute | solution.py:1104
  72.8 105.2 %all-to-all-start = ((bf16[4,1024,256]{2,1,0:T(8,128)(2,1)}), bf16[4,1024,256]{2,1,0:T(8,128)(2,1)}, u32[]{:S(2)}, u32[]{:S(2)}) async-start(bf16[4,1024,256]{2,1,0:T(8,128)(2,1)} %param.20), calls=%async_computation | async-start | bytes 4194304 | tf_op jit(solution)/shard_map/all_to_all | solution.py:1225
  77.3 611.2 %reduce-scatter.2.cloned.1.call-start = ((), (), s32[]{:S(2)}) async-start(), calls=%async_computation.5 | async-start | bytes 19464192 | tf_op jit(solution)/shard_map/reduce_scatter | solution.py:1430
  97.8 85.3 %collective-permute-start.7 = (bf16[2,4,2,400,256]{4,3,2,1,0:T(8,128)(2,1)S(1)}, bf16[2,4,2,400,256]{4,3,2,1,0:T(8,128)(2,1)}, u32[]{:S(2)}, u32[]{:S(2)}) collective-permute-start(bf16[2,4,2,400,256]{4,3,2,1,0:T(8,128)(2,1)S(1)} %pad_maximum_fusion.wq_ref.wk_ref.wv_ref), channel_id=1, source_target_pairs={{0,4},{4,0},{1,5},{5,1},{2,6},{6,2},{3,7},{7,3},{8,12},{12,8},{9,1... | collective-permute-start | bytes 9830408 | tf_op jit(solution)/shard_map/ppermute | solution.py:1104
  98.1 25.7 %collective-permute-start.10 = (bf16[160,256]{1,0:T(8,128)(2,1)S(1)}, bf16[160,256]{1,0:T(8,128)(2,1)S(1)}, u32[]{:S(2)}, u32[]{:S(2)}) collective-permute-start(bf16[160,256]{1,0:T(8,128)(2,1)S(1)} %constant_dynamic-update-slice_fusion.4), channel_id=1, source_target_pairs={{0,3},{1,2},{2,1},{3,0},{4,7},{5,6},{6,5},{7,4},{8,11},{9,10},{10,... | collective-permute-start | bytes 245768 | tf_op jit(solution)/shard_map/ppermute | solution.py:1104
  99.8 54.2 %collective-permute-start.11 = (bf16[160,256]{1,0:T(8,128)(2,1)S(1)}, bf16[160,256]{1,0:T(8,128)(2,1)S(1)}, u32[]{:S(2)}, u32[]{:S(2)}) collective-permute-start(bf16[160,256]{1,0:T(8,128)(2,1)S(1)} %constant_dynamic-update-slice_fusion.4), channel_id=1, source_target_pairs={{0,2},{1,3},{2,0},{3,1},{4,6},{5,7},{6,4},{7,5},{8,10},{9,11},{10,... | collective-permute-start | bytes 245768 | tf_op jit(solution)/shard_map/ppermute | solution.py:1104
  99.8 54.2 %collective-permute-start.12 = (bf16[160,256]{1,0:T(8,128)(2,1)S(1)}, bf16[160,256]{1,0:T(8,128)(2,1)S(1)}, u32[]{:S(2)}, u32[]{:S(2)}) collective-permute-start(bf16[160,256]{1,0:T(8,128)(2,1)S(1)} %constant_dynamic-update-slice_fusion.4), channel_id=1, source_target_pairs={{0,1},{1,0},{2,3},{3,2},{4,5},{5,4},{6,7},{7,6},{8,9},{9,8},{10,11... | collective-permute-start | bytes 245768 | tf_op jit(solution)/shard_map/ppermute | solution.py:1104
  156.2 10.1 %collective-permute-start.15 = (bf16[2,160,256]{2,1,0:T(8,128)(2,1)S(1)}, bf16[2,160,256]{2,1,0:T(8,128)(2,1)S(1)}, u32[]{:S(2)}, u32[]{:S(2)}) collective-permute-start(bf16[2,160,256]{2,1,0:T(8,128)(2,1)S(1)} %pad_maximum_fusion.13), channel_id=1, source_target_pairs={{0,16},{8,24},{16,0},{24,8},{1,17},{9,25},{17,1},{25,9},{2,18},{10... | collective-permute-start | bytes 491528 | tf_op jit(solution)/shard_map/ppermute | solution.py:1104
  177.4 22.5 %collective-permute-start.17 = (bf16[2,4,2,160,256]{4,3,2,1,0:T(8,128)(2,1)}, bf16[2,4,2,160,256]{4,3,2,1,0:T(8,128)(2,1)}, u32[]{:S(2)}, u32[]{:S(2)}) collective-permute-start(bf16[2,4,2,160,256]{4,3,2,1,0:T(8,128)(2,1)} %pad_maximum_fusion.3.sq_ref.wk_ref.wv_ref.init_ref), channel_id=1, source_target_pairs={{0,4},{4,0},{1,5},{5,1},{2,6},{6,2},{3,7},{7,3},{8,12},{12,8},{9,1... | collective-permute-start | bytes 3932168 | tf_op jit(solution)/shard_map/ppermute | solution.py:1104
  218.3 14.5 %collective-permute-start.18 = (bf16[512,1024]{1,0:T(8,128)(2,1)}, bf16[512,1024]{1,0:T(8,128)(2,1)S(1)}, u32[]{:S(2)}, u32[]{:S(2)}) collective-permute-start(bf16[512,1024]{1,0:T(8,128)(2,1)} %get-tuple-element.59), channel_id=1, source_target_pairs={{0,4},{1,5},{2,6},{3,7},{8,12},{9,13},{10,14},{11,15},{16,20},{17,... | collective-permute-start | bytes 3145736 | tf_op jit(solution)/shard_map/ppermute | solution.py:24
  222.1 12.2 %collective-permute-start.8 = (bf16[1,512,1024]{2,1,0:T(8,128)(2,1)}, bf16[1,512,1024]{2,1,0:T(8,128)(2,1)S(1)}, u32[]{:S(2)}, u32[]{:S(2)}) collective-permute-start(bf16[1,512,1024]{2,1,0:T(8,128)(2,1)} %slice_bitcast_fusion.3), channel_id=1, source_target_pairs={{0,4},{1,5},{2,6},{3,7},{8,12},{9,13},{10,14},{11,15},{16,20},{17,... | collective-permute-start | bytes 3145736 | tf_op jit(solution)/shard_map/ppermute | solution.py:24
  224.7 9.7 %collective-permute-start.9 = (bf16[1,512,1024]{2,1,0:T(8,128)(2,1)}, bf16[1,512,1024]{2,1,0:T(8,128)(2,1)S(1)}, u32[]{:S(2)}, u32[]{:S(2)}) collective-permute-start(bf16[1,512,1024]{2,1,0:T(8,128)(2,1)} %slice_bitcast_fusion.2), channel_id=1, source_target_pairs={{0,4},{1,5},{2,6},{3,7},{8,12},{9,13},{10,14},{11,15},{16,20},{17,... | collective-permute-start | bytes 3145736 | tf_op jit(solution)/shard_map/ppermute | solution.py:24
  439.7 14.6 %collective-permute-start.19 = (bf16[512,1024]{1,0:T(8,128)(2,1)}, bf16[512,1024]{1,0:T(8,128)(2,1)S(1)}, u32[]{:S(2)}, u32[]{:S(2)}) collective-permute-start(bf16[512,1024]{1,0:T(8,128)(2,1)} %get-tuple-element.72), channel_id=1, source_target_pairs={{4,0},{5,1},{6,2},{7,3},{12,8},{13,9},{14,10},{15,11},{20,16},{21,... | collective-permute-start | bytes 3145736 | tf_op jit(solution)/shard_map/ppermute | solution.py:24
  443.6 14.5 %collective-permute-start.20 = (bf16[1,512,1024]{2,1,0:T(8,128)(2,1)}, bf16[1,512,1024]{2,1,0:T(8,128)(2,1)S(1)}, u32[]{:S(2)}, u32[]{:S(2)}) collective-permute-start(bf16[1,512,1024]{2,1,0:T(8,128)(2,1)} %slice_bitcast_fusion.1), channel_id=1, source_target_pairs={{4,0},{5,1},{6,2},{7,3},{12,8},{13,9},{14,10},{15,11},{20,16},{21,... | collective-permute-start | bytes 3145736 | tf_op jit(solution)/shard_map/ppermute | solution.py:24
  446.0 14.6 %collective-permute-start.21 = (bf16[1,512,1024]{2,1,0:T(8,128)(2,1)}, bf16[1,512,1024]{2,1,0:T(8,128)(2,1)S(1)}, u32[]{:S(2)}, u32[]{:S(2)}) collective-permute-start(bf16[1,512,1024]{2,1,0:T(8,128)(2,1)} %slice_bitcast_fusion), channel_id=1, source_target_pairs={{4,0},{5,1},{6,2},{7,3},{12,8},{13,9},{14,10},{15,11},{20,16},{21,... | collective-permute-start | bytes 3145736 | tf_op jit(solution)/shard_map/ppermute | solution.py:24
  517.1 12.6 %collective-permute-start.22 = (bf16[4,4,560,256]{3,2,1,0:T(8,128)(2,1)}, bf16[4,4,560,256]{3,2,1,0:T(8,128)(2,1)}, u32[]{:S(2)}, u32[]{:S(2)}) collective-permute-start(bf16[4,4,560,256]{3,2,1,0:T(8,128)(2,1)} %get-tuple-element.180), channel_id=1, source_target_pairs={{0,4},{4,0},{1,5},{5,1},{2,6},{6,2},{3,7},{7,3},{8,12},{12,8},{9,1... | collective-permute-start | bytes 13762568 | tf_op jit(solution)/shard_map/ppermute | solution.py:1104
  517.4 85.4 %all-to-all-start.1 = ((bf16[4,1024,256]{2,1,0:T(8,128)(2,1)}), bf16[4,1024,256]{2,1,0:T(8,128)(2,1)S(1)}, u32[]{:S(2)}, u32[]{:S(2)}) async-start(bf16[4,1024,256]{2,1,0:T(8,128)(2,1)} %get-tuple-element.63), calls=%async_computation.1 | async-start | bytes 4194304 | tf_op jit(solution)/shard_map/all_to_all | solution.py:1416
  534.9 75.9 %collective-permute-start.25 = (bf16[2,2,560,256]{3,2,0,1:T(8,128)(2,1)}, bf16[2,2,560,256]{3,2,0,1:T(8,128)(2,1)}, u32[]{:S(2)}, u32[]{:S(2)}) collective-permute-start(bf16[2,2,560,256]{3,2,0,1:T(8,128)(2,1)} %fusion.5), channel_id=1, source_target_pairs={{0,16},{8,24},{16,0},{24,8},{1,17},{9,25},{17,1},{25,9},{2,18},{10... | collective-permute-start | bytes 3440648 | tf_op jit(solution)/shard_map/ppermute | solution.py:1104
  602.7 56.1 %all-to-all-start.2 = ((bf16[4,1024,256]{2,1,0:T(8,128)(2,1)}), bf16[4,1024,256]{2,1,0:T(8,128)(2,1)}, u32[]{:S(2)}, u32[]{:S(2)}) async-start(bf16[4,1024,256]{2,1,0:T(8,128)(2,1)} %get-tuple-element.83), calls=%async_computation.2 | async-start | bytes 4194304 | tf_op jit(solution)/shard_map/all_to_all | solution.py:1517
  609.5 28.2 %collective-permute-start.23 = (bf16[2,2,560,256]{3,2,0,1:T(8,128)(2,1)S(1)}, bf16[2,2,560,256]{3,2,0,1:T(8,128)(2,1)S(1)}, u32[]{:S(2)}, u32[]{:S(2)}) collective-permute-start(bf16[2,2,560,256]{3,2,0,1:T(8,128)(2,1)S(1)} %fusion.3), channel_id=1, source_target_pairs={{0,8},{8,0},{16,24},{24,16},{1,9},{9,1},{17,25},{25,17},{2,10},{10... | collective-permute-start | bytes 3440648 | tf_op jit(solution)/shard_map/ppermute | solution.py:1104
  613.6 35.1 %collective-permute-start.26 = (bf16[2,560,256]{2,1,0:T(8,128)(2,1)}, bf16[2,560,256]{2,1,0:T(8,128)(2,1)}, u32[]{:S(2)}, u32[]{:S(2)}) collective-permute-start(bf16[2,560,256]{2,1,0:T(8,128)(2,1)} %dynamic-slice_bitcast_fusion), channel_id=1, source_target_pairs={{0,8},{8,0},{16,24},{24,16},{1,9},{9,1},{17,25},{25,17},{2,10},{10... | collective-permute-start | bytes 1720328 | tf_op jit(solution)/shard_map/ppermute | solution.py:1104
  639.1 13.0 %collective-permute-start.24 = (bf16[2,560,256]{2,1,0:T(8,128)(2,1)S(1)}, bf16[2,560,256]{2,1,0:T(8,128)(2,1)}, u32[]{:S(2)}, u32[]{:S(2)}) collective-permute-start(bf16[2,560,256]{2,1,0:T(8,128)(2,1)S(1)} %dynamic-slice_bitcast_fusion.1), channel_id=1, source_target_pairs={{0,16},{8,24},{16,0},{24,8},{1,17},{9,25},{17,1},{25,9},{2,18},{10... | collective-permute-start | bytes 1720328 | tf_op jit(solution)/shard_map/ppermute | solution.py:1104
  654.4 13.6 %collective-permute-start.27 = (bf16[560,256]{1,0:T(8,128)(2,1)}, bf16[560,256]{1,0:T(8,128)(2,1)S(1)}, u32[]{:S(2)}, u32[]{:S(2)}) collective-permute-start(bf16[560,256]{1,0:T(8,128)(2,1)} %get-tuple-element.144), channel_id=1, source_target_pairs={{0,1},{1,0},{2,3},{3,2},{4,5},{5,4},{6,7},{7,6},{8,9},{9,8},{10,11... | collective-permute-start | bytes 860168 | tf_op jit(solution)/shard_map/ppermute | solution.py:1104
  655.8 21.9 %collective-permute-start.28 = (bf16[560,256]{1,0:T(8,128)(2,1)}, bf16[560,256]{1,0:T(8,128)(2,1)}, u32[]{:S(2)}, u32[]{:S(2)}) collective-permute-start(bf16[560,256]{1,0:T(8,128)(2,1)} %get-tuple-element.145), channel_id=1, source_target_pairs={{0,2},{1,3},{2,0},{3,1},{4,6},{5,7},{6,4},{7,5},{8,10},{9,11},{10,... | collective-permute-start | bytes 860168 | tf_op jit(solution)/shard_map/ppermute | solution.py:1104
  658.1 19.6 %collective-permute-start.29 = (bf16[560,256]{1,0:T(8,128)(2,1)}, bf16[560,256]{1,0:T(8,128)(2,1)}, u32[]{:S(2)}, u32[]{:S(2)}) collective-permute-start(bf16[560,256]{1,0:T(8,128)(2,1)} %get-tuple-element.146), channel_id=1, source_target_pairs={{0,3},{1,2},{2,1},{3,0},{4,7},{5,6},{6,5},{7,4},{8,11},{9,10},{10,... | collective-permute-start | bytes 860168 | tf_op jit(solution)/shard_map/ppermute | solution.py:1104
  (35 other events, 389.2 us)
Sparse Core Ops, SparseCore 0:
  10.9 184.5 all-gather.1
  369.0 237.3 reduce-scatter.1

commit v2 on v1

--- a/solution.py
+++ b/solution.py
@@ -657,6 +657,10 @@
     return block.reshape(-1, block.shape[-1])
 
 
+def joined(tok_ref):
+    return jnp.concatenate([tok_ref[part] for part in range(tok_ref.shape[0])], axis=1).astype(F32)
+
+
 def inverse_rms(x):
     return lax.rsqrt(jnp.mean(x * x, axis=-1, keepdims=True) + EPSILON)
 
@@ -671,7 +675,7 @@
 ):
     @pl.when(pl.program_id(0) == 0)
     def _():
-        x = tok_ref[...].astype(F32)
+        x = joined(tok_ref)
         ain_ref[...] = (x * inverse_rms(x) * gain_ref[...]).astype(BF)
 
     a = ain_ref[...]
@@ -950,7 +954,7 @@
 
     @pl.when(t == 0)
     def _():
-        mid_ref[...] = tok_ref[...].astype(F32) + part
+        mid_ref[...] = joined(tok_ref) + part
 
     @pl.when(t > 0)
     def _():
@@ -1031,7 +1035,7 @@
 
     @pl.when(t == 0)
     def _():
-        x = tok_ref[...].astype(F32)
+        x = joined(tok_ref)
         ain_t[...] = (x * inverse_rms(x) * gain_ref[...]).astype(BF).T
         acc_ref[...] = jnp.zeros_like(acc_ref)
 
@@ -1063,7 +1067,7 @@
 
     @pl.when(t == pl.num_programs(0) - 1)
     def _():
-        x = tok_ref[...].astype(F32)
+        x = joined(tok_ref)
         inverse = inverse_rms(x)
         normed = x * inverse
         ga = acc_ref[...]
@@ -1117,7 +1121,7 @@
     return jnp.stack([jnp.where(first, own, other), jnp.where(first, other, own)], axis=dim)
 
 
-def gather_pairs(item):
+def gather_pairs(item, beside):
     shards = lax.axis_size("tp")
     half = shards // 2
     tp = lax.axis_index("tp")
@@ -1140,7 +1144,8 @@
     low = ordered(y_bit, low, low_y, 0)
     high = ordered(x_bit, high, high_x, 1)
     own = jnp.stack([low, high]).reshape((2, 4, half) + item.shape)
-    return own, across(own, "ctx", 1)
+    own, beside = lax.optimization_barrier((own, beside))
+    return own, across(own, "ctx", 1), beside
 
 
 def scatter_pairs(own, other):
@@ -1221,23 +1226,33 @@
     def beside(item):
         return jnp.moveaxis(item, 0, 1).reshape(map_rows, shard_width)
 
-    first_own, first_other = gather_pairs(jnp.concatenate([w_query, w_key, w_value, tail], axis=0))
-    x = lax.all_to_all(tokens, "tp", 0, 2, tiled=True).reshape(rows, width)
-    second_own, second_other = gather_pairs(
+    x = lax.all_to_all(tokens, "tp", 0, 0, tiled=True)
+    first_own, first_other, x = gather_pairs(
         jnp.concatenate(
-            [state_query, state_init, beside(state_key), beside(state_value)], axis=0
-        )
-    )
+            [
+                w_query, w_key, w_value, state_query, state_init,
+                beside(state_key), beside(state_value), tail,
+            ],
+            axis=0,
+        ),
+        x,
+    )
+    x = x.reshape(shards, rows, shard_width)
     late_width = 2 * hidden + shard_width
     late = pl.pallas_call(
         pack_kernel, out_shape=jax.ShapeDtypeStruct((own_rows, late_width), BF)
     )(w_up, w_down, w_out)
+    late, first_own = lax.optimization_barrier((late, first_own))
     late = lax.all_gather(late, everywhere, axis=0, tiled=True)
     late = late.reshape(shards, groups, own_rows, late_width)
 
-    at_tail = 3 * own_rows
+    at_slots = 3 * own_rows
+    at_init = at_slots + own_slots
+    at_maps = at_init + own_slots
+    at_vectors = at_maps + 2 * map_rows
+    full_rows = at_vectors + 16
     small = ordered(
-        ctx_index, first_own[:, :, :, at_tail], first_other[:, :, :, at_tail], 2
+        ctx_index, first_own[:, :, :, at_vectors], first_other[:, :, :, at_vectors], 2
     )
     small = jnp.moveaxis(small, 3, 1).reshape(shards, groups, shard_width)
     ends = np.cumsum([0] + sizes)
@@ -1276,7 +1291,7 @@
     queries, keys, values, _ = call(
         project_kernel,
         (shards,),
-        [whole((rows, width)), whole((1, width))] + weight(0) + weight(1) + weight(2),
+        [whole((shards, rows, shard_width)), whole((1, width))] + weight(0) + weight(1) + weight(2),
         [column, column, column, whole((rows, width))],
         [wide] * 4,
     )(place, x, gain_one, *([first_own, first_other] * 3))
@@ -1292,10 +1307,10 @@
     def turned(n):
         return units - 1 - n
 
-    query_slots = of_head(own_slots, 0)
-    init_slots = of_head(own_slots, 1)
-    key_maps = of_head(map_rows, 2 * own_slots // map_rows)
-    value_maps = of_head(map_rows, 2 * own_slots // map_rows + 1)
+    query_slots = of_head(own_slots, at_slots // own_slots)
+    init_slots = of_head(own_slots, at_init // own_slots)
+    key_maps = of_head(map_rows, at_maps // map_rows)
+    value_maps = of_head(map_rows, at_maps // map_rows + 1)
     channel = pl.BlockSpec((1, head), lambda h, n, *_: (0, h))
     slot_rows = units * slots
     slot_f32 = jax.ShapeDtypeStruct((slot_rows, width), F32)
@@ -1312,7 +1327,7 @@
         [slot, slot_of_seq],
         [slot_f32, message],
         [slot_scratch],
-    )(place, second_own, second_other, keys, values, gate)
+    )(place, first_own, first_other, keys, values, gate)
     power = gate**blocks
     lead = carry(accumulated, power, "ctx", False)
     lead_power = jnp.ones_like(gate)
@@ -1355,7 +1370,7 @@
 
     attend_args = (
         place, info, queries, keys, values, keys, values, halo_keys, halo_values,
-        second_own, second_other, second_own, second_other,
+        first_own, first_other, first_own, first_other,
     )
     attended, lse, states, moved = call(
         functools.partial(attend_kernel, blocks=blocks),
@@ -1366,7 +1381,7 @@
         [wide, jax.ShapeDtypeStruct((units, heads, 1, BLOCK), F32), slot_low, slot_low],
         [pltpu.VMEM((BLOCK, 2 * BLOCK), F32), slot_scratch],
         2,
-    )(*attend_args, contrib, second_own, second_other, lead, lead_power, gate, forward_bias)
+    )(*attend_args, contrib, first_own, first_other, lead, lead_power, gate, forward_bias)
 
     out_weight = pl.BlockSpec(
         (1, groups, own_rows, shard_width), lambda t, *_: (t, 0, 0, 2 * hidden // shard_width)
@@ -1374,7 +1389,7 @@
     middle, mlp_in = pl.pallas_call(
         out_kernel,
         grid=(shards,),
-        in_specs=[column, out_weight, whole((rows, width)), whole((1, width))],
+        in_specs=[column, out_weight, whole((shards, rows, shard_width)), whole((1, width))],
         out_specs=[whole((rows, width)), whole((rows, width))],
         out_shape=[wide32, wide],
         compiler_params=params(),
@@ -1463,6 +1478,7 @@
         ],
         2,
     )(*attend_args, states, gate, backward_bias, grad_attended, attended, lse)
+    dk, output = lax.optimization_barrier((dk, output))
     sum_at = np.arange(back_span) - BLOCK
     sum_hot = one_hot(sum_at, sum_at > -BLOCK, buckets)
     bias_grad = jnp.dot(bias_sum[:, 0], sum_hot, precision=exact)
@@ -1486,15 +1502,10 @@
         [wide, wide, slot_sum, slot_sum, jax.ShapeDtypeStruct((heads, 1, head), F32)],
         [slot_scratch],
     )(
-        place, second_own, second_other, keys, values, direct, moved, later, gate,
+        place, first_own, first_other, keys, values, direct, moved, later, gate,
         dk, dv, dk_before, dv_before, back_keys, back_values,
     )
 
-    at_slots = 3 * own_rows
-    at_init = at_slots + own_slots
-    at_maps = at_init + own_slots
-    at_vectors = at_maps + 2 * map_rows
-    full_rows = at_vectors + 16
     maps_of = pl.BlockSpec((local_heads, head, head), lambda t, *_: (t, 0, 0))
     slots_of = pl.BlockSpec((slots, shard_width), lambda t, *_: (0, t))
     piece = pl.BlockSpec((1, pairs, full_rows, shard_width), lambda t, *_: (t, 0, 0, 0))
@@ -1502,7 +1513,8 @@
     token_grad, gain_one_grad, grad_own, grad_other = call(
         project_back_kernel,
         (shards,),
-        [whole((rows, width)), whole((rows, width)), whole((1, width)), column, column, column]
+        [whole((shards, rows, shard_width)), whole((rows, width)), whole((1, width))]
+        + [column, column, column]
         + weight(0) + weight(1) + weight(2) + [slots_of, slots_of, maps_of, maps_of],
         [whole((shards, rows, shard_width)), whole((1, width)), piece, piece],
         [split, jax.ShapeDtypeStruct((1, width), F32), pieces, pieces],

time: 713 us -> 597 us (0.84)
  waiting for transfers between devices: 263 us -> 162 us
  local copies, waits for them, and re-layouts: 52.9 us -> 42.9 us
  starting transfers between devices: 53.8 us -> 46 us
    all_to_all x1, waiting for transfers between devices: 66.2 us -> 0.01 us  [sequence_body(): output = lax.all_to_all(output, 'tp', 0, 0, tiled=True)]
    ppermute x24 -> x16, waiting for transfers between devices: 185 us -> 127 us  [across(): lax.ppermute(value, axis, [(source, source ^ bit) for source in range(cou...]
    all_gather x1, waiting for transfers between devices: 0.02 us -> 20.7 us  [sequence_body(): late = lax.all_gather(late, everywhere, axis=0, tiled=True)]
    ppermute x24 -> x16, starting transfers between devices: 27.4 us -> 23.6 us  [across(): lax.ppermute(value, axis, [(source, source ^ bit) for source in range(cou...]
    unnamed x77 -> x65, local copies, waits for them, and re-layouts: 16.7 us -> 14.3 us
  transfers between devices with their start and end apart: 35 -> 27, of which waited for: 19 -> 17; matrix products, arithmetic and copies ran while one was open for 10% -> 10% of each run, Pallas kernels for 28% -> 34%
where the time goes in v2:
time: 597 us; the launch traced here: 586 us
  Pallas kernels  290 us (49%)
  waiting for transfers between devices  162 us (27%)
  starting transfers between devices  46 us (8%)
  local copies, waits for them, and re-layouts  42.9 us (7%)
  other arithmetic  26.4 us (4%)
  between operations  14.9 us (2%)
    ppermute x16, waiting for transfers between devices, across(): lax.ppermute(value, axis, [(source, source ^ bit) for source in range(cou...  127 us
    pallas_call x1, Pallas kernels, sequence_body(): call(mlp_kernel, (shards * per_shard, 2), [whole((rows, width)), pl.Block...  71.5 us
    pallas_call x1, Pallas kernels, sequence_body(): call(functools.partial(attend_back_kernel, blocks=blocks), (heads, units)...  68.4 us
    pallas_call x1, Pallas kernels, sequence_body(): call(functools.partial(attend_kernel, blocks=blocks), (heads, units), att...  42.2 us
    pallas_call x1, Pallas kernels, sequence_body(): call(functools.partial(read_back_kernel, blocks=blocks), (heads, units),...  29.1 us
    pallas_call x1, Pallas kernels, sequence_body(): call(project_back_kernel, (shards,), [whole((shards, rows, shard_width)),...  24.8 us
    ppermute x16, starting transfers between devices, across(): lax.ppermute(value, axis, [(source, source ^ bit) for source in range(cou...  23.6 us
    all_gather x1, waiting for transfers between devices, sequence_body(): late = lax.all_gather(late, everywhere, axis=0, tiled=True)  20.7 us
  transfers between devices with their start and end apart: 27, of which 17 were waited for; matrix products, arithmetic and copies ran while one was open for 10% of the time, Pallas kernels for 34%

profile of v2, /device:TPU:0, one launch (start us, length us, event | category | flops | bytes accessed | tf_op | source)
XLA Modules:
  0.0 585.7 jit_solution(3717716944379311604)
XLA Ops:
  15.0 5.1 collective-permute-start
  20.7 7.3 %collective-permute-done = bf16[560,256]{1,0:T(8,128)(2,1)S(1)} collective-permute-done((bf16[560,256]{1,0:T(8,128)(2,1)S(1)}, bf16[560,256]{1,0:T(8,128)(2,1)S(1)}, u32[]{:S(2)}, u32[]{:S(2)}) %collective-permute-start) | collective-permute-done | bytes 286752 | tf_op jit(solution)/shard_map/ppermute | solution.py:1108
  27.9 16.6 %collective-permute-done.1 = bf16[560,256]{1,0:T(8,128)(2,1)S(1)} collective-permute-done((bf16[560,256]{1,0:T(8,128)(2,1)S(1)}, bf16[560,256]{1,0:T(8,128)(2,1)S(1)}, u32[]{:S(2)}, u32[]{:S(2)}) %collective-permute-start.1) | collective-permute-done | bytes 286752 | tf_op jit(solution)/shard_map/ppermute | solution.py:1108
  49.3 3.7 all-to-all-start
  53.1 6.4 %collective-permute-done.3 = bf16[2,560,256]{2,1,0:T(8,128)(2,1)S(1)} collective-permute-done((bf16[2,560,256]{2,1,0:T(8,128)(2,1)S(1)}, bf16[2,560,256]{2,1,0:T(8,128)(2,1)S(1)}, u32[]{:S(2)}, u32[]{:S(2)}) %collective-permute-start.3) | collective-permute-done | bytes 573472 | tf_op jit(solution)/shard_map/ppermute | solution.py:1108
  69.9 20.4 %collective-permute-done.6 = bf16[2,2,560,256]{3,2,1,0:T(8,128)(2,1)} collective-permute-done((bf16[2,2,560,256]{3,2,1,0:T(8,128)(2,1)}, bf16[2,2,560,256]{3,2,1,0:T(8,128)(2,1)}, u32[]{:S(2)}, u32[]{:S(2)}) %collective-permute-start.6) | collective-permute-done | bytes 1146912 | tf_op jit(solution)/shard_map/ppermute | solution.py:1108
  96.7 3.5 all-to-all-done.tok_ref
  101.1 7.3 %collective-permute-done.7.wqo_ref.wko_ref.wvo_ref.sqo_ref.inito_ref = bf16[2,4,2,560,256]{4,3,2,1,0:T(8,128)(2,1)} collective-permute-done((bf16[2,4,2,560,256]{4,3,2,1,0:T(8,128)(2,1)}, bf16[2,4,2,560,256]{4,3,2,1,0:T(8,128)(2,1)}, u32[]{:S(2)}, u32[]{:S(2)}) %collective-permute-start.7) | collective-permute-done | bytes 4587552 | tf_op jit(solution)/shard_map/ppermute | solution.py:1108
  111.1 12.2 %shard_map.316 = (bf16[1024,1024]{1,0:T(8,128)(2,1)}, bf16[1024,1024]{1,0:T(8,128)(2,1)}, bf16[1024,1024]{1,0:T(8,128)(2,1)}, bf16[1024,1024]{1,0:T(8,128)(2,1)}) custom-call(s32[2]{0:T(128)} %pad_add_fusion.place_ref, bf16[4,1024,256]{2,1,0:T(8,128)(2,1)} %copy-done.4, f32[1,1024]{1,0:T(1,128)} %reshape.345.gain_ref, ...), custom_call_target="tpu_custom_call" | custom-call | tf_op jit(solution)/shard_map/pallas_call | solution.py:1291
  123.3 18.4 %shard_map.317 = (f32[1024,1024]{1,0:T(8,128)}, bf16[512,1024]{1,0:T(8,128)(2,1)}) custom-call(s32[2]{0:T(128)} %pad_add_fusion.place_ref, bf16[2,4,2,560,256]{4,3,2,1,0:T(8,128)(2,1)} %pad_maximum_fusion.wq_ref.wk_ref.wv_ref.sq_ref.init_ref, bf16[2,4,2,560,256]{4,3,2,1,0:T(8,128)(2,1)} %collective-permute-done.7.wqo_ref.wko_ref.wvo_ref.sqo_ref.inito_ref, ...), custom_call_target="tpu_custom_call" | custom-call | tf_op jit(solution)/shard_map/pallas_call | solution.py:1323
  158.6 42.2 %shard_map.318 = (bf16[1024,1024]{1,0:T(8,128)(2,1)}, f32[2,8,1,512]{3,2,1,0:T(1,128)}, bf16[1024,1024]{1,0:T(8,128)(2,1)}, bf16[1024,1024]{1,0:T(8,128)(2,1)}) custom-call(s32[2]{0:T(128)} %pad_add_fusion.place_ref, s32[2,2]{1,0:T(2,128)} %add_bitcast_fusion.info_ref, bf16[1024,1024]{1,0:T(8,128)(2,1)} %get-tuple-element.64.q_ref, ...), custom_call_target="tpu_custom_call" | custom-call | tf_op jit(solution)/shard_map/pallas_call | solution.py:1375
  200.8 20.7 %all-gather.2.cloned.1.call-done = bf16[4096,2304]{1,0:T(8,128)(2,1)} async-done(((bf16[128,2304]{1,0:T(8,128)(2,1)}), bf16[4096,2304]{1,0:T(8,128)(2,1)}) %all-gather.2.cloned.1.call-update) | async-done | bytes 18874384 | tf_op jit(solution)/shard_map/all_gather | solution.py:1246
  221.5 10.0 %shard_map.319 = (f32[1024,1024]{1,0:T(8,128)}, bf16[1024,1024]{1,0:T(8,128)(2,1)}) custom-call(bf16[1024,1024]{1,0:T(8,128)(2,1)} %get-tuple-element.70.att_ref.o_ref, bf16[4,8,128,2304]{3,2,1,0:T(8,128)(2,1)} %bitcast.134, bf16[4,1024,256]{2,1,0:T(8,128)(2,1)} %copy-done.4, f32[1,1024]{1,0:T(1,128)} %reshape.349.gain_ref), custom_call_target="tpu_custom_call" | custom-call | tf_op jit(solution)/shard_map/pallas_call | solution.py:1389
  231.5 71.5 %shard_map.320 = (bf16[4,1024,256]{2,1,0:T(8,128)(2,1)}, bf16[1024,1024]{1,0:T(8,128)(2,1)}, f32[1,1024]{1,0:T(1,128)}, bf16[4,8,128,2304]{3,2,1,0:T(8,128)(2,1)}) custom-call(s32[2]{0:T(128)} %pad_add_fusion.place_ref, bf16[1024,1024]{1,0:T(8,128)(2,1)} %get-tuple-element.72.min_ref, bf16[4096,1024]{1,0:T(8,128)(2,1)} %bitcast.147, ...), custom_call_target="tpu_custom_call" | custom-call | tf_op jit(solution)/shard_map/pallas_call | solution.py:1401
  303.0 9.1 %shard_map.321 = (bf16[1024,1024]{1,0:T(8,128)(2,1)}, bf16[4,8,128,2304]{3,2,1,0:T(8,128)(2,1)}) custom-call(bf16[1024,1024]{1,0:T(8,128)(2,1)} %get-tuple-element.74.gmid_ref, bf16[4,8,128,2304]{3,2,1,0:T(8,128)(2,1)} %bitcast.137, bf16[1024,1024]{1,0:T(8,128)(2,1)} %get-tuple-element.70.att_ref.o_ref, ...), custom_call_target="tpu_custom_call", output_to_operand_aliasing={{1}: (3, {})} | custom-call | tf_op jit(solution)/shard_map/pallas_call | solution.py:1433
  312.2 4.2 all-to-all-start.1
  317.8 68.4 %shard_map.322 = (bf16[1024,1024]{1,0:T(8,128)(2,1)}, f32[1024,1024]{1,0:T(8,128)}, f32[1024,1024]{1,0:T(8,128)}, bf16[1024,1024]{1,0:T(8,128)(2,1)}, bf16[1024,...) custom-call(s32[2]{0:T(128)} %pad_add_fusion.place_ref, ...), custom_call_target="tpu_custom_call" | custom-call | tf_op jit(solution)/shard_map/pallas_call | solution.py:1465
  394.3 5.2 collective-permute-done.11
  399.5 2.8 convert_element_type.199.later_ref
  404.1 2.5 collective-permute-done.13
  406.6 29.1 %shard_map.323 = (bf16[1024,1024]{1,0:T(8,128)(2,1)}, bf16[1024,1024]{1,0:T(8,128)(2,1)}, f32[512,1024]{1,0:T(8,128)}, f32[512,1024]{1,0:T(8,128)}, f32[8,1,128]{2,1,0:T(1,128)}) custom-call(s32[2]{0:T(128)} %pad_add_fusion.place_ref, bf16[2,4,2,560,256]{4,3,2,1,0:T(8,128)(2,1)} %pad_maximum_fusion.wq_ref.wk_ref.wv_ref.sq_ref.init_ref, ...), custom_call_target="tpu_custom_call" | custom-call | tf_op jit(solution)/shard_map/pallas_call | solution.py:1495
  435.8 24.8 %shard_map.324 = (bf16[4,1024,256]{2,1,0:T(8,128)(2,1)}, f32[1,1024]{1,0:T(1,128)}, bf16[4,4,560,256]{3,2,1,0:T(8,128)(2,1)}, bf16[4,4,560,256]{3,2,1,0:T(8,128)(2,1)}) custom-call(s32[2]{0:T(128)} %pad_add_fusion.place_ref, bf16[4,1024,256]{2,1,0:T(8,128)(2,1)} %copy-done.4, bf16[1024,1024]{1,0:T(8,128)(2,1)} %get-tuple-element.74.gmid_ref, ...), custom_call_target="tpu_custom_call" | custom-call | tf_op jit(solution)/shard_map/pallas_call | solution.py:1513
  462.1 2.9 collective-permute-start.14
  465.0 5.2 all-to-all-start.2
  470.1 2.7 fusion.32
  473.2 2.7 fusion.33
  478.9 32.9 %collective-permute-done.17 = bf16[2,2,560,256]{3,2,0,1:T(8,128)(2,1)S(1)} collective-permute-done((bf16[2,2,560,256]{3,2,0,1:T(8,128)(2,1)S(1)}, bf16[2,2,560,256]{3,2,0,1:T(8,128)(2,1)S(1)}, u32[]{:S(2)}, u32[]{:S(2)}) %collective-permute-start.17) | collective-permute-done | bytes 1146912 | tf_op jit(solution)/shard_map/ppermute | solution.py:1108
  516.1 13.4 %collective-permute-done.18 = bf16[2,560,256]{2,1,0:T(8,128)(2,1)S(1)} collective-permute-done((bf16[2,560,256]{2,1,0:T(8,128)(2,1)S(1)}, bf16[2,560,256]{2,1,0:T(8,128)(2,1)S(1)}, u32[]{:S(2)}, u32[]{:S(2)}) %collective-permute-start.18) | collective-permute-done | bytes 573472 | tf_op jit(solution)/shard_map/ppermute | solution.py:1108
  534.5 3.2 collective-permute-start.19
  541.2 13.4 %collective-permute-done.19 = bf16[560,256]{1,0:T(8,128)(2,1)S(1)} collective-permute-done((bf16[560,256]{1,0:T(8,128)(2,1)}, bf16[560,256]{1,0:T(8,128)(2,1)S(1)}, u32[]{:S(2)}, u32[]{:S(2)}) %collective-permute-start.19) | collective-permute-done | bytes 286752 | tf_op jit(solution)/shard_map/ppermute | solution.py:1108
  554.6 6.6 %collective-permute-done.20 = bf16[560,256]{1,0:T(8,128)(2,1)} collective-permute-done((bf16[560,256]{1,0:T(8,128)(2,1)}, bf16[560,256]{1,0:T(8,128)(2,1)}, u32[]{:S(2)}, u32[]{:S(2)}) %collective-permute-start.20) | collective-permute-done | bytes 286752 | tf_op jit(solution)/shard_map/ppermute | solution.py:1108
  575.5 3.0 copy.144
  (192 shorter events, 93.2 us)
Async XLA Ops:
  15.0 12.9 %collective-permute-start = (bf16[560,256]{1,0:T(8,128)(2,1)S(1)}, bf16[560,256]{1,0:T(8,128)(2,1)S(1)}, u32[]{:S(2)}, u32[]{:S(2)}) collective-permute-start(bf16[560,256]{1,0:T(8,128)(2,1)S(1)} %constant_dynamic-update-slice_fusion), channel_id=1, source_target_pairs={{0,3},{1,2},{2,1},{3,0},{4,7},{5,6},{6,5},{7,4},{8,11},{9,10},{10,... | collective-permute-start | bytes 860168 | tf_op jit(solution)/shard_map/ppermute | solution.py:1108
  20.1 24.4 %collective-permute-start.1 = (bf16[560,256]{1,0:T(8,128)(2,1)S(1)}, bf16[560,256]{1,0:T(8,128)(2,1)S(1)}, u32[]{:S(2)}, u32[]{:S(2)}) collective-permute-start(bf16[560,256]{1,0:T(8,128)(2,1)S(1)} %constant_dynamic-update-slice_fusion), channel_id=1, source_target_pairs={{0,2},{1,3},{2,0},{3,1},{4,6},{5,7},{6,4},{7,5},{8,10},{9,11},{10,... | collective-permute-start | bytes 860168 | tf_op jit(solution)/shard_map/ppermute | solution.py:1108
  20.1 24.4 %collective-permute-start.2 = (bf16[560,256]{1,0:T(8,128)(2,1)S(1)}, bf16[560,256]{1,0:T(8,128)(2,1)S(1)}, u32[]{:S(2)}, u32[]{:S(2)}) collective-permute-start(bf16[560,256]{1,0:T(8,128)(2,1)S(1)} %constant_dynamic-update-slice_fusion), channel_id=1, source_target_pairs={{0,1},{1,0},{2,3},{3,2},{4,5},{5,4},{6,7},{7,6},{8,9},{9,8},{10,11... | collective-permute-start | bytes 860168 | tf_op jit(solution)/shard_map/ppermute | solution.py:1108
  45.4 14.1 %collective-permute-start.3 = (bf16[2,560,256]{2,1,0:T(8,128)(2,1)S(1)}, bf16[2,560,256]{2,1,0:T(8,128)(2,1)S(1)}, u32[]{:S(2)}, u32[]{:S(2)}) collective-permute-start(bf16[2,560,256]{2,1,0:T(8,128)(2,1)S(1)} %pad_maximum_fusion.5), channel_id=1, source_target_pairs={{0,8},{8,0},{16,24},{24,16},{1,9},{9,1},{17,25},{25,17},{2,10},{10... | collective-permute-start | bytes 1720328 | tf_op jit(solution)/shard_map/ppermute | solution.py:1108
  47.8 14.1 %collective-permute-start.5 = (bf16[2,560,256]{2,1,0:T(8,128)(2,1)}, bf16[2,560,256]{2,1,0:T(8,128)(2,1)}, u32[]{:S(2)}, u32[]{:S(2)}) collective-permute-start(bf16[2,560,256]{2,1,0:T(8,128)(2,1)} %pad_maximum_fusion.6), channel_id=1, source_target_pairs={{0,16},{8,24},{16,0},{24,8},{1,17},{9,25},{17,1},{25,9},{2,18},{10... | collective-permute-start | bytes 1720328 | tf_op jit(solution)/shard_map/ppermute | solution.py:1108
  49.3 50.8 %all-to-all-start = ((bf16[4,1024,256]{2,1,0:T(8,128)(2,1)}), bf16[4,1024,256]{2,1,0:T(8,128)(2,1)S(1)}, u32[]{:S(2)}, u32[]{:S(2)}) async-start(bf16[4,1024,256]{2,1,0:T(8,128)(2,1)} %param.20), calls=%async_computation | async-start | bytes 4194304 | tf_op jit(solution)/shard_map/all_to_all | solution.py:1229
  53.1 168.4 %all-gather.2.cloned.1.call-start = ((), (), s32[]{:S(2)}) async-start(), calls=%async_computation.4 | async-start | bytes 19464192 | tf_op jit(solution)/shard_map/all_gather | solution.py:1246
  64.8 25.5 %collective-permute-start.6 = (bf16[2,2,560,256]{3,2,1,0:T(8,128)(2,1)}, bf16[2,2,560,256]{3,2,1,0:T(8,128)(2,1)}, u32[]{:S(2)}, u32[]{:S(2)}) collective-permute-start(bf16[2,2,560,256]{3,2,1,0:T(8,128)(2,1)} %pad_maximum_fusion.4), channel_id=1, source_target_pairs={{0,8},{8,0},{16,24},{24,16},{1,9},{9,1},{17,25},{25,17},{2,10},{10... | collective-permute-start | bytes 3440648 | tf_op jit(solution)/shard_map/ppermute | solution.py:1108
  66.4 26.0 %collective-permute-start.4 = (bf16[2,2,560,256]{3,2,1,0:T(8,128)(2,1)}, bf16[2,2,560,256]{3,2,1,0:T(8,128)(2,1)}, u32[]{:S(2)}, u32[]{:S(2)}) collective-permute-start(bf16[2,2,560,256]{3,2,1,0:T(8,128)(2,1)} %pad_maximum_fusion.3), channel_id=1, source_target_pairs={{0,16},{8,24},{16,0},{24,8},{1,17},{9,25},{17,1},{25,9},{2,18},{10... | collective-permute-start | bytes 3440648 | tf_op jit(solution)/shard_map/ppermute | solution.py:1108
  100.2 11.0 %copy-start.4 = (bf16[4,1024,256]{2,1,0:T(8,128)(2,1)}, bf16[4,1024,256]{2,1,0:T(8,128)(2,1)S(1)}, u32[]{:S(2)}) copy-start(bf16[4,1024,256]{2,1,0:T(8,128)(2,1)S(1)} %all-to-all-done.tok_ref) | copy-start | bytes 6291460
  100.2 471.8 %reduce-scatter.2.cloned.1.call-start = ((), (), s32[]{:S(2)}) async-start(), calls=%async_computation.5 | async-start | bytes 19464192 | tf_op jit(solution)/shard_map/reduce_scatter | solution.py:1445
  100.2 8.1 %collective-permute-start.7 = (bf16[2,4,2,560,256]{4,3,2,1,0:T(8,128)(2,1)}, bf16[2,4,2,560,256]{4,3,2,1,0:T(8,128)(2,1)}, u32[]{:S(2)}, u32[]{:S(2)}) collective-permute-start(bf16[2,4,2,560,256]{4,3,2,1,0:T(8,128)(2,1)} %pad_maximum_fusion.wq_ref.wk_ref.wv_ref.sq_ref.init_ref), channel_id=1, source_target_pairs={{0,4},{4,0},{1,5},{5,1},{2,6},{6,2},{3,7},{7,3},{8,12},{12,8},{9,1... | collective-permute-start | bytes 13762568 | tf_op jit(solution)/shard_map/ppermute | solution.py:1108
  123.3 20.7 %copy-start.2 = (bf16[1024,1024]{1,0:T(8,128)(2,1)S(1)}, bf16[1024,1024]{1,0:T(8,128)(2,1)}, u32[]{:S(2)}) copy-start(bf16[1024,1024]{1,0:T(8,128)(2,1)} %get-tuple-element.65.k_ref.kp_ref) | copy-start | bytes 6291460
  141.8 14.0 %collective-permute-start.10 = (bf16[512,1024]{1,0:T(8,128)(2,1)}, bf16[512,1024]{1,0:T(8,128)(2,1)S(1)}, u32[]{:S(2)}, u32[]{:S(2)}) collective-permute-start(bf16[512,1024]{1,0:T(8,128)(2,1)} %get-tuple-element.68), channel_id=1, source_target_pairs={{0,4},{1,5},{2,6},{3,7},{8,12},{9,13},{10,14},{11,15},{16,20},{17,... | collective-permute-start | bytes 3145736 | tf_op jit(solution)/shard_map/ppermute | solution.py:24
  145.1 10.0 %copy-start.21 = (f32[1,1024]{1,0:T(1,128)S(1)}, f32[1,1024]{1,0:T(1,128)}, u32[]{:S(2)}) copy-start(f32[1,1024]{1,0:T(1,128)} %reshape.348.gate_ref) | copy-start | bytes 12292
  145.1 12.1 %collective-permute-start.8 = (bf16[1,512,1024]{2,1,0:T(8,128)(2,1)}, bf16[1,512,1024]{2,1,0:T(8,128)(2,1)S(1)}, u32[]{:S(2)}, u32[]{:S(2)}) collective-permute-start(bf16[1,512,1024]{2,1,0:T(8,128)(2,1)} %slice_bitcast_fusion.3), channel_id=1, source_target_pairs={{0,4},{1,5},{2,6},{3,7},{8,12},{9,13},{10,14},{11,15},{16,20},{17,... | collective-permute-start | bytes 3145736 | tf_op jit(solution)/shard_map/ppermute | solution.py:24
  147.7 9.6 %collective-permute-start.9 = (bf16[1,512,1024]{2,1,0:T(8,128)(2,1)}, bf16[1,512,1024]{2,1,0:T(8,128)(2,1)S(1)}, u32[]{:S(2)}, u32[]{:S(2)}) collective-permute-start(bf16[1,512,1024]{2,1,0:T(8,128)(2,1)} %slice_bitcast_fusion.2), channel_id=1, source_target_pairs={{0,4},{1,5},{2,6},{3,7},{8,12},{9,13},{10,14},{11,15},{16,20},{17,... | collective-permute-start | bytes 3145736 | tf_op jit(solution)/shard_map/ppermute | solution.py:24
  312.2 90.1 %all-to-all-start.1 = ((bf16[4,1024,256]{2,1,0:T(8,128)(2,1)}), bf16[4,1024,256]{2,1,0:T(8,128)(2,1)S(1)}, u32[]{:S(2)}, u32[]{:S(2)}) async-start(bf16[4,1024,256]{2,1,0:T(8,128)(2,1)} %get-tuple-element.79), calls=%async_computation.1 | async-start | bytes 4194304 | tf_op jit(solution)/shard_map/all_to_all | solution.py:1431
  386.2 13.3 %collective-permute-start.11 = (bf16[512,1024]{1,0:T(8,128)(2,1)}, bf16[512,1024]{1,0:T(8,128)(2,1)}, u32[]{:S(2)}, u32[]{:S(2)}) collective-permute-start(bf16[512,1024]{1,0:T(8,128)(2,1)} %get-tuple-element.84), channel_id=1, source_target_pairs={{4,0},{5,1},{6,2},{7,3},{12,8},{13,9},{14,10},{15,11},{20,16},{21,... | collective-permute-start | bytes 3145736 | tf_op jit(solution)/shard_map/ppermute | solution.py:24
  390.1 14.0 %collective-permute-start.12 = (bf16[1,512,1024]{2,1,0:T(8,128)(2,1)}, bf16[1,512,1024]{2,1,0:T(8,128)(2,1)S(1)}, u32[]{:S(2)}, u32[]{:S(2)}) collective-permute-start(bf16[1,512,1024]{2,1,0:T(8,128)(2,1)} %slice_bitcast_fusion.1), channel_id=1, source_target_pairs={{4,0},{5,1},{6,2},{7,3},{12,8},{13,9},{14,10},{15,11},{20,16},{21,... | collective-permute-start | bytes 3145736 | tf_op jit(solution)/shard_map/ppermute | solution.py:24
  392.4 14.2 %collective-permute-start.13 = (bf16[1,512,1024]{2,1,0:T(8,128)(2,1)}, bf16[1,512,1024]{2,1,0:T(8,128)(2,1)}, u32[]{:S(2)}, u32[]{:S(2)}) collective-permute-start(bf16[1,512,1024]{2,1,0:T(8,128)(2,1)} %slice_bitcast_fusion), channel_id=1, source_target_pairs={{4,0},{5,1},{6,2},{7,3},{12,8},{13,9},{14,10},{15,11},{20,16},{21,... | collective-permute-start | bytes 3145736 | tf_op jit(solution)/shard_map/ppermute | solution.py:24
  435.8 25.5 %copy-start.24 = (f32[8,1,128]{2,1,0:T(1,128)S(1)}, f32[8,1,128]{2,1,0:T(1,128)}, u32[]{:S(2)}) copy-start(f32[8,1,128]{2,1,0:T(1,128)} %get-tuple-element.99) | copy-start | bytes 12292
  462.1 11.1 %collective-permute-start.14 = (bf16[4,4,560,256]{3,2,1,0:T(8,128)(2,1)}, bf16[4,4,560,256]{3,2,1,0:T(8,128)(2,1)}, u32[]{:S(2)}, u32[]{:S(2)}) collective-permute-start(bf16[4,4,560,256]{3,2,1,0:T(8,128)(2,1)} %get-tuple-element.180), channel_id=1, source_target_pairs={{0,4},{4,0},{1,5},{5,1},{2,6},{6,2},{3,7},{7,3},{8,12},{12,8},{9,1... | collective-permute-start | bytes 13762568 | tf_op jit(solution)/shard_map/ppermute | solution.py:1108
  465.0 76.3 %all-to-all-start.2 = ((bf16[4,1024,256]{2,1,0:T(8,128)(2,1)}), bf16[4,1024,256]{2,1,0:T(8,128)(2,1)}, u32[]{:S(2)}, u32[]{:S(2)}) async-start(bf16[4,1024,256]{2,1,0:T(8,128)(2,1)} %get-tuple-element.95), calls=%async_computation.2 | async-start | bytes 4194304 | tf_op jit(solution)/shard_map/all_to_all | solution.py:1529
  476.4 35.5 %collective-permute-start.17 = (bf16[2,2,560,256]{3,2,0,1:T(8,128)(2,1)S(1)}, bf16[2,2,560,256]{3,2,0,1:T(8,128)(2,1)S(1)}, u32[]{:S(2)}, u32[]{:S(2)}) collective-permute-start(bf16[2,2,560,256]{3,2,0,1:T(8,128)(2,1)S(1)} %fusion.5), channel_id=1, source_target_pairs={{0,16},{8,24},{16,0},{24,8},{1,17},{9,25},{17,1},{25,9},{2,18},{10... | collective-permute-start | bytes 3440648 | tf_op jit(solution)/shard_map/ppermute | solution.py:1108
  478.3 35.1 %collective-permute-start.15 = (bf16[2,2,560,256]{3,2,0,1:T(8,128)(2,1)S(1)}, bf16[2,2,560,256]{3,2,0,1:T(8,128)(2,1)S(1)}, u32[]{:S(2)}, u32[]{:S(2)}) collective-permute-start(bf16[2,2,560,256]{3,2,0,1:T(8,128)(2,1)S(1)} %fusion.3), channel_id=1, source_target_pairs={{0,8},{8,0},{16,24},{24,16},{1,9},{9,1},{17,25},{25,17},{2,10},{10... | collective-permute-start | bytes 3440648 | tf_op jit(solution)/shard_map/ppermute | solution.py:1108
  512.3 17.2 %collective-permute-start.18 = (bf16[2,560,256]{2,1,0:T(8,128)(2,1)S(1)}, bf16[2,560,256]{2,1,0:T(8,128)(2,1)S(1)}, u32[]{:S(2)}, u32[]{:S(2)}) collective-permute-start(bf16[2,560,256]{2,1,0:T(8,128)(2,1)S(1)} %dynamic-slice_bitcast_fusion), channel_id=1, source_target_pairs={{0,8},{8,0},{16,24},{24,16},{1,9},{9,1},{17,25},{25,17},{2,10},{10... | collective-permute-start | bytes 1720328 | tf_op jit(solution)/shard_map/ppermute | solution.py:1108
  515.0 17.1 %collective-permute-start.16 = (bf16[2,560,256]{2,1,0:T(8,128)(2,1)}, bf16[2,560,256]{2,1,0:T(8,128)(2,1)}, u32[]{:S(2)}, u32[]{:S(2)}) collective-permute-start(bf16[2,560,256]{2,1,0:T(8,128)(2,1)} %dynamic-slice_bitcast_fusion.1), channel_id=1, source_target_pairs={{0,16},{8,24},{16,0},{24,8},{1,17},{9,25},{17,1},{25,9},{2,18},{10... | collective-permute-start | bytes 1720328 | tf_op jit(solution)/shard_map/ppermute | solution.py:1108
  516.1 16.0 %copy-start.10 = (bf16[2,2,560,256]{3,2,0,1:T(8,128)(2,1)S(1)}, bf16[2,2,560,256]{3,2,0,1:T(8,128)(2,1)}, u32[]{:S(2)}) copy-start(bf16[2,2,560,256]{3,2,0,1:T(8,128)(2,1)} %copy-done.9) | copy-start | bytes 3440644
  534.5 20.2 %collective-permute-start.19 = (bf16[560,256]{1,0:T(8,128)(2,1)}, bf16[560,256]{1,0:T(8,128)(2,1)S(1)}, u32[]{:S(2)}, u32[]{:S(2)}) collective-permute-start(bf16[560,256]{1,0:T(8,128)(2,1)} %get-tuple-element.156), channel_id=1, source_target_pairs={{0,1},{1,0},{2,3},{3,2},{4,5},{5,4},{6,7},{7,6},{8,9},{9,8},{10,11... | collective-permute-start | bytes 860168 | tf_op jit(solution)/shard_map/ppermute | solution.py:1108
  537.7 23.5 %collective-permute-start.20 = (bf16[560,256]{1,0:T(8,128)(2,1)}, bf16[560,256]{1,0:T(8,128)(2,1)}, u32[]{:S(2)}, u32[]{:S(2)}) collective-permute-start(bf16[560,256]{1,0:T(8,128)(2,1)} %get-tuple-element.157), channel_id=1, source_target_pairs={{0,2},{1,3},{2,0},{3,1},{4,6},{5,7},{6,4},{7,5},{8,10},{9,11},{10,... | collective-permute-start | bytes 860168 | tf_op jit(solution)/shard_map/ppermute | solution.py:1108
  539.9 21.3 %collective-permute-start.21 = (bf16[560,256]{1,0:T(8,128)(2,1)}, bf16[560,256]{1,0:T(8,128)(2,1)}, u32[]{:S(2)}, u32[]{:S(2)}) collective-permute-start(bf16[560,256]{1,0:T(8,128)(2,1)} %get-tuple-element.158), channel_id=1, source_target_pairs={{0,3},{1,2},{2,1},{3,0},{4,7},{5,6},{6,5},{7,4},{8,11},{9,10},{10,... | collective-permute-start | bytes 860168 | tf_op jit(solution)/shard_map/ppermute | solution.py:1108
  (21 other events, 70.9 us)
Sparse Core Ops, SparseCore 0:
  100.3 121.1 all-gather.1
  312.3 238.2 reduce-scatter.1

commit v3 on v2

--- a/solution.py
+++ b/solution.py
@@ -671,7 +671,7 @@
 
 def project_kernel(
     place_ref, tok_ref, gain_ref, wq_ref, wqo_ref, wk_ref, wko_ref, wv_ref, wvo_ref,
-    q_ref, k_ref, v_ref, ain_ref,
+    q_ref, k_ref, v_ref, ain_ref, lastk_ref, lastv_ref,
 ):
     @pl.when(pl.program_id(0) == 0)
     def _():
@@ -683,6 +683,11 @@
         (wq_ref, wqo_ref, q_ref), (wk_ref, wko_ref, k_ref), (wv_ref, wvo_ref, v_ref)
     ):
         o_ref[...] = nn(a, merged(place_ref, w_ref, w_other)).astype(BF)
+    length = k_ref.shape[0] * BLOCK // lastk_ref.shape[0]
+    for item in range(lastk_ref.shape[0] // BLOCK):
+        last = slice((item + 1) * length - BLOCK, (item + 1) * length)
+        lastk_ref[item * BLOCK : (item + 1) * BLOCK] = k_ref[last]
+        lastv_ref[item * BLOCK : (item + 1) * BLOCK] = v_ref[last]
 
 
 def read_kernel(
@@ -788,7 +793,7 @@
     place_ref, info_ref, q_ref, k_ref, v_ref, kp_ref, vp_ref, hk_ref, hv_ref,
     wk_ref, wko_ref, wv_ref, wvo_ref, st_ref, gate_ref, u_ref, do_ref, o_ref, lse_ref,
     dq_ref, dk_ref, dv_ref, dkp_ref, dvp_ref, direct_ref, gwk_ref, gwv_ref, gb_ref, total_ref,
-    bias_ref, sum_ref, dq_acc, state_acc, *, blocks,
+    firstk_ref, firstv_ref, bias_ref, sum_ref, dq_acc, state_acc, *, blocks,
 ):
     step_at = pl.program_id(1)
     n = pl.num_programs(1) - 1 - step_at
@@ -873,6 +878,11 @@
         dkp_ref[...] = jnp.zeros_like(dkp_ref)
         dvp_ref[...] = jnp.zeros_like(dvp_ref)
 
+    @pl.when(first)
+    def _():
+        firstk_ref[...] = dkp_ref[...]
+        firstv_ref[...] = dvp_ref[...]
+
     dq_ref[...] = (dq_acc[...] * factor).astype(BF)
 
     @pl.when(n == 0)
@@ -934,6 +944,19 @@
     gsq_ref[...] += tn(ds, k) * factor
 
 
+def item_kernel(wq_ref, wk_ref, wv_ref, sq_ref, init_ref, mk_ref, mv_ref, tail_ref, out_ref):
+    at = 0
+    for w_ref in (wq_ref, wk_ref, wv_ref, sq_ref, init_ref):
+        out_ref[at : at + w_ref.shape[0]] = w_ref[...]
+        at += w_ref.shape[0]
+    for w_ref in (mk_ref, mv_ref):
+        heads, rows, lanes = w_ref.shape
+        for item in range(heads):
+            out_ref[at : at + rows, item * lanes : (item + 1) * lanes] = w_ref[item]
+        at += rows
+    out_ref[at:] = tail_ref[...]
+
+
 def pack_kernel(up_ref, down_ref, out_ref, packed_ref):
     hidden = up_ref.shape[1]
     packed_ref[:, :hidden] = up_ref[...]
@@ -946,6 +969,40 @@
     up_ref[...] = packed_ref[:, :hidden].astype(F32)
     down_ref[...] = packed_ref[:, hidden : 2 * hidden].astype(F32).T
     out_ref[...] = packed_ref[:, 2 * hidden :].astype(F32).T
+
+
+def finish_kernel(*refs):
+    place_ref, refs = refs[0], refs[1:]
+    terms, outs = refs[:-12], refs[-12:-1]
+    sum_ref = refs[-1]
+    total = terms[0][...].astype(F32)
+    for term in terms[1:]:
+        total = total + term[...].astype(F32)
+    at = 0
+    for out_ref in outs[:5]:
+        out_ref[...] = total[at : at + out_ref.shape[0]]
+        at += out_ref.shape[0]
+    for out_ref in outs[5:7]:
+        heads, rows, lanes = out_ref.shape
+        for item in range(heads):
+            out_ref[item] = total[at : at + rows, item * lanes : (item + 1) * lanes]
+        at += rows
+    sum_ref[...] = total[at:]
+    shard, group = place_ref[1], place_ref[2]
+    lanes = sum_ref.shape[1]
+    for index, out_ref in enumerate(outs[7:]):
+        heads, columns = out_ref.shape
+        if index < 3:
+            stride = HEAD_SIZE
+            row = sum_ref[pl.ds(index * len(terms) + shard, 1), :]
+            shift = group * columns
+        else:
+            stride = columns * (HEAD_SIZE // outs[7].shape[1])
+            row = sum_ref[index * len(terms) : index * len(terms) + 1, :]
+            shift = (shard * heads) * stride + group * columns
+        row = pltpu.roll(row, lax.rem(lanes - shift, lanes), 1)
+        for item in range(heads):
+            out_ref[item : item + 1, :] = row[:, item * stride : item * stride + columns]
 
 
 def out_kernel(att_ref, wo_ref, tok_ref, gain_ref, mid_ref, min_ref):
@@ -1094,7 +1151,10 @@
 def carry(value, power, axis, backward):
     count = lax.axis_size(axis)
     sign = -1 if backward else 1
-    total = from_behind(value.astype(BF), axis, sign).astype(F32)
+    total = from_behind(value.astype(BF), axis, sign)
+    if count == 2:
+        return total
+    total = total.astype(F32)
     step = 1
     while step < count - 1:
         moved = from_behind(total.astype(BF), axis, sign * step).astype(F32)
@@ -1121,7 +1181,7 @@
     return jnp.stack([jnp.where(first, own, other), jnp.where(first, other, own)], axis=dim)
 
 
-def gather_pairs(item, beside):
+def gather_pairs(item, beside, behind):
     shards = lax.axis_size("tp")
     half = shards // 2
     tp = lax.axis_index("tp")
@@ -1141,11 +1201,11 @@
     high = ordered(y_bit, high, high_y, 0)
     low_y = across(low, "dp", 2)
     high_x = across(high, "dp", 1)
+    low_y, high_x, beside, behind = lax.optimization_barrier((low_y, high_x, beside, behind))
     low = ordered(y_bit, low, low_y, 0)
     high = ordered(x_bit, high, high_x, 1)
     own = jnp.stack([low, high]).reshape((2, 4, half) + item.shape)
-    own, beside = lax.optimization_barrier((own, beside))
-    return own, across(own, "ctx", 1), beside
+    return own, across(own, "ctx", 1), beside, behind
 
 
 def scatter_pairs(own, other):
@@ -1171,10 +1231,9 @@
     low = add_low(take(low, y_bit, 1), low_moved)
     high = add_low(take(high, x_bit, 1), high_moved)
     kept = jnp.concatenate([low, high])
-    total = take(kept, tp, 0).astype(F32)
-    for k in range(1, shards):
-        total = total + across(take(kept, tp ^ k, 0), "tp", k).astype(F32)
-    return total
+    return [take(kept, tp, 0)] + [
+        across(take(kept, tp ^ k, 0), "tp", k) for k in range(1, shards)
+    ]
 
 
 def sequence_body(
@@ -1204,7 +1263,8 @@
     dp_index = lax.axis_index("dp")
     head = HEAD_SIZE
     map_rows = state_key.shape[1]
-    place = jnp.stack([ctx_index, tp_index]).astype(jnp.int32)
+    group = dp_index * lax.axis_size("ctx") + ctx_index
+    place = jnp.stack([ctx_index, tp_index, group]).astype(jnp.int32)
 
     def call(kernel, grid, in_specs, out_specs, out_shape, scratch=(), prefetch=1, **more):
         return pl.pallas_call(
@@ -1218,49 +1278,36 @@
             **more,
         )
 
-    vectors = (gain_attn, gain_mlp, gate_bias, bias_table)
-    sizes = [item.size for item in vectors]
-    tail = jnp.concatenate([item.reshape(-1) for item in vectors])
-    tail = jnp.pad(tail, (0, 16 * shard_width - tail.size)).reshape(16, shard_width)
-
-    def beside(item):
-        return jnp.moveaxis(item, 0, 1).reshape(map_rows, shard_width)
-
-    x = lax.all_to_all(tokens, "tp", 0, 0, tiled=True)
-    first_own, first_other, x = gather_pairs(
-        jnp.concatenate(
-            [
-                w_query, w_key, w_value, state_query, state_init,
-                beside(state_key), beside(state_value), tail,
-            ],
-            axis=0,
-        ),
-        x,
-    )
-    x = x.reshape(shards, rows, shard_width)
-    late_width = 2 * hidden + shard_width
-    late = pl.pallas_call(
-        pack_kernel, out_shape=jax.ShapeDtypeStruct((own_rows, late_width), BF)
-    )(w_up, w_down, w_out)
-    late, first_own = lax.optimization_barrier((late, first_own))
-    late = lax.all_gather(late, everywhere, axis=0, tiled=True)
-    late = late.reshape(shards, groups, own_rows, late_width)
-
     at_slots = 3 * own_rows
     at_init = at_slots + own_slots
     at_maps = at_init + own_slots
     at_vectors = at_maps + 2 * map_rows
     full_rows = at_vectors + 16
+    vectors = (gain_attn, gain_mlp, gate_bias, bias_table)
+    ends = np.cumsum([0] + [item.shape[1] for item in vectors])
+    tail = jnp.concatenate(vectors, axis=1)
+    tail = jnp.pad(tail, ((0, 16 - local_heads), (0, shard_width - tail.shape[1])))
+    item = pl.pallas_call(
+        item_kernel, out_shape=jax.ShapeDtypeStruct((full_rows, shard_width), BF)
+    )(w_query, w_key, w_value, state_query, state_init, state_key, state_value, tail)
+    x = lax.all_to_all(tokens, "tp", 0, 0, tiled=True)
+    late_width = 2 * hidden + shard_width
+    late = pl.pallas_call(
+        pack_kernel, out_shape=jax.ShapeDtypeStruct((own_rows, late_width), BF)
+    )(w_up, w_down, w_out)
+    first_own, first_other, x, late = gather_pairs(item, x, late)
+    x = x.reshape(shards, rows, shard_width)
+    late = lax.all_gather(late, everywhere, axis=0, tiled=True)
+    late = late.reshape(shards, groups, own_rows, late_width)
+
+    at_heads = slice(at_vectors, at_vectors + local_heads)
     small = ordered(
-        ctx_index, first_own[:, :, :, at_vectors], first_other[:, :, :, at_vectors], 2
-    )
-    small = jnp.moveaxis(small, 3, 1).reshape(shards, groups, shard_width)
-    ends = np.cumsum([0] + sizes)
+        ctx_index, first_own[:, :, :, at_heads], first_other[:, :, :, at_heads], 2
+    )
 
     def spread(index):
-        item = small[:, :, ends[index] : ends[index + 1]]
-        item = item.reshape(shards, groups, local_heads, -1)
-        return jnp.moveaxis(item, 1, 2).reshape(heads, -1).astype(F32)
+        part = small[..., ends[index] : ends[index + 1]]
+        return jnp.transpose(part, (0, 3, 4, 1, 2, 5)).reshape(heads, -1).astype(F32)
 
     gain_one = spread(0).reshape(1, width)
     gain_two = spread(1).reshape(1, width)
@@ -1288,18 +1335,18 @@
     wide = jax.ShapeDtypeStruct((rows, width), BF)
     wide32 = jax.ShapeDtypeStruct((rows, width), F32)
     split = jax.ShapeDtypeStruct((shards, rows, shard_width), BF)
-    queries, keys, values, _ = call(
+    halo = jax.ShapeDtypeStruct((seqs * BLOCK, width), BF)
+    halo_column = pl.BlockSpec((seqs * BLOCK, shard_width), lambda t, *_: (0, t))
+    queries, keys, values, _, last_keys, last_values = call(
         project_kernel,
         (shards,),
         [whole((shards, rows, shard_width)), whole((1, width))] + weight(0) + weight(1) + weight(2),
-        [column, column, column, whole((rows, width))],
-        [wide] * 4,
+        [column, column, column, whole((rows, width)), halo_column, halo_column],
+        [wide] * 4 + [halo] * 2,
     )(place, x, gain_one, *([first_own, first_other] * 3))
 
-    key_blocks = keys.reshape(seqs, blocks, BLOCK, width)
-    value_blocks = values.reshape(seqs, blocks, BLOCK, width)
-    halo_keys = from_behind(key_blocks[:, -1], "ctx", 1).reshape(seqs * BLOCK, width)
-    halo_values = from_behind(value_blocks[:, -1], "ctx", 1).reshape(seqs * BLOCK, width)
+    halo_keys = from_behind(last_keys, "ctx", 1)
+    halo_values = from_behind(last_values, "ctx", 1)
 
     def along(rows_of, index):
         return pl.BlockSpec((rows_of, head), lambda h, n, *_: (index(n), h))
@@ -1395,7 +1442,7 @@
         compiler_params=params(),
     )(attended, late, x, gain_two)
 
-    tile = 512
+    tile = min(hidden, 1024)
     per_shard = hidden // tile
     tile_block = (1, groups, own_rows, tile)
     output, middle_grad, gain_two_grad, late_grad = call(
@@ -1459,18 +1506,20 @@
     back_own = along(BLOCK, turned)
     back_slot = along(slots, turned)
     back_of_seq = along(slots, lambda n: turned(n) // blocks)
+    key_of_seq = along(BLOCK, lambda n: turned(n) // blocks)
     (
         grad_queries, dk, dv, dk_before, dv_before, direct, key_map_grad, value_map_grad,
-        bias_sum, gathered,
+        bias_sum, gathered, first_keys, first_values,
     ) = call(
         functools.partial(attend_back_kernel, blocks=blocks),
         (heads, units),
         attend_specs(turned)
         + [back_slot, channel, vector(back_span), back_own, back_own, lse_spec(turned)],
-        [back_own] * 5 + [back_slot, head_map, head_map, vector(back_span), back_of_seq],
+        [back_own] * 5 + [back_slot, head_map, head_map, vector(back_span), back_of_seq]
+        + [key_of_seq, key_of_seq],
         [
             wide, wide32, wide32, wide, wide, slot_f32, head_sum, head_sum,
-            jax.ShapeDtypeStruct((heads, 1, back_span), F32), message,
+            jax.ShapeDtypeStruct((heads, 1, back_span), F32), message, halo, halo,
         ],
         [
             pltpu.VMEM((2 * BLOCK, BLOCK), F32), pltpu.VMEM((128, back_span), F32),
@@ -1484,12 +1533,9 @@
     bias_grad = jnp.dot(bias_sum[:, 0], sum_hot, precision=exact)
 
     later = carry(gathered, power, "ctx", True)
-    first_keys = dk_before.reshape(seqs, blocks, BLOCK, width)[:, 0]
-    first_values = dv_before.reshape(seqs, blocks, BLOCK, width)[:, 0]
-    back_keys = from_behind(first_keys, "ctx", -1).reshape(seqs * BLOCK, width)
-    back_values = from_behind(first_values, "ctx", -1).reshape(seqs * BLOCK, width)
+    back_keys = from_behind(first_keys, "ctx", -1)
+    back_values = from_behind(first_values, "ctx", -1)
     following = along(BLOCK, lambda n: jnp.minimum(turned(n) + 1, units - 1))
-    key_of_seq = along(BLOCK, lambda n: turned(n) // blocks)
     kept_slot = pl.BlockSpec((slots, head), lambda h, n, *_: (0, h))
     slot_sum = jax.ShapeDtypeStruct((slots, width), F32)
     grad_keys, grad_values, slot_query_grad, init_grad, gate_grad = call(
@@ -1536,37 +1582,35 @@
     )
     grad_own = lax.dynamic_update_slice(grad_own, vector_rows, (0, 0, at_vectors, 0))
     grad_other = lax.dynamic_update_slice(grad_other, vector_rows, (0, 0, at_vectors, 0))
-    grads = scatter_pairs(grad_own, grad_other)
-    vector_grads = grads[at_vectors:].reshape(-1)
-    group = dp_index * lax.axis_size("ctx") + ctx_index
-
-    def own_part(index, like):
-        begin = sum(item.size for item in vector_sums[:index])
-        item = vector_grads[begin : begin + vector_sums[index].size].reshape(heads, -1)
-        return lax.dynamic_slice(
-            item, (tp_index * local_heads, group * like.shape[1]), like.shape
-        )
-
-    def apart(item):
-        return jnp.moveaxis(item.reshape(map_rows, local_heads, head), 1, 0)
-
+    terms = scatter_pairs(grad_own, grad_other)
+    terms, up_grad, down_grad, out_grad = lax.optimization_barrier(
+        (terms, up_grad, down_grad, out_grad)
+    )
+    parts = (
+        w_query, w_key, w_value, state_query, state_init, state_key, state_value,
+        gain_attn, gain_mlp, gate_bias, bias_table,
+    )
+    sums = call(
+        finish_kernel,
+        (1,),
+        [whole((full_rows, shard_width))] * shards,
+        [whole(item.shape) for item in parts],
+        [jax.ShapeDtypeStruct(item.shape, F32) for item in parts],
+        [pltpu.VMEM((16, shard_width), F32)],
+    )(place, *terms)
     return (
         output.reshape(seq_count, length, shard_width),
         token_grad.reshape(seq_count, length, shard_width),
-        grads[:own_rows],
-        grads[own_rows : 2 * own_rows],
-        grads[2 * own_rows : at_slots],
+        *sums[:3],
         out_grad,
         up_grad,
         down_grad,
-        grads[at_slots:at_init],
-        grads[at_init:at_maps],
-        own_part(0, gain_attn),
-        own_part(1, gain_mlp),
-        own_part(3, bias_table),
-        own_part(2, gate_bias),
-        apart(grads[at_maps : at_maps + map_rows]),
-        apart(grads[at_maps + map_rows : at_vectors]),
+        *sums[3:5],
+        sums[7],
+        sums[8],
+        sums[10],
+        sums[9],
+        *sums[5:7],
     )
 
 

time: 597 us -> 584 us (0.978)
  local copies, waits for them, and re-layouts: 42.9 us -> 22.6 us
  waiting for transfers between devices: 162 us -> 170 us
    reduce_scatter x1, waiting for transfers between devices: 0.01 us -> 26.7 us  [sequence_body(): lax.psum_scatter(late_grad.reshape(shards * groups * own_rows, late_width...]
    ppermute x16, waiting for transfers between devices: 127 us -> 111 us  [across(): lax.ppermute(value, axis, [(source, source ^ bit) for source in range(cou...]
    unnamed x65 -> x54, local copies, waits for them, and re-layouts: 14.3 us -> 9.65 us
  transfers between devices with their start and end apart: 27 -> 27, of which waited for: 17 -> 15; matrix products, arithmetic and copies ran while one was open for 10% -> 7% of each run, Pallas kernels for 34% -> 35%
where the time goes in v3:
time: 584 us; the launch traced here: 575 us
  Pallas kernels  293 us (50%)
  waiting for transfers between devices  170 us (29%)
  starting transfers between devices  45.6 us (8%)
  other arithmetic  25.6 us (4%)
  local copies, waits for them, and re-layouts  22.6 us (4%)
  between operations  14.8 us (3%)
    ppermute x16, waiting for transfers between devices, across(): lax.ppermute(value, axis, [(source, source ^ bit) for source in range(cou...  111 us
    pallas_call x1, Pallas kernels, sequence_body(): call(mlp_kernel, (shards * per_shard, 2), [whole((rows, width)), pl.Block...  68.6 us
    pallas_call x1, Pallas kernels, sequence_body(): call(functools.partial(attend_back_kernel, blocks=blocks), (heads, units)...  68.6 us
    pallas_call x1, Pallas kernels, sequence_body(): call(functools.partial(attend_kernel, blocks=blocks), (heads, units), att...  42.7 us
    pallas_call x1, Pallas kernels, sequence_body(): call(functools.partial(read_back_kernel, blocks=blocks), (heads, units),...  29.2 us
    reduce_scatter x1, waiting for transfers between devices, sequence_body(): lax.psum_scatter(late_grad.reshape(shards * groups * own_rows, late_width...  26.7 us
    pallas_call x1, Pallas kernels, sequence_body(): call(project_back_kernel, (shards,), [whole((shards, rows, shard_width)),...  25.1 us
    ppermute x16, starting transfers between devices, across(): lax.ppermute(value, axis, [(source, source ^ bit) for source in range(cou...  22.9 us
  transfers between devices with their start and end apart: 27, of which 15 were waited for; matrix products, arithmetic and copies ran while one was open for 7% of the time, Pallas kernels for 35%

profile of v3, /device:TPU:0, one launch (start us, length us, event | category | flops | bytes accessed | tf_op | source)
XLA Modules:
  0.0 575.5 jit_solution(2926146400203817028)
XLA Ops:
  10.2 5.1 collective-permute-start
  15.9 5.0 all-to-all-start
  23.4 28.8 %collective-permute-done.1 = bf16[560,256]{1,0:T(8,128)(2,1)S(1)} collective-permute-done((bf16[560,256]{1,0:T(8,128)(2,1)}, bf16[560,256]{1,0:T(8,128)(2,1)S(1)}, u32[]{:S(2)}, u32[]{:S(2)}) %collective-permute-start.1) | collective-permute-done | bytes 286752 | tf_op jit(solution)/shard_map/ppermute | solution.py:1168
  59.1 9.4 %collective-permute-done.5 = bf16[2,560,256]{2,1,0:T(8,128)(2,1)} collective-permute-done((bf16[2,560,256]{2,1,0:T(8,128)(2,1)}, bf16[2,560,256]{2,1,0:T(8,128)(2,1)}, u32[]{:S(2)}, u32[]{:S(2)}) %collective-permute-start.5) | collective-permute-done | bytes 573472 | tf_op jit(solution)/shard_map/ppermute | solution.py:1168
  79.0 16.6 %collective-permute-done.6 = bf16[2,2,560,256]{3,2,1,0:T(8,128)(2,1)} collective-permute-done((bf16[2,2,560,256]{3,2,1,0:T(8,128)(2,1)}, bf16[2,2,560,256]{3,2,1,0:T(8,128)(2,1)}, u32[]{:S(2)}, u32[]{:S(2)}) %collective-permute-start.6) | collective-permute-done | bytes 1146912 | tf_op jit(solution)/shard_map/ppermute | solution.py:1168
  95.6 4.3 collective-permute-done.4
  100.0 2.9 select_bitcast_fusion.1
  103.6 2.7 pad_maximum_fusion.wq_ref.wk_ref.wv_ref.sq_ref.init_ref
  107.1 7.5 %collective-permute-done.7.wqo_ref.wko_ref.wvo_ref.sqo_ref.inito_ref = bf16[2,4,2,560,256]{4,3,2,1,0:T(8,128)(2,1)} collective-permute-done((bf16[2,4,2,560,256]{4,3,2,1,0:T(8,128)(2,1)}, bf16[2,4,2,560,256]{4,3,2,1,0:T(8,128)(2,1)}, u32[]{:S(2)}, u32[]{:S(2)}) %collective-permute-start.7) | collective-permute-done | bytes 4587552 | tf_op jit(solution)/shard_map/ppermute | solution.py:1168
  118.0 12.4 %shard_map.317 = (bf16[1024,1024]{1,0:T(8,128)(2,1)}, bf16[1024,1024]{1,0:T(8,128)(2,1)}, bf16[1024,1024]{1,0:T(8,128)(2,1)}, bf16[1024,1024]{1,0:T(8,128)(2,1)}...) custom-call(s32[3]{0:T(128)} %pad_add_fusion.place_ref.refs_0_, bf16[4,1024,256]{2,1,0:T(8,128)(2,1)} %copy-done, ...), custom_call_target="tpu_custom_call" | custom-call | tf_op jit(solution)/shard_map/pallas_call | solution.py:1340
  130.4 18.4 %shard_map.318 = (f32[1024,1024]{1,0:T(8,128)}, bf16[512,1024]{1,0:T(8,128)(2,1)}) custom-call(s32[3]{0:T(128)} %pad_add_fusion.place_ref.refs_0_, bf16[2,4,2,560,256]{4,3,2,1,0:T(8,128)(2,1)} %pad_maximum_fusion.wq_ref.wk_ref.wv_ref.sq_ref.init_ref, bf16[2,4,2,560,256]{4,3,2,1,0:T(8,128)(2,1)} %collective-permute-done.7.wqo_ref.wko_ref.wvo_ref.sqo_ref.inito_ref, ...), custom_call_target="tpu_custom_call" | custom-call | tf_op jit(solution)/shard_map/pallas_call | solution.py:1370
  161.7 42.7 %shard_map.319 = (bf16[1024,1024]{1,0:T(8,128)(2,1)}, f32[2,8,1,512]{3,2,1,0:T(1,128)}, bf16[1024,1024]{1,0:T(8,128)(2,1)}, bf16[1024,1024]{1,0:T(8,128)(2,1)}) custom-call(s32[3]{0:T(128)} %pad_add_fusion.place_ref.refs_0_, s32[2,2]{1,0:T(2,128)} %add_bitcast_fusion.info_ref, bf16[1024,1024]{1,0:T(8,128)(2,1)} %get-tuple-element.86.q_ref, ...), custom_call_target="tpu_custom_call" | custom-call | tf_op jit(solution)/shard_map/pallas_call | solution.py:1422
  204.4 17.0 %all-gather.2.cloned.1.call-done = bf16[4096,2304]{1,0:T(8,128)(2,1)} async-done(((bf16[128,2304]{1,0:T(8,128)(2,1)}), bf16[4096,2304]{1,0:T(8,128)(2,1)}) %all-gather.2.cloned.1.call-update) | async-done | bytes 18874384 | tf_op jit(solution)/shard_map/all_gather | solution.py:1300
  221.4 10.0 %shard_map.320 = (f32[1024,1024]{1,0:T(8,128)}, bf16[1024,1024]{1,0:T(8,128)(2,1)}) custom-call(bf16[1024,1024]{1,0:T(8,128)(2,1)} %get-tuple-element.94.att_ref.o_ref, bf16[4,8,128,2304]{3,2,1,0:T(8,128)(2,1)} %bitcast.92, bf16[4,1024,256]{2,1,0:T(8,128)(2,1)} %copy-done, f32[1,1024]{1,0:T(1,128)} %reshape.198.gain_ref), custom_call_target="tpu_custom_call" | custom-call | tf_op jit(solution)/shard_map/pallas_call | solution.py:1436
  231.4 68.6 %shard_map.321 = (bf16[4,1024,256]{2,1,0:T(8,128)(2,1)}, bf16[1024,1024]{1,0:T(8,128)(2,1)}, f32[1,1024]{1,0:T(1,128)}, bf16[4,8,128,2304]{3,2,1,0:T(8,128)(2,1)}) custom-call(s32[3]{0:T(128)} %pad_add_fusion.place_ref.refs_0_, bf16[1024,1024]{1,0:T(8,128)(2,1)} %get-tuple-element.96.min_ref, bf16[4096,1024]{1,0:T(8,128)(2,1)} %bitcast.105, ...), custom_call_target="tpu_custom_call" | custom-call | tf_op jit(solution)/shard_map/pallas_call | solution.py:1448
  300.0 9.2 %shard_map.322 = (bf16[1024,1024]{1,0:T(8,128)(2,1)}, bf16[4,8,128,2304]{3,2,1,0:T(8,128)(2,1)}) custom-call(bf16[1024,1024]{1,0:T(8,128)(2,1)} %get-tuple-element.98.gmid_ref, bf16[4,8,128,2304]{3,2,1,0:T(8,128)(2,1)} %bitcast.95, bf16[1024,1024]{1,0:T(8,128)(2,1)} %get-tuple-element.94.att_ref.o_ref, ...), custom_call_target="tpu_custom_call", output_to_operand_aliasing={{1}: (3, {})} | custom-call | tf_op jit(solution)/shard_map/pallas_call | solution.py:1480
  309.2 3.8 all-to-all-start.1
  314.4 68.6 %shard_map.323 = (bf16[1024,1024]{1,0:T(8,128)(2,1)}, f32[1024,1024]{1,0:T(8,128)}, f32[1024,1024]{1,0:T(8,128)}, bf16[1024,1024]{1,0:T(8,128)(2,1)}, bf16[1024,...) custom-call(s32[3]{0:T(128)} %pad_add_fusion.place_ref.refs_0_, ...), custom_call_target="tpu_custom_call" | custom-call | tf_op jit(solution)/shard_map/pallas_call | solution.py:1513
  388.3 7.8 %collective-permute-done.11.later_ref = bf16[512,1024]{1,0:T(8,128)(2,1)S(1)} collective-permute-done((bf16[512,1024]{1,0:T(8,128)(2,1)}, bf16[512,1024]{1,0:T(8,128)(2,1)S(1)}, u32[]{:S(2)}, u32[]{:S(2)}) %collective-permute-start.11) | collective-permute-done | bytes 1048608 | tf_op jit(solution)/shard_map/ppermute | solution.py:24
  399.9 29.2 %shard_map.324 = (bf16[1024,1024]{1,0:T(8,128)(2,1)}, bf16[1024,1024]{1,0:T(8,128)(2,1)}, f32[512,1024]{1,0:T(8,128)}, f32[512,1024]{1,0:T(8,128)}, f32[8,1,128]{2,1,0:T(1,128)}) custom-call(s32[3]{0:T(128)} %pad_add_fusion.place_ref.refs_0_, bf16[2,4,2,560,256]{4,3,2,1,0:T(8,128)(2,1)} %pad_maximum_fusion.wq_ref.wk_ref.wv_ref.sq_ref.init_ref, ...), custom_call_target="tpu_custom_call" | custom-call | tf_op jit(solution)/shard_map/pallas_call | solution.py:1541
  429.1 25.1 %shard_map.325 = (bf16[4,1024,256]{2,1,0:T(8,128)(2,1)}, f32[1,1024]{1,0:T(1,128)}, bf16[4,4,560,256]{3,2,1,0:T(8,128)(2,1)}, bf16[4,4,560,256]{3,2,1,0:T(8,128)(2,1)}) custom-call(s32[3]{0:T(128)} %pad_add_fusion.place_ref.refs_0_, bf16[4,1024,256]{2,1,0:T(8,128)(2,1)} %copy-done, bf16[1024,1024]{1,0:T(8,128)(2,1)} %get-tuple-element.98.gmid_ref, ...), custom_call_target="tpu_custom_call" | custom-call | tf_op jit(solution)/shard_map/pallas_call | solution.py:1559
  456.6 5.0 all-to-all-start.2
  461.6 2.7 fusion.42
  464.7 2.6 fusion.43
  470.2 24.9 %collective-permute-done.17 = bf16[2,2,560,256]{3,2,0,1:T(8,128)(2,1)S(1)} collective-permute-done((bf16[2,2,560,256]{3,2,0,1:T(8,128)(2,1)S(1)}, bf16[2,2,560,256]{3,2,0,1:T(8,128)(2,1)S(1)}, u32[]{:S(2)}, u32[]{:S(2)}) %collective-permute-start.17) | collective-permute-done | bytes 1146912 | tf_op jit(solution)/shard_map/ppermute | solution.py:1168
  500.4 10.5 %collective-permute-done.18 = bf16[2,560,256]{2,1,0:T(8,128)(2,1)} collective-permute-done((bf16[2,560,256]{2,1,0:T(8,128)(2,1)}, bf16[2,560,256]{2,1,0:T(8,128)(2,1)}, u32[]{:S(2)}, u32[]{:S(2)}) %collective-permute-start.18) | collective-permute-done | bytes 573472 | tf_op jit(solution)/shard_map/ppermute | solution.py:1168
  512.1 6.5 %collective-permute-done.16 = bf16[2,560,256]{2,1,0:T(8,128)(2,1)} collective-permute-done((bf16[2,560,256]{2,1,0:T(8,128)(2,1)}, bf16[2,560,256]{2,1,0:T(8,128)(2,1)}, u32[]{:S(2)}, u32[]{:S(2)}) %collective-permute-start.16) | collective-permute-done | bytes 573472 | tf_op jit(solution)/shard_map/ppermute | solution.py:1168
  522.8 4.8 collective-permute-start.20
  527.6 3.8 all-to-all-done.2
  531.4 26.7 %reduce-scatter.2.cloned.1.call-done.packed_ref = bf16[128,2304]{1,0:T(8,128)(2,1)} async-done(((bf16[4096,2304]{1,0:T(8,128)(2,1)}), bf16[128,2304]{1,0:T(8,128)(2,1)}) %reduce-scatter.2.cloned.1.call-update) | async-done | bytes 589840 | tf_op jit(solution)/shard_map/reduce_scatter | solution.py:1492
  561.2 2.8 shard_map.327
  565.4 3.0 copy.84
  (149 shorter events, 72.4 us)
Async XLA Ops:
  10.2 42.7 %copy-start.12 = (bf16[560,256]{1,0:T(8,128)(2,1)S(1)}, bf16[560,256]{1,0:T(8,128)(2,1)}, u32[]{:S(2)}) copy-start(bf16[560,256]{1,0:T(8,128)(2,1)} %shard_map.315) | copy-start | bytes 860164
  10.2 13.2 %collective-permute-start = (bf16[560,256]{1,0:T(8,128)(2,1)}, bf16[560,256]{1,0:T(8,128)(2,1)S(1)}, u32[]{:S(2)}, u32[]{:S(2)}) collective-permute-start(bf16[560,256]{1,0:T(8,128)(2,1)} %shard_map.315), channel_id=1, source_target_pairs={{0,3},{1,2},{2,1},{3,0},{4,7},{5,6},{6,5},{7,4},{8,11},{9,10},{10,... | collective-permute-start | bytes 860168 | tf_op jit(solution)/shard_map/ppermute | solution.py:1168
  15.3 36.9 %collective-permute-start.1 = (bf16[560,256]{1,0:T(8,128)(2,1)}, bf16[560,256]{1,0:T(8,128)(2,1)S(1)}, u32[]{:S(2)}, u32[]{:S(2)}) collective-permute-start(bf16[560,256]{1,0:T(8,128)(2,1)} %shard_map.315), channel_id=1, source_target_pairs={{0,2},{1,3},{2,0},{3,1},{4,6},{5,7},{6,4},{7,5},{8,10},{9,11},{10,... | collective-permute-start | bytes 860168 | tf_op jit(solution)/shard_map/ppermute | solution.py:1168
  15.3 37.6 %collective-permute-start.2 = (bf16[560,256]{1,0:T(8,128)(2,1)}, bf16[560,256]{1,0:T(8,128)(2,1)}, u32[]{:S(2)}, u32[]{:S(2)}) collective-permute-start(bf16[560,256]{1,0:T(8,128)(2,1)} %shard_map.315), channel_id=1, source_target_pairs={{0,1},{1,0},{2,3},{3,2},{4,5},{5,4},{6,7},{7,6},{8,9},{9,8},{10,11... | collective-permute-start | bytes 860168 | tf_op jit(solution)/shard_map/ppermute | solution.py:1168
  15.9 84.0 %all-to-all-start = ((bf16[4,1024,256]{2,1,0:T(8,128)(2,1)}), bf16[4,1024,256]{2,1,0:T(8,128)(2,1)S(1)}, u32[]{:S(2)}, u32[]{:S(2)}) async-start(bf16[4,1024,256]{2,1,0:T(8,128)(2,1)} %param.20), calls=%async_computation | async-start | bytes 4194304 | tf_op jit(solution)/shard_map/all_to_all | solution.py:1293
  21.0 200.4 %all-gather.2.cloned.1.call-start = ((), (), s32[]{:S(2)}) async-start(), calls=%async_computation.4 | async-start | bytes 19464192 | tf_op jit(solution)/shard_map/all_gather | solution.py:1300
  23.4 28.8 %copy-start.20 = (bf16[560,256]{1,0:T(8,128)(2,1)}, bf16[560,256]{1,0:T(8,128)(2,1)S(1)}, u32[]{:S(2)}) copy-start(bf16[560,256]{1,0:T(8,128)(2,1)S(1)} %collective-permute-done) | copy-start | bytes 860164
  55.2 13.3 %collective-permute-start.5 = (bf16[2,560,256]{2,1,0:T(8,128)(2,1)}, bf16[2,560,256]{2,1,0:T(8,128)(2,1)}, u32[]{:S(2)}, u32[]{:S(2)}) collective-permute-start(bf16[2,560,256]{2,1,0:T(8,128)(2,1)} %pad_maximum_fusion.6), channel_id=1, source_target_pairs={{0,16},{8,24},{16,0},{24,8},{1,17},{9,25},{17,1},{25,9},{2,18},{10... | collective-permute-start | bytes 1720328 | tf_op jit(solution)/shard_map/ppermute | solution.py:1168
  57.6 14.8 %collective-permute-start.3 = (bf16[2,560,256]{2,1,0:T(8,128)(2,1)}, bf16[2,560,256]{2,1,0:T(8,128)(2,1)}, u32[]{:S(2)}, u32[]{:S(2)}) collective-permute-start(bf16[2,560,256]{2,1,0:T(8,128)(2,1)} %pad_maximum_fusion.5), channel_id=1, source_target_pairs={{0,8},{8,0},{16,24},{24,16},{1,9},{9,1},{17,25},{25,17},{2,10},{10... | collective-permute-start | bytes 1720328 | tf_op jit(solution)/shard_map/ppermute | solution.py:1168
  70.9 24.7 %collective-permute-start.6 = (bf16[2,2,560,256]{3,2,1,0:T(8,128)(2,1)}, bf16[2,2,560,256]{3,2,1,0:T(8,128)(2,1)}, u32[]{:S(2)}, u32[]{:S(2)}) collective-permute-start(bf16[2,2,560,256]{3,2,1,0:T(8,128)(2,1)} %pad_maximum_fusion.4), channel_id=1, source_target_pairs={{0,8},{8,0},{16,24},{24,16},{1,9},{9,1},{17,25},{25,17},{2,10},{10... | collective-permute-start | bytes 3440648 | tf_op jit(solution)/shard_map/ppermute | solution.py:1168
  75.5 24.4 %collective-permute-start.4 = (bf16[2,2,560,256]{3,2,1,0:T(8,128)(2,1)}, bf16[2,2,560,256]{3,2,1,0:T(8,128)(2,1)}, u32[]{:S(2)}, u32[]{:S(2)}) collective-permute-start(bf16[2,2,560,256]{3,2,1,0:T(8,128)(2,1)} %pad_maximum_fusion.3), channel_id=1, source_target_pairs={{0,16},{8,24},{16,0},{24,8},{1,17},{9,25},{17,1},{25,9},{2,18},{10... | collective-permute-start | bytes 3440648 | tf_op jit(solution)/shard_map/ppermute | solution.py:1168
  100.0 458.1 %reduce-scatter.2.cloned.1.call-start = ((), (), s32[]{:S(2)}) async-start(), calls=%async_computation.5 | async-start | bytes 19464192 | tf_op jit(solution)/shard_map/reduce_scatter | solution.py:1492
  106.5 8.1 %collective-permute-start.7 = (bf16[2,4,2,560,256]{4,3,2,1,0:T(8,128)(2,1)}, bf16[2,4,2,560,256]{4,3,2,1,0:T(8,128)(2,1)}, u32[]{:S(2)}, u32[]{:S(2)}) collective-permute-start(bf16[2,4,2,560,256]{4,3,2,1,0:T(8,128)(2,1)} %pad_maximum_fusion.wq_ref.wk_ref.wv_ref.sq_ref.init_ref), channel_id=1, source_target_pairs={{0,4},{4,0},{1,5},{5,1},{2,6},{6,2},{3,7},{7,3},{8,12},{12,8},{9,1... | collective-permute-start | bytes 13762568 | tf_op jit(solution)/shard_map/ppermute | solution.py:1168
  130.4 29.1 %copy-start.22 = (f32[1,1024]{1,0:T(1,128)S(1)}, f32[1,1024]{1,0:T(1,128)}, u32[]{:S(2)}) copy-start(f32[1,1024]{1,0:T(1,128)} %reshape.197.gate_ref) | copy-start | bytes 12292
  148.8 11.3 %collective-permute-start.10 = (bf16[512,1024]{1,0:T(8,128)(2,1)}, bf16[512,1024]{1,0:T(8,128)(2,1)S(1)}, u32[]{:S(2)}, u32[]{:S(2)}) collective-permute-start(bf16[512,1024]{1,0:T(8,128)(2,1)} %get-tuple-element.92), channel_id=1, source_target_pairs={{0,4},{1,5},{2,6},{3,7},{8,12},{9,13},{10,14},{11,15},{16,20},{17,... | collective-permute-start | bytes 3145736 | tf_op jit(solution)/shard_map/ppermute | solution.py:24
  150.8 9.3 %collective-permute-start.8 = (bf16[512,1024]{1,0:T(8,128)(2,1)}, bf16[512,1024]{1,0:T(8,128)(2,1)S(1)}, u32[]{:S(2)}, u32[]{:S(2)}) collective-permute-start(bf16[512,1024]{1,0:T(8,128)(2,1)} %get-tuple-element.89), channel_id=1, source_target_pairs={{0,4},{1,5},{2,6},{3,7},{8,12},{9,13},{10,14},{11,15},{16,20},{17,... | collective-permute-start | bytes 3145736 | tf_op jit(solution)/shard_map/ppermute | solution.py:24
  152.2 7.9 %collective-permute-start.9 = (bf16[512,1024]{1,0:T(8,128)(2,1)}, bf16[512,1024]{1,0:T(8,128)(2,1)S(1)}, u32[]{:S(2)}, u32[]{:S(2)}) collective-permute-start(bf16[512,1024]{1,0:T(8,128)(2,1)} %get-tuple-element.90), channel_id=1, source_target_pairs={{0,4},{1,5},{2,6},{3,7},{8,12},{9,13},{10,14},{11,15},{16,20},{17,... | collective-permute-start | bytes 3145736 | tf_op jit(solution)/shard_map/ppermute | solution.py:24
  309.2 79.1 %all-to-all-start.1 = ((bf16[4,1024,256]{2,1,0:T(8,128)(2,1)}), bf16[4,1024,256]{2,1,0:T(8,128)(2,1)S(1)}, u32[]{:S(2)}, u32[]{:S(2)}) async-start(bf16[4,1024,256]{2,1,0:T(8,128)(2,1)} %get-tuple-element.103), calls=%async_computation.1 | async-start | bytes 4194304 | tf_op jit(solution)/shard_map/all_to_all | solution.py:1478
  314.4 72.5 %copy-start.15 = (f32[1536,32]{1,0:T(8,128)S(1)}, f32[1536,32]{1,0:T(8,128)}, u32[]{:S(2)}) copy-start(f32[1536,32]{1,0:T(8,128)} %constant.109.clone) | copy-start | bytes 589828
  314.4 73.9 %copy-start.23 = (f32[1,1024]{1,0:T(1,128)S(1)}, f32[1,1024]{1,0:T(1,128)}, u32[]{:S(2)}) copy-start(f32[1,1024]{1,0:T(1,128)} %get-tuple-element.124) | copy-start | bytes 12292
  383.0 13.1 %collective-permute-start.11 = (bf16[512,1024]{1,0:T(8,128)(2,1)}, bf16[512,1024]{1,0:T(8,128)(2,1)S(1)}, u32[]{:S(2)}, u32[]{:S(2)}) collective-permute-start(bf16[512,1024]{1,0:T(8,128)(2,1)} %get-tuple-element.108), channel_id=1, source_target_pairs={{4,0},{5,1},{6,2},{7,3},{12,8},{13,9},{14,10},{15,11},{20,16},{21,... | collective-permute-start | bytes 3145736 | tf_op jit(solution)/shard_map/ppermute | solution.py:24
  384.3 13.4 %collective-permute-start.12 = (bf16[512,1024]{1,0:T(8,128)(2,1)}, bf16[512,1024]{1,0:T(8,128)(2,1)}, u32[]{:S(2)}, u32[]{:S(2)}) collective-permute-start(bf16[512,1024]{1,0:T(8,128)(2,1)} %get-tuple-element.113), channel_id=1, source_target_pairs={{4,0},{5,1},{6,2},{7,3},{12,8},{13,9},{14,10},{15,11},{20,16},{21,... | collective-permute-start | bytes 3145736 | tf_op jit(solution)/shard_map/ppermute | solution.py:24
  385.6 14.3 %collective-permute-start.13 = (bf16[512,1024]{1,0:T(8,128)(2,1)}, bf16[512,1024]{1,0:T(8,128)(2,1)}, u32[]{:S(2)}, u32[]{:S(2)}) collective-permute-start(bf16[512,1024]{1,0:T(8,128)(2,1)} %get-tuple-element.114), channel_id=1, source_target_pairs={{4,0},{5,1},{6,2},{7,3},{12,8},{13,9},{14,10},{15,11},{20,16},{21,... | collective-permute-start | bytes 3145736 | tf_op jit(solution)/shard_map/ppermute | solution.py:24
  455.7 9.0 %collective-permute-start.14 = (bf16[4,4,560,256]{3,2,1,0:T(8,128)(2,1)}, bf16[4,4,560,256]{3,2,1,0:T(8,128)(2,1)}, u32[]{:S(2)}, u32[]{:S(2)}) collective-permute-start(bf16[4,4,560,256]{3,2,1,0:T(8,128)(2,1)} %get-tuple-element.183), channel_id=1, source_target_pairs={{0,4},{4,0},{1,5},{5,1},{2,6},{6,2},{3,7},{7,3},{8,12},{12,8},{9,1... | collective-permute-start | bytes 13762568 | tf_op jit(solution)/shard_map/ppermute | solution.py:1168
  456.6 74.8 %all-to-all-start.2 = ((bf16[4,1024,256]{2,1,0:T(8,128)(2,1)}), bf16[4,1024,256]{2,1,0:T(8,128)(2,1)}, u32[]{:S(2)}, u32[]{:S(2)}) async-start(bf16[4,1024,256]{2,1,0:T(8,128)(2,1)} %get-tuple-element.121), calls=%async_computation.2 | async-start | bytes 4194304 | tf_op jit(solution)/shard_map/all_to_all | solution.py:1575
  467.8 27.3 %collective-permute-start.17 = (bf16[2,2,560,256]{3,2,0,1:T(8,128)(2,1)S(1)}, bf16[2,2,560,256]{3,2,0,1:T(8,128)(2,1)S(1)}, u32[]{:S(2)}, u32[]{:S(2)}) collective-permute-start(bf16[2,2,560,256]{3,2,0,1:T(8,128)(2,1)S(1)} %fusion.5), channel_id=1, source_target_pairs={{0,16},{8,24},{16,0},{24,8},{1,17},{9,25},{17,1},{25,9},{2,18},{10... | collective-permute-start | bytes 3440648 | tf_op jit(solution)/shard_map/ppermute | solution.py:1168
  469.7 28.1 %collective-permute-start.15 = (bf16[2,2,560,256]{3,2,0,1:T(8,128)(2,1)S(1)}, bf16[2,2,560,256]{3,2,0,1:T(8,128)(2,1)S(1)}, u32[]{:S(2)}, u32[]{:S(2)}) collective-permute-start(bf16[2,2,560,256]{3,2,0,1:T(8,128)(2,1)S(1)} %fusion.3), channel_id=1, source_target_pairs={{0,8},{8,0},{16,24},{24,16},{1,9},{9,1},{17,25},{25,17},{2,10},{10... | collective-permute-start | bytes 3440648 | tf_op jit(solution)/shard_map/ppermute | solution.py:1168
  496.4 14.5 %collective-permute-start.18 = (bf16[2,560,256]{2,1,0:T(8,128)(2,1)}, bf16[2,560,256]{2,1,0:T(8,128)(2,1)}, u32[]{:S(2)}, u32[]{:S(2)}) collective-permute-start(bf16[2,560,256]{2,1,0:T(8,128)(2,1)} %dynamic-slice_bitcast_fusion), channel_id=1, source_target_pairs={{0,8},{8,0},{16,24},{24,16},{1,9},{9,1},{17,25},{25,17},{2,10},{10... | collective-permute-start | bytes 1720328 | tf_op jit(solution)/shard_map/ppermute | solution.py:1168
  500.1 18.5 %collective-permute-start.16 = (bf16[2,560,256]{2,1,0:T(8,128)(2,1)}, bf16[2,560,256]{2,1,0:T(8,128)(2,1)}, u32[]{:S(2)}, u32[]{:S(2)}) collective-permute-start(bf16[2,560,256]{2,1,0:T(8,128)(2,1)} %dynamic-slice_bitcast_fusion.1), channel_id=1, source_target_pairs={{0,16},{8,24},{16,0},{24,8},{1,17},{9,25},{17,1},{25,9},{2,18},{10... | collective-permute-start | bytes 1720328 | tf_op jit(solution)/shard_map/ppermute | solution.py:1168
  521.1 39.2 %collective-permute-start.19 = (bf16[560,256]{1,0:T(8,128)(2,1)}, bf16[560,256]{1,0:T(8,128)(2,1)S(1)}, u32[]{:S(2)}, u32[]{:S(2)}) collective-permute-start(bf16[560,256]{1,0:T(8,128)(2,1)} %get-tuple-element.170), channel_id=1, source_target_pairs={{0,1},{1,0},{2,3},{3,2},{4,5},{5,4},{6,7},{7,6},{8,9},{9,8},{10,11... | collective-permute-start | bytes 860168 | tf_op jit(solution)/shard_map/ppermute | solution.py:1168
  522.8 37.5 %collective-permute-start.20 = (bf16[560,256]{1,0:T(8,128)(2,1)S(1)}, bf16[560,256]{1,0:T(8,128)(2,1)S(1)}, u32[]{:S(2)}, u32[]{:S(2)}) collective-permute-start(bf16[560,256]{1,0:T(8,128)(2,1)S(1)} %get-tuple-element.171), channel_id=1, source_target_pairs={{0,2},{1,3},{2,0},{3,1},{4,6},{5,7},{6,4},{7,5},{8,10},{9,11},{10,... | collective-permute-start | bytes 860168 | tf_op jit(solution)/shard_map/ppermute | solution.py:1168
  527.6 32.7 %collective-permute-start.21 = (bf16[560,256]{1,0:T(8,128)(2,1)S(1)}, bf16[560,256]{1,0:T(8,128)(2,1)S(1)}, u32[]{:S(2)}, u32[]{:S(2)}) collective-permute-start(bf16[560,256]{1,0:T(8,128)(2,1)S(1)} %get-tuple-element.168), channel_id=1, source_target_pairs={{0,3},{1,2},{2,1},{3,0},{4,7},{5,6},{6,5},{7,4},{8,11},{9,10},{10,... | collective-permute-start | bytes 860168 | tf_op jit(solution)/shard_map/ppermute | solution.py:1168
  (21 other events, 110.4 us)
Sparse Core Ops, SparseCore 0:
  100.1 121.2 all-gather.1
  309.3 248.7 reduce-scatter.1

commit v4 on v3

--- a/solution.py
+++ b/solution.py
@@ -671,7 +671,7 @@
 
 def project_kernel(
     place_ref, tok_ref, gain_ref, wq_ref, wqo_ref, wk_ref, wko_ref, wv_ref, wvo_ref,
-    q_ref, k_ref, v_ref, ain_ref, lastk_ref, lastv_ref,
+    q_ref, k_ref, v_ref, ain_ref, last_ref,
 ):
     @pl.when(pl.program_id(0) == 0)
     def _():
@@ -683,11 +683,11 @@
         (wq_ref, wqo_ref, q_ref), (wk_ref, wko_ref, k_ref), (wv_ref, wvo_ref, v_ref)
     ):
         o_ref[...] = nn(a, merged(place_ref, w_ref, w_other)).astype(BF)
-    length = k_ref.shape[0] * BLOCK // lastk_ref.shape[0]
-    for item in range(lastk_ref.shape[0] // BLOCK):
+    length = k_ref.shape[0] * BLOCK // last_ref.shape[1]
+    for item in range(last_ref.shape[1] // BLOCK):
         last = slice((item + 1) * length - BLOCK, (item + 1) * length)
-        lastk_ref[item * BLOCK : (item + 1) * BLOCK] = k_ref[last]
-        lastv_ref[item * BLOCK : (item + 1) * BLOCK] = v_ref[last]
+        last_ref[0, item * BLOCK : (item + 1) * BLOCK] = k_ref[last]
+        last_ref[1, item * BLOCK : (item + 1) * BLOCK] = v_ref[last]
 
 
 def read_kernel(
@@ -957,6 +957,17 @@
     out_ref[at:] = tail_ref[...]
 
 
+def assemble_kernel(place_ref, low_ref, lowy_ref, high_ref, highx_ref, own_ref):
+    x_bit = place_ref[3]
+    y_bit = place_ref[4]
+    for x in range(2):
+        own_ref[0, 2 * y_bit + x] = low_ref[x]
+        own_ref[0, 2 * (1 - y_bit) + x] = lowy_ref[x]
+    for y in range(2):
+        own_ref[1, 2 * y + x_bit] = high_ref[y]
+        own_ref[1, 2 * y + 1 - x_bit] = highx_ref[y]
+
+
 def pack_kernel(up_ref, down_ref, out_ref, packed_ref):
     hidden = up_ref.shape[1]
     packed_ref[:, :hidden] = up_ref[...]
@@ -973,7 +984,9 @@
 
 def finish_kernel(*refs):
     place_ref, refs = refs[0], refs[1:]
-    terms, outs = refs[:-12], refs[-12:-1]
+    for from_ref, to_ref in zip(refs[:2], refs[-3:-1]):
+        to_ref[...] = from_ref[...]
+    terms, outs = refs[2:-14], refs[-14:-3]
     sum_ref = refs[-1]
     total = terms[0][...].astype(F32)
     for term in terms[1:]:
@@ -1181,7 +1194,7 @@
     return jnp.stack([jnp.where(first, own, other), jnp.where(first, other, own)], axis=dim)
 
 
-def gather_pairs(item, beside, behind):
+def gather_pairs(item, beside, behind, place):
     shards = lax.axis_size("tp")
     half = shards // 2
     tp = lax.axis_index("tp")
@@ -1195,16 +1208,24 @@
         bit *= 2
     low = jnp.stack(parts[:half])
     high = jnp.stack(parts[half:])
+    low, high, behind = lax.optimization_barrier((low, high, behind))
     low_x = across(low, "dp", 1)
     high_y = across(high, "dp", 2)
     low = ordered(x_bit, low, low_x, 0)
     high = ordered(y_bit, high, high_y, 0)
     low_y = across(low, "dp", 2)
     high_x = across(high, "dp", 1)
-    low_y, high_x, beside, behind = lax.optimization_barrier((low_y, high_x, beside, behind))
-    low = ordered(y_bit, low, low_y, 0)
-    high = ordered(x_bit, high, high_x, 1)
-    own = jnp.stack([low, high]).reshape((2, 4, half) + item.shape)
+    piece = pl.BlockSpec((2, 1) + item.shape, lambda i, *_: (0, i, 0, 0))
+    own = pl.pallas_call(
+        assemble_kernel,
+        grid_spec=pltpu.PrefetchScalarGridSpec(
+            num_scalar_prefetch=1, grid=(half,), in_specs=[piece] * 4,
+            out_specs=pl.BlockSpec((2, 4, 1) + item.shape, lambda i, *_: (0, 0, i, 0, 0)),
+        ),
+        out_shape=jax.ShapeDtypeStruct((2, 4, half) + item.shape, BF),
+        compiler_params=params(),
+    )(place, low, low_y, high, high_x)
+    own, beside = lax.optimization_barrier((own, beside))
     return own, across(own, "ctx", 1), beside, behind
 
 
@@ -1264,7 +1285,7 @@
     head = HEAD_SIZE
     map_rows = state_key.shape[1]
     group = dp_index * lax.axis_size("ctx") + ctx_index
-    place = jnp.stack([ctx_index, tp_index, group]).astype(jnp.int32)
+    place = jnp.stack([ctx_index, tp_index, group, dp_index % 2, dp_index // 2]).astype(jnp.int32)
 
     def call(kernel, grid, in_specs, out_specs, out_shape, scratch=(), prefetch=1, **more):
         return pl.pallas_call(
@@ -1295,7 +1316,7 @@
     late = pl.pallas_call(
         pack_kernel, out_shape=jax.ShapeDtypeStruct((own_rows, late_width), BF)
     )(w_up, w_down, w_out)
-    first_own, first_other, x, late = gather_pairs(item, x, late)
+    first_own, first_other, x, late = gather_pairs(item, x, late, place)
     x = x.reshape(shards, rows, shard_width)
     late = lax.all_gather(late, everywhere, axis=0, tiled=True)
     late = late.reshape(shards, groups, own_rows, late_width)
@@ -1336,17 +1357,16 @@
     wide32 = jax.ShapeDtypeStruct((rows, width), F32)
     split = jax.ShapeDtypeStruct((shards, rows, shard_width), BF)
     halo = jax.ShapeDtypeStruct((seqs * BLOCK, width), BF)
-    halo_column = pl.BlockSpec((seqs * BLOCK, shard_width), lambda t, *_: (0, t))
-    queries, keys, values, _, last_keys, last_values = call(
+    halo_column = pl.BlockSpec((2, seqs * BLOCK, shard_width), lambda t, *_: (0, 0, t))
+    queries, keys, values, _, last_blocks = call(
         project_kernel,
         (shards,),
         [whole((shards, rows, shard_width)), whole((1, width))] + weight(0) + weight(1) + weight(2),
-        [column, column, column, whole((rows, width)), halo_column, halo_column],
-        [wide] * 4 + [halo] * 2,
+        [column, column, column, whole((rows, width)), halo_column],
+        [wide] * 4 + [jax.ShapeDtypeStruct((2, seqs * BLOCK, width), BF)],
     )(place, x, gain_one, *([first_own, first_other] * 3))
 
-    halo_keys = from_behind(last_keys, "ctx", 1)
-    halo_values = from_behind(last_values, "ctx", 1)
+    halos = from_behind(last_blocks, "ctx", 1)
 
     def along(rows_of, index):
         return pl.BlockSpec((rows_of, head), lambda h, n, *_: (index(n), h))
@@ -1375,6 +1395,7 @@
         [slot_f32, message],
         [slot_scratch],
     )(place, first_own, first_other, keys, values, gate)
+    halos, accumulated = lax.optimization_barrier((halos, accumulated))
     power = gate**blocks
     lead = carry(accumulated, power, "ctx", False)
     lead_power = jnp.ones_like(gate)
@@ -1405,9 +1426,12 @@
 
     def attend_specs(index):
         before = along(BLOCK, lambda n: jnp.maximum(index(n) - 1, 0))
-        by_seq = along(BLOCK, lambda n: index(n) // blocks)
+        by_seq = [
+            pl.BlockSpec((None, BLOCK, head), lambda h, n, *_, part=part: (part, index(n) // blocks, h))
+            for part in range(2)
+        ]
         here = along(BLOCK, index)
-        return [here, here, here, before, before, by_seq, by_seq] + key_maps + value_maps
+        return [here, here, here, before, before] + by_seq + key_maps + value_maps
 
     def lse_spec(index):
         return pl.BlockSpec((1, 1, 1, BLOCK), lambda h, n, *_: (index(n), h, 0, 0))
@@ -1416,7 +1440,7 @@
         return pl.BlockSpec((1, 1, size), lambda h, *_: (h, 0, 0))
 
     attend_args = (
-        place, info, queries, keys, values, keys, values, halo_keys, halo_values,
+        place, info, queries, keys, values, keys, values, halos, halos,
         first_own, first_other, first_own, first_other,
     )
     attended, lse, states, moved = call(
@@ -1493,14 +1517,6 @@
         late_grad.reshape(shards * groups * own_rows, late_width), everywhere,
         scatter_dimension=0, tiled=True,
     )
-    up_grad, down_grad, out_grad = pl.pallas_call(
-        unpack_kernel,
-        out_shape=[
-            jax.ShapeDtypeStruct(w_up.shape, F32), jax.ShapeDtypeStruct(w_down.shape, F32),
-            jax.ShapeDtypeStruct(w_out.shape, F32),
-        ],
-    )(late_grad)
-
     head_sum = jax.ShapeDtypeStruct((heads, head, head), F32)
     head_map = pl.BlockSpec((1, head, head), lambda h, n, *_: (h, 0, 0))
     back_own = along(BLOCK, turned)
@@ -1583,9 +1599,6 @@
     grad_own = lax.dynamic_update_slice(grad_own, vector_rows, (0, 0, at_vectors, 0))
     grad_other = lax.dynamic_update_slice(grad_other, vector_rows, (0, 0, at_vectors, 0))
     terms = scatter_pairs(grad_own, grad_other)
-    terms, up_grad, down_grad, out_grad = lax.optimization_barrier(
-        (terms, up_grad, down_grad, out_grad)
-    )
     parts = (
         w_query, w_key, w_value, state_query, state_init, state_key, state_value,
         gain_attn, gain_mlp, gate_bias, bias_table,
@@ -1593,14 +1606,23 @@
     sums = call(
         finish_kernel,
         (1,),
-        [whole((full_rows, shard_width))] * shards,
-        [whole(item.shape) for item in parts],
-        [jax.ShapeDtypeStruct(item.shape, F32) for item in parts],
+        [whole(output.shape)] * 2 + [whole((full_rows, shard_width))] * shards,
+        [whole(item.shape) for item in parts] + [whole(output.shape)] * 2,
+        [jax.ShapeDtypeStruct(item.shape, F32) for item in parts]
+        + [jax.ShapeDtypeStruct(output.shape, BF)] * 2,
         [pltpu.VMEM((16, shard_width), F32)],
-    )(place, *terms)
+    )(place, output, token_grad, *terms)
+    late_grad, sums = lax.optimization_barrier((late_grad, sums))
+    up_grad, down_grad, out_grad = pl.pallas_call(
+        unpack_kernel,
+        out_shape=[
+            jax.ShapeDtypeStruct(w_up.shape, F32), jax.ShapeDtypeStruct(w_down.shape, F32),
+            jax.ShapeDtypeStruct(w_out.shape, F32),
+        ],
+    )(late_grad)
     return (
-        output.reshape(seq_count, length, shard_width),
-        token_grad.reshape(seq_count, length, shard_width),
+        sums[11].reshape(seq_count, length, shard_width),
+        sums[12].reshape(seq_count, length, shard_width),
         *sums[:3],
         out_grad,
         up_grad,

time: 584 us -> 575 us (0.985)
  other arithmetic: 25.6 us -> 14.9 us
  local copies, waits for them, and re-layouts: 22.6 us -> 16.3 us
  Pallas kernels: 293 us -> 299 us
    reduce_scatter x1, waiting for transfers between devices: 26.7 us -> 0.02 us  [sequence_body(): lax.psum_scatter(late_grad.reshape(shards * groups * own_rows, late_width...]
    ppermute x16, waiting for transfers between devices: 111 us -> 137 us  [across(): lax.ppermute(value, axis, [(source, source ^ bit) for source in range(cou...]
    all_gather x1, waiting for transfers between devices: 17 us -> 0.02 us  [sequence_body(): late = lax.all_gather(late, everywhere, axis=0, tiled=True)]
    all_to_all x1, waiting for transfers between devices: 0.01 us -> 14.7 us  [sequence_body(): x = lax.all_to_all(tokens, 'tp', 0, 0, tiled=True)]
    pallas_call x1 -> x2, Pallas kernels: 2.8 us -> 9.99 us  [the longest x1 5.49 us: sequence_body(): call(finish_kernel, (1,), [whole(output.shape)] * 2 + [whole((full_rows,...]
    unnamed x54 -> x36, local copies, waits for them, and re-layouts: 9.65 us -> 2.87 us
    another operation x9 -> x5, other arithmetic: 9.79 us -> 3.52 us  [ordered(): jnp.stack([jnp.where(first, own, other), jnp.where(first, other, own)], a...]
    ppermute x6 -> x5, waiting for transfers between devices: 11.5 us -> 12.6 us  [from_behind(): lax.ppermute(value, axis, [(source, source + steps) for source in range(f...]
  transfers between devices with their start and end apart: 27 -> 26, of which waited for: 15 -> 16; matrix products, arithmetic and copies ran while one was open for 7% -> 5% of each run, Pallas kernels for 35% -> 37%
where the time goes in v4:
time: 575 us; the launch traced here: 565 us
  Pallas kernels  299 us (52%)
  waiting for transfers between devices  170 us (30%)
  starting transfers between devices  45 us (8%)
  local copies, waits for them, and re-layouts  16.3 us (3%)
  other arithmetic  14.9 us (3%)
  between operations  14.7 us (3%)
    ppermute x16, waiting for transfers between devices, across(): lax.ppermute(value, axis, [(source, source ^ bit) for source in range(cou...  137 us
    pallas_call x1, Pallas kernels, sequence_body(): call(mlp_kernel, (shards * per_shard, 2), [whole((rows, width)), pl.Block...  68.6 us
    pallas_call x1, Pallas kernels, sequence_body(): call(functools.partial(attend_back_kernel, blocks=blocks), (heads, units)...  68.6 us
    pallas_call x1, Pallas kernels, sequence_body(): call(functools.partial(attend_kernel, blocks=blocks), (heads, units), att...  42.1 us
    pallas_call x1, Pallas kernels, sequence_body(): call(functools.partial(read_back_kernel, blocks=blocks), (heads, units),...  29.2 us
    pallas_call x1, Pallas kernels, sequence_body(): call(project_back_kernel, (shards,), [whole((shards, rows, shard_width)),...  24.8 us
    ppermute x16, starting transfers between devices, across(): lax.ppermute(value, axis, [(source, source ^ bit) for source in range(cou...  22.3 us
    pallas_call x1, Pallas kernels, sequence_body(): call(functools.partial(read_kernel, blocks=blocks), (heads, units), query...  18.3 us
  transfers between devices with their start and end apart: 26, of which 16 were waited for; matrix products, arithmetic and copies ran while one was open for 5% of the time, Pallas kernels for 37%

profile of v4, /device:TPU:0, one launch (start us, length us, event | category | flops | bytes accessed | tf_op | source)
XLA Modules:
  0.0 564.6 jit_solution(5981883733798042139)
XLA Ops:
  10.3 5.1 collective-permute-start
  17.9 5.5 collective-permute-done
  23.4 16.6 %collective-permute-done.1 = bf16[560,256]{1,0:T(8,128)(2,1)S(1)} collective-permute-done((bf16[560,256]{1,0:T(8,128)(2,1)}, bf16[560,256]{1,0:T(8,128)(2,1)S(1)}, u32[]{:S(2)}, u32[]{:S(2)}) %collective-permute-start.1) | collective-permute-done | bytes 286752 | tf_op jit(solution)/shard_map/ppermute | solution.py:1181
  42.0 3.8 all-to-all-start
  48.8 15.2 %collective-permute-done.5 = bf16[2,560,256]{2,1,0:T(8,128)(2,1)S(1)} collective-permute-done((bf16[2,560,256]{2,1,0:T(8,128)(2,1)S(1)}, bf16[2,560,256]{2,1,0:T(8,128)(2,1)S(1)}, u32[]{:S(2)}, u32[]{:S(2)}) %collective-permute-start.5) | collective-permute-done | bytes 573472 | tf_op jit(solution)/shard_map/ppermute | solution.py:1181
  70.4 19.7 %collective-permute-done.6.highx_ref = bf16[2,2,560,256]{3,2,1,0:T(8,128)(2,1)} collective-permute-done((bf16[2,2,560,256]{3,2,1,0:T(8,128)(2,1)S(1)}, bf16[2,2,560,256]{3,2,1,0:T(8,128)(2,1)}, u32[]{:S(2)}, u32[]{:S(2)}) %collective-permute-start.6) | collective-permute-done | bytes 1146912 | tf_op jit(solution)/shard_map/ppermute | solution.py:1181
  90.1 3.6 collective-permute-done.4.lowy_ref
  93.8 4.5 shard_map.317.wq_ref.wk_ref.wv_ref.sq_ref.init_ref
  98.3 14.7 %all-to-all-done.tok_ref = bf16[4,1024,256]{2,1,0:T(8,128)(2,1)S(1)} async-done(((bf16[4,1024,256]{2,1,0:T(8,128)(2,1)}), bf16[4,1024,256]{2,1,0:T(8,128)(2,1)S(1)}, u32[]{:S(2)}, u32[]{:S(2)}) %all-to-all-start) | async-done | bytes 2097184 | tf_op jit(solution)/shard_map/all_to_all | solution.py:1314
  113.0 8.1 %collective-permute-done.7.wqo_ref.wko_ref.wvo_ref.sqo_ref.inito_ref = bf16[2,4,2,560,256]{4,3,2,1,0:T(8,128)(2,1)} collective-permute-done((bf16[2,4,2,560,256]{4,3,2,1,0:T(8,128)(2,1)}, bf16[2,4,2,560,256]{4,3,2,1,0:T(8,128)(2,1)}, u32[]{:S(2)}, u32[]{:S(2)}) %collective-permute-start.7) | collective-permute-done | bytes 4587552 | tf_op jit(solution)/shard_map/ppermute | solution.py:1181
  122.8 12.4 %shard_map.318 = (bf16[1024,1024]{1,0:T(8,128)(2,1)}, bf16[1024,1024]{1,0:T(8,128)(2,1)}, bf16[1024,1024]{1,0:T(8,128)(2,1)}, bf16[1024,1024]{1,0:T(8,128)(2,1)}, bf16[2,512,1024]{2,1,0:T(8,128)(2,1)}) custom-call(s32[5]{0:T(128)} %stack.72.place_ref.refs_0_, bf16[4,1024,256]{2,1,0:T(8,128)(2,1)} %copy-done, f32[1,1024]{1,0:T(1,128)} %reshape.190.gain_ref, ...), custom_call_target="tpu_custom_call" | custom-call | tf_op jit(solution)/shard_map/pallas_call | solution.py:1361
  138.2 18.3 %shard_map.319 = (f32[1024,1024]{1,0:T(8,128)}, bf16[512,1024]{1,0:T(8,128)(2,1)}) custom-call(s32[5]{0:T(128)} %stack.72.place_ref.refs_0_, bf16[2,4,2,560,256]{4,3,2,1,0:T(8,128)(2,1)} %shard_map.317.wq_ref.wk_ref.wv_ref.sq_ref.init_ref, bf16[2,4,2,560,256]{4,3,2,1,0:T(8,128)(2,1)} %collective-permute-done.7.wqo_ref.wko_ref.wvo_ref.sqo_ref.inito_ref, ...), custom_call_target="tpu_custom_call" | custom-call | tf_op jit(solution)/shard_map/pallas_call | solution.py:1390
  165.5 42.1 %shard_map.320 = (bf16[1024,1024]{1,0:T(8,128)(2,1)}, f32[2,8,1,512]{3,2,1,0:T(1,128)}, bf16[1024,1024]{1,0:T(8,128)(2,1)}, bf16[1024,1024]{1,0:T(8,128)(2,1)}) custom-call(s32[5]{0:T(128)} %stack.72.place_ref.refs_0_, s32[2,2]{1,0:T(2,128)} %add_bitcast_fusion.info_ref, bf16[1024,1024]{1,0:T(8,128)(2,1)} %get-tuple-element.98.q_ref, ...), custom_call_target="tpu_custom_call" | custom-call | tf_op jit(solution)/shard_map/pallas_call | solution.py:1446
  207.6 10.0 %shard_map.321 = (f32[1024,1024]{1,0:T(8,128)}, bf16[1024,1024]{1,0:T(8,128)(2,1)}) custom-call(bf16[1024,1024]{1,0:T(8,128)(2,1)} %get-tuple-element.106.att_ref.o_ref, bf16[4,8,128,2304]{3,2,1,0:T(8,128)(2,1)} %bitcast.84, bf16[4,1024,256]{2,1,0:T(8,128)(2,1)} %copy-done, f32[1,1024]{1,0:T(1,128)} %reshape.193.gain_ref), custom_call_target="tpu_custom_call" | custom-call | tf_op jit(solution)/shard_map/pallas_call | solution.py:1460
  217.6 68.6 %shard_map.322 = (bf16[4,1024,256]{2,1,0:T(8,128)(2,1)}, bf16[1024,1024]{1,0:T(8,128)(2,1)}, f32[1,1024]{1,0:T(1,128)}, bf16[4,8,128,2304]{3,2,1,0:T(8,128)(2,1)}) custom-call(s32[5]{0:T(128)} %stack.72.place_ref.refs_0_, bf16[1024,1024]{1,0:T(8,128)(2,1)} %get-tuple-element.108.min_ref, bf16[4096,1024]{1,0:T(8,128)(2,1)} %bitcast.93, ...), custom_call_target="tpu_custom_call" | custom-call | tf_op jit(solution)/shard_map/pallas_call | solution.py:1472
  286.2 9.2 %shard_map.323 = (bf16[1024,1024]{1,0:T(8,128)(2,1)}, bf16[4,8,128,2304]{3,2,1,0:T(8,128)(2,1)}) custom-call(bf16[1024,1024]{1,0:T(8,128)(2,1)} %get-tuple-element.110.gmid_ref, bf16[4,8,128,2304]{3,2,1,0:T(8,128)(2,1)} %bitcast.87, bf16[1024,1024]{1,0:T(8,128)(2,1)} %get-tuple-element.106.att_ref.o_ref, ...), custom_call_target="tpu_custom_call", output_to_operand_aliasing={{1}: (3, {})} | custom-call | tf_op jit(solution)/shard_map/pallas_call | solution.py:1504
  295.5 6.2 %all-to-all-start.1 = ((bf16[4,1024,256]{2,1,0:T(8,128)(2,1)}), bf16[4,1024,256]{2,1,0:T(8,128)(2,1)S(1)}, u32[]{:S(2)}, u32[]{:S(2)}) async-start(bf16[4,1024,256]{2,1,0:T(8,128)(2,1)} %get-tuple-element.117), calls=%async_computation.2 | async-start | bytes 4194304 | tf_op jit(solution)/shard_map/all_to_all | solution.py:1502
  303.1 68.6 %shard_map.324 = (bf16[1024,1024]{1,0:T(8,128)(2,1)}, f32[1024,1024]{1,0:T(8,128)}, f32[1024,1024]{1,0:T(8,128)}, bf16[1024,1024]{1,0:T(8,128)(2,1)}, bf16[1024,...) custom-call(s32[5]{0:T(128)} %stack.72.place_ref.refs_0_, ...), custom_call_target="tpu_custom_call" | custom-call | tf_op jit(solution)/shard_map/pallas_call | solution.py:1529
  377.0 8.8 %collective-permute-done.10.later_ref = bf16[512,1024]{1,0:T(8,128)(2,1)S(1)} collective-permute-done((bf16[512,1024]{1,0:T(8,128)(2,1)}, bf16[512,1024]{1,0:T(8,128)(2,1)S(1)}, u32[]{:S(2)}, u32[]{:S(2)}) %collective-permute-start.10) | collective-permute-done | bytes 1048608 | tf_op jit(solution)/shard_map/ppermute | solution.py:24
  389.6 29.2 %shard_map.325 = (bf16[1024,1024]{1,0:T(8,128)(2,1)}, bf16[1024,1024]{1,0:T(8,128)(2,1)}, f32[512,1024]{1,0:T(8,128)}, f32[512,1024]{1,0:T(8,128)}, f32[8,1,128]{2,1,0:T(1,128)}) custom-call(s32[5]{0:T(128)} %stack.72.place_ref.refs_0_, bf16[2,4,2,560,256]{4,3,2,1,0:T(8,128)(2,1)} %shard_map.317.wq_ref.wk_ref.wv_ref.sq_ref.init_ref, ...), custom_call_target="tpu_custom_call" | custom-call | tf_op jit(solution)/shard_map/pallas_call | solution.py:1557
  418.8 24.8 %shard_map.326 = (bf16[4,1024,256]{2,1,0:T(8,128)(2,1)}, f32[1,1024]{1,0:T(1,128)}, bf16[4,4,560,256]{3,2,1,0:T(8,128)(2,1)}, bf16[4,4,560,256]{3,2,1,0:T(8,128)(2,1)}) custom-call(s32[5]{0:T(128)} %stack.72.place_ref.refs_0_, bf16[4,1024,256]{2,1,0:T(8,128)(2,1)} %copy-done, bf16[1024,1024]{1,0:T(8,128)(2,1)} %get-tuple-element.110.gmid_ref, ...), custom_call_target="tpu_custom_call" | custom-call | tf_op jit(solution)/shard_map/pallas_call | solution.py:1575
  446.2 5.1 all-to-all-start.2
  451.3 2.7 fusion.40
  454.3 2.7 fusion.41
  460.6 24.0 %collective-permute-done.16 = bf16[2,2,560,256]{3,2,0,1:T(8,128)(2,1)S(1)} collective-permute-done((bf16[2,2,560,256]{3,2,0,1:T(8,128)(2,1)S(1)}, bf16[2,2,560,256]{3,2,0,1:T(8,128)(2,1)S(1)}, u32[]{:S(2)}, u32[]{:S(2)}) %collective-permute-start.16) | collective-permute-done | bytes 1146912 | tf_op jit(solution)/shard_map/ppermute | solution.py:1181
  490.7 9.6 %collective-permute-done.17 = bf16[2,560,256]{2,1,0:T(8,128)(2,1)} collective-permute-done((bf16[2,560,256]{2,1,0:T(8,128)(2,1)}, bf16[2,560,256]{2,1,0:T(8,128)(2,1)}, u32[]{:S(2)}, u32[]{:S(2)}) %collective-permute-start.17) | collective-permute-done | bytes 573472 | tf_op jit(solution)/shard_map/ppermute | solution.py:1181
  501.5 8.5 %collective-permute-done.15 = bf16[2,560,256]{2,1,0:T(8,128)(2,1)} collective-permute-done((bf16[2,560,256]{2,1,0:T(8,128)(2,1)}, bf16[2,560,256]{2,1,0:T(8,128)(2,1)}, u32[]{:S(2)}, u32[]{:S(2)}) %collective-permute-start.15) | collective-permute-done | bytes 573472 | tf_op jit(solution)/shard_map/ppermute | solution.py:1181
  514.2 2.6 collective-permute-start.20
  516.8 5.6 all-to-all-done.2.refs_2_
  522.4 18.6 %collective-permute-done.18.refs_4_ = bf16[560,256]{1,0:T(8,128)(2,1)S(1)} collective-permute-done((bf16[560,256]{1,0:T(8,128)(2,1)}, bf16[560,256]{1,0:T(8,128)(2,1)S(1)}, u32[]{:S(2)}, u32[]{:S(2)}) %collective-permute-start.18) | collective-permute-done | bytes 286752 | tf_op jit(solution)/shard_map/ppermute | solution.py:1181
  541.0 8.0 %collective-permute-done.19.refs_5_ = bf16[560,256]{1,0:T(8,128)(2,1)S(1)} collective-permute-done((bf16[560,256]{1,0:T(8,128)(2,1)S(1)}, bf16[560,256]{1,0:T(8,128)(2,1)S(1)}, u32[]{:S(2)}, u32[]{:S(2)}) %collective-permute-start.19) | collective-permute-done | bytes 286752 | tf_op jit(solution)/shard_map/ppermute | solution.py:1181
  549.8 5.5 shard_map.327
  (123 shorter events, 62.1 us)
Async XLA Ops:
  7.2 200.5 %all-gather.2.cloned.1.call-start = ((), (), s32[]{:S(2)}) async-start(), calls=%async_computation.4 | async-start | bytes 19464192 | tf_op jit(solution)/shard_map/all_gather | solution.py:1321
  10.3 13.1 %collective-permute-start = (bf16[560,256]{1,0:T(8,128)(2,1)}, bf16[560,256]{1,0:T(8,128)(2,1)S(1)}, u32[]{:S(2)}, u32[]{:S(2)}) collective-permute-start(bf16[560,256]{1,0:T(8,128)(2,1)} %shard_map.315), channel_id=1, source_target_pairs={{0,3},{1,2},{2,1},{3,0},{4,7},{5,6},{6,5},{7,4},{8,11},{9,10},{10,... | collective-permute-start | bytes 860168 | tf_op jit(solution)/shard_map/ppermute | solution.py:1181
  15.4 24.6 %collective-permute-start.1 = (bf16[560,256]{1,0:T(8,128)(2,1)}, bf16[560,256]{1,0:T(8,128)(2,1)S(1)}, u32[]{:S(2)}, u32[]{:S(2)}) collective-permute-start(bf16[560,256]{1,0:T(8,128)(2,1)} %shard_map.315), channel_id=1, source_target_pairs={{0,2},{1,3},{2,0},{3,1},{4,6},{5,7},{6,4},{7,5},{8,10},{9,11},{10,... | collective-permute-start | bytes 860168 | tf_op jit(solution)/shard_map/ppermute | solution.py:1181
  15.4 24.6 %collective-permute-start.2 = (bf16[560,256]{1,0:T(8,128)(2,1)}, bf16[560,256]{1,0:T(8,128)(2,1)S(1)}, u32[]{:S(2)}, u32[]{:S(2)}) collective-permute-start(bf16[560,256]{1,0:T(8,128)(2,1)} %shard_map.315), channel_id=1, source_target_pairs={{0,1},{1,0},{2,3},{3,2},{4,5},{5,4},{6,7},{7,6},{8,9},{9,8},{10,11... | collective-permute-start | bytes 860168 | tf_op jit(solution)/shard_map/ppermute | solution.py:1181
  42.0 71.0 %all-to-all-start = ((bf16[4,1024,256]{2,1,0:T(8,128)(2,1)}), bf16[4,1024,256]{2,1,0:T(8,128)(2,1)S(1)}, u32[]{:S(2)}, u32[]{:S(2)}) async-start(bf16[4,1024,256]{2,1,0:T(8,128)(2,1)} %param.20), calls=%async_computation | async-start | bytes 4194304 | tf_op jit(solution)/shard_map/all_to_all | solution.py:1314
  45.7 509.6 %reduce-scatter.2.cloned.1.call-start = ((), (), s32[]{:S(2)}) async-start(), calls=%async_computation.5 | async-start | bytes 19464192 | tf_op jit(solution)/shard_map/reduce_scatter | solution.py:1516
  45.7 18.2 %collective-permute-start.5 = (bf16[2,560,256]{2,1,0:T(8,128)(2,1)S(1)}, bf16[2,560,256]{2,1,0:T(8,128)(2,1)S(1)}, u32[]{:S(2)}, u32[]{:S(2)}) collective-permute-start(bf16[2,560,256]{2,1,0:T(8,128)(2,1)S(1)} %get-tuple-element.95), channel_id=1, source_target_pairs={{0,16},{8,24},{16,0},{24,8},{1,17},{9,25},{17,1},{25,9},{2,18},{10... | collective-permute-start | bytes 1720328 | tf_op jit(solution)/shard_map/ppermute | solution.py:1181
  47.3 18.5 %collective-permute-start.3 = (bf16[2,560,256]{2,1,0:T(8,128)(2,1)}, bf16[2,560,256]{2,1,0:T(8,128)(2,1)}, u32[]{:S(2)}, u32[]{:S(2)}) collective-permute-start(bf16[2,560,256]{2,1,0:T(8,128)(2,1)} %get-tuple-element.94), channel_id=1, source_target_pairs={{0,8},{8,0},{16,24},{24,16},{1,9},{9,1},{17,25},{25,17},{2,10},{10... | collective-permute-start | bytes 1720328 | tf_op jit(solution)/shard_map/ppermute | solution.py:1181
  64.2 25.9 %collective-permute-start.6 = (bf16[2,2,560,256]{3,2,1,0:T(8,128)(2,1)S(1)}, bf16[2,2,560,256]{3,2,1,0:T(8,128)(2,1)}, u32[]{:S(2)}, u32[]{:S(2)}) collective-permute-start(bf16[2,2,560,256]{3,2,1,0:T(8,128)(2,1)S(1)} %pad_maximum_fusion.1.high_ref), channel_id=1, source_target_pairs={{0,8},{8,0},{16,24},{24,16},{1,9},{9,1},{17,25},{25,17},{2,10},{10... | collective-permute-start | bytes 3440648 | tf_op jit(solution)/shard_map/ppermute | solution.py:1181
  68.2 25.5 %collective-permute-start.4 = (bf16[2,2,560,256]{3,2,1,0:T(8,128)(2,1)}, bf16[2,2,560,256]{3,2,1,0:T(8,128)(2,1)}, u32[]{:S(2)}, u32[]{:S(2)}) collective-permute-start(bf16[2,2,560,256]{3,2,1,0:T(8,128)(2,1)} %pad_maximum_fusion.low_ref), channel_id=1, source_target_pairs={{0,16},{8,24},{16,0},{24,8},{1,17},{9,25},{17,1},{25,9},{2,18},{10... | collective-permute-start | bytes 3440648 | tf_op jit(solution)/shard_map/ppermute | solution.py:1181
  113.0 8.1 %collective-permute-start.7 = (bf16[2,4,2,560,256]{4,3,2,1,0:T(8,128)(2,1)}, bf16[2,4,2,560,256]{4,3,2,1,0:T(8,128)(2,1)}, u32[]{:S(2)}, u32[]{:S(2)}) collective-permute-start(bf16[2,4,2,560,256]{4,3,2,1,0:T(8,128)(2,1)} %shard_map.317.wq_ref.wk_ref.wv_ref.sq_ref.init_ref), channel_id=1, source_target_pairs={{0,4},{4,0},{1,5},{5,1},{2,6},{6,2},{3,7},{7,3},{8,12},{12,8},{9,1... | collective-permute-start | bytes 13762568 | tf_op jit(solution)/shard_map/ppermute | solution.py:1181
  135.2 21.3 %collective-permute-start.8 = (bf16[2,512,1024]{2,1,0:T(8,128)(2,1)}, bf16[2,512,1024]{2,1,0:T(8,128)(2,1)S(1)}, u32[]{:S(2)}, u32[]{:S(2)}) collective-permute-start(bf16[2,512,1024]{2,1,0:T(8,128)(2,1)} %get-tuple-element.101), channel_id=1, source_target_pairs={{0,4},{1,5},{2,6},{3,7},{8,12},{9,13},{10,14},{11,15},{16,20},{17,... | collective-permute-start | bytes 6291464 | tf_op jit(solution)/shard_map/ppermute | solution.py:24
  138.2 25.6 %copy-start.14 = (f32[1,1024]{1,0:T(1,128)S(1)}, f32[1,1024]{1,0:T(1,128)}, u32[]{:S(2)}) copy-start(f32[1,1024]{1,0:T(1,128)} %reshape.192.gate_ref) | copy-start | bytes 12292
  156.6 7.9 %collective-permute-start.9 = (bf16[512,1024]{1,0:T(8,128)(2,1)}, bf16[512,1024]{1,0:T(8,128)(2,1)S(1)}, u32[]{:S(2)}, u32[]{:S(2)}) collective-permute-start(bf16[512,1024]{1,0:T(8,128)(2,1)} %get-tuple-element.105), channel_id=1, source_target_pairs={{0,4},{1,5},{2,6},{3,7},{8,12},{9,13},{10,14},{11,15},{16,20},{17,... | collective-permute-start | bytes 3145736 | tf_op jit(solution)/shard_map/ppermute | solution.py:24
  295.5 81.5 %all-to-all-start.1 = ((bf16[4,1024,256]{2,1,0:T(8,128)(2,1)}), bf16[4,1024,256]{2,1,0:T(8,128)(2,1)S(1)}, u32[]{:S(2)}, u32[]{:S(2)}) async-start(bf16[4,1024,256]{2,1,0:T(8,128)(2,1)} %get-tuple-element.117), calls=%async_computation.2 | async-start | bytes 4194304 | tf_op jit(solution)/shard_map/all_to_all | solution.py:1502
  303.1 72.5 %copy-start.9 = (f32[1536,32]{1,0:T(8,128)S(1)}, f32[1536,32]{1,0:T(8,128)}, u32[]{:S(2)}) copy-start(f32[1536,32]{1,0:T(8,128)} %constant.113.clone) | copy-start | bytes 589828
  303.1 73.9 %copy-start.15 = (f32[1,1024]{1,0:T(1,128)S(1)}, f32[1,1024]{1,0:T(1,128)}, u32[]{:S(2)}) copy-start(f32[1,1024]{1,0:T(1,128)} %get-tuple-element.138) | copy-start | bytes 12292
  371.7 14.1 %collective-permute-start.10 = (bf16[512,1024]{1,0:T(8,128)(2,1)}, bf16[512,1024]{1,0:T(8,128)(2,1)S(1)}, u32[]{:S(2)}, u32[]{:S(2)}) collective-permute-start(bf16[512,1024]{1,0:T(8,128)(2,1)} %get-tuple-element.122), channel_id=1, source_target_pairs={{4,0},{5,1},{6,2},{7,3},{12,8},{13,9},{14,10},{15,11},{20,16},{21,... | collective-permute-start | bytes 3145736 | tf_op jit(solution)/shard_map/ppermute | solution.py:24
  373.0 14.5 %collective-permute-start.11 = (bf16[512,1024]{1,0:T(8,128)(2,1)}, bf16[512,1024]{1,0:T(8,128)(2,1)}, u32[]{:S(2)}, u32[]{:S(2)}) collective-permute-start(bf16[512,1024]{1,0:T(8,128)(2,1)} %get-tuple-element.127), channel_id=1, source_target_pairs={{4,0},{5,1},{6,2},{7,3},{12,8},{13,9},{14,10},{15,11},{20,16},{21,... | collective-permute-start | bytes 3145736 | tf_op jit(solution)/shard_map/ppermute | solution.py:24
  374.3 15.3 %collective-permute-start.12 = (bf16[512,1024]{1,0:T(8,128)(2,1)}, bf16[512,1024]{1,0:T(8,128)(2,1)}, u32[]{:S(2)}, u32[]{:S(2)}) collective-permute-start(bf16[512,1024]{1,0:T(8,128)(2,1)} %get-tuple-element.128), channel_id=1, source_target_pairs={{4,0},{5,1},{6,2},{7,3},{12,8},{13,9},{14,10},{15,11},{20,16},{21,... | collective-permute-start | bytes 3145736 | tf_op jit(solution)/shard_map/ppermute | solution.py:24
  377.0 41.8 %copy-start.2 = (bf16[4,1024,256]{2,1,0:T(8,128)(2,1)}, bf16[4,1024,256]{2,1,0:T(8,128)(2,1)S(1)}, u32[]{:S(2)}) copy-start(bf16[4,1024,256]{2,1,0:T(8,128)(2,1)S(1)} %all-to-all-done.1.refs_1_) | copy-start | bytes 6291460
  418.8 25.6 %copy-start.16 = (f32[8,1,128]{2,1,0:T(1,128)S(1)}, f32[8,1,128]{2,1,0:T(1,128)}, u32[]{:S(2)}) copy-start(f32[8,1,128]{2,1,0:T(1,128)} %get-tuple-element.139) | copy-start | bytes 12292
  445.2 9.1 %collective-permute-start.13 = (bf16[4,4,560,256]{3,2,1,0:T(8,128)(2,1)}, bf16[4,4,560,256]{3,2,1,0:T(8,128)(2,1)}, u32[]{:S(2)}, u32[]{:S(2)}) collective-permute-start(bf16[4,4,560,256]{3,2,1,0:T(8,128)(2,1)} %get-tuple-element.201), channel_id=1, source_target_pairs={{0,4},{4,0},{1,5},{5,1},{2,6},{6,2},{3,7},{7,3},{8,12},{12,8},{9,1... | collective-permute-start | bytes 13762568 | tf_op jit(solution)/shard_map/ppermute | solution.py:1181
  446.2 76.2 %all-to-all-start.2 = ((bf16[4,1024,256]{2,1,0:T(8,128)(2,1)}), bf16[4,1024,256]{2,1,0:T(8,128)(2,1)S(1)}, u32[]{:S(2)}, u32[]{:S(2)}) async-start(bf16[4,1024,256]{2,1,0:T(8,128)(2,1)} %get-tuple-element.135), calls=%async_computation.3 | async-start | bytes 4194304 | tf_op jit(solution)/shard_map/all_to_all | solution.py:1591
  457.5 27.2 %collective-permute-start.16 = (bf16[2,2,560,256]{3,2,0,1:T(8,128)(2,1)S(1)}, bf16[2,2,560,256]{3,2,0,1:T(8,128)(2,1)S(1)}, u32[]{:S(2)}, u32[]{:S(2)}) collective-permute-start(bf16[2,2,560,256]{3,2,0,1:T(8,128)(2,1)S(1)} %fusion.5), channel_id=1, source_target_pairs={{0,16},{8,24},{16,0},{24,8},{1,17},{9,25},{17,1},{25,9},{2,18},{10... | collective-permute-start | bytes 3440648 | tf_op jit(solution)/shard_map/ppermute | solution.py:1181
  458.9 27.8 %collective-permute-start.14 = (bf16[2,2,560,256]{3,2,0,1:T(8,128)(2,1)S(1)}, bf16[2,2,560,256]{3,2,0,1:T(8,128)(2,1)S(1)}, u32[]{:S(2)}, u32[]{:S(2)}) collective-permute-start(bf16[2,2,560,256]{3,2,0,1:T(8,128)(2,1)S(1)} %fusion.3), channel_id=1, source_target_pairs={{0,8},{8,0},{16,24},{24,16},{1,9},{9,1},{17,25},{25,17},{2,10},{10... | collective-permute-start | bytes 3440648 | tf_op jit(solution)/shard_map/ppermute | solution.py:1181
  485.9 14.4 %collective-permute-start.17 = (bf16[2,560,256]{2,1,0:T(8,128)(2,1)}, bf16[2,560,256]{2,1,0:T(8,128)(2,1)}, u32[]{:S(2)}, u32[]{:S(2)}) collective-permute-start(bf16[2,560,256]{2,1,0:T(8,128)(2,1)} %dynamic-slice_bitcast_fusion), channel_id=1, source_target_pairs={{0,8},{8,0},{16,24},{24,16},{1,9},{9,1},{17,25},{25,17},{2,10},{10... | collective-permute-start | bytes 1720328 | tf_op jit(solution)/shard_map/ppermute | solution.py:1181
  489.0 21.0 %collective-permute-start.15 = (bf16[2,560,256]{2,1,0:T(8,128)(2,1)}, bf16[2,560,256]{2,1,0:T(8,128)(2,1)}, u32[]{:S(2)}, u32[]{:S(2)}) collective-permute-start(bf16[2,560,256]{2,1,0:T(8,128)(2,1)} %dynamic-slice_bitcast_fusion.1), channel_id=1, source_target_pairs={{0,16},{8,24},{16,0},{24,8},{1,17},{9,25},{17,1},{25,9},{2,18},{10... | collective-permute-start | bytes 1720328 | tf_op jit(solution)/shard_map/ppermute | solution.py:1181
  512.4 28.6 %collective-permute-start.18 = (bf16[560,256]{1,0:T(8,128)(2,1)}, bf16[560,256]{1,0:T(8,128)(2,1)S(1)}, u32[]{:S(2)}, u32[]{:S(2)}) collective-permute-start(bf16[560,256]{1,0:T(8,128)(2,1)} %get-tuple-element.188), channel_id=1, source_target_pairs={{0,1},{1,0},{2,3},{3,2},{4,5},{5,4},{6,7},{7,6},{8,9},{9,8},{10,11... | collective-permute-start | bytes 860168 | tf_op jit(solution)/shard_map/ppermute | solution.py:1181
  512.4 36.6 %collective-permute-start.19 = (bf16[560,256]{1,0:T(8,128)(2,1)S(1)}, bf16[560,256]{1,0:T(8,128)(2,1)S(1)}, u32[]{:S(2)}, u32[]{:S(2)}) collective-permute-start(bf16[560,256]{1,0:T(8,128)(2,1)S(1)} %get-tuple-element.189), channel_id=1, source_target_pairs={{0,2},{1,3},{2,0},{3,1},{4,6},{5,7},{6,4},{7,5},{8,10},{9,11},{10,... | collective-permute-start | bytes 860168 | tf_op jit(solution)/shard_map/ppermute | solution.py:1181
  514.2 34.8 %collective-permute-start.20 = (bf16[560,256]{1,0:T(8,128)(2,1)S(1)}, bf16[560,256]{1,0:T(8,128)(2,1)S(1)}, u32[]{:S(2)}, u32[]{:S(2)}) collective-permute-start(bf16[560,256]{1,0:T(8,128)(2,1)S(1)} %get-tuple-element.186), channel_id=1, source_target_pairs={{0,3},{1,2},{2,1},{3,0},{4,7},{5,6},{6,5},{7,4},{8,11},{9,10},{10,... | collective-permute-start | bytes 860168 | tf_op jit(solution)/shard_map/ppermute | solution.py:1181
  522.4 26.6 %copy-start.3 = (bf16[4,1024,256]{2,1,0:T(8,128)(2,1)}, bf16[4,1024,256]{2,1,0:T(8,128)(2,1)S(1)}, u32[]{:S(2)}) copy-start(bf16[4,1024,256]{2,1,0:T(8,128)(2,1)S(1)} %all-to-all-done.2.refs_2_) | copy-start | bytes 6291460
  (12 other events, 82.5 us)
Sparse Core Ops, SparseCore 0:
  42.1 153.0 all-gather.1
  295.6 253.3 reduce-scatter.1

commit v5 on v4

--- a/solution.py
+++ b/solution.py
@@ -1087,19 +1087,22 @@
         gmid_ref[...] = (cot_ref[...].astype(F32) + back).astype(BF)
 
 
-def out_back_kernel(gmid_ref, wo_ref, att_ref, late_ref, gatt_ref, gwo_ref, gmid_t):
+def out_gradient_kernel(gmid_ref, att_ref, late_ref, gwo_ref, gmid_t):
     @pl.when(pl.program_id(0) == 0)
     def _():
         gmid_t[...] = gmid_ref[...].T
 
+    gwo_ref[...] = nn(gmid_t[...], att_ref[...]).astype(BF).reshape(gwo_ref.shape)
+
+
+def out_back_kernel(gmid_ref, wo_ref, gatt_ref):
     gatt_ref[...] = nn(gmid_ref[...], flat(wo_ref)).astype(BF)
-    gwo_ref[...] = nn(gmid_t[...], att_ref[...]).astype(BF).reshape(gwo_ref.shape)
-
-
-def project_back_kernel(
-    place_ref, tok_ref, gmid_ref, gain_ref, gq_ref, gk_ref, gv_ref,
-    wq_ref, wqo_ref, wk_ref, wko_ref, wv_ref, wvo_ref, gsq_ref, ginit_ref, gmk_ref, gmv_ref,
-    gtok_ref, ggain_ref, gown_ref, gother_ref, ain_t, acc_ref, pack_ref,
+
+
+def weight_back_kernel(
+    place_ref, tok_ref, gain_ref, gq_ref, gk_ref, gv_ref, wq_ref, wqo_ref, wk_ref, wko_ref,
+    wv_ref, wvo_ref, gsq_ref, ginit_ref, gmk_ref, gmv_ref,
+    gown_ref, gother_ref, ggain_ref, ain_t, pack_ref, product_ref,
 ):
     t = pl.program_id(0)
 
@@ -1107,18 +1110,17 @@
     def _():
         x = joined(tok_ref)
         ain_t[...] = (x * inverse_rms(x) * gain_ref[...]).astype(BF).T
-        acc_ref[...] = jnp.zeros_like(acc_ref)
+        product_ref[...] = jnp.zeros_like(product_ref)
 
     groups, _, lanes = pack_ref.shape
     at = 0
     for g_ref, w_ref, w_other in (
         (gq_ref, wq_ref, wqo_ref), (gk_ref, wk_ref, wko_ref), (gv_ref, wv_ref, wvo_ref)
     ):
-        g = g_ref[...]
-        acc_ref[...] += nt(g, merged(place_ref, w_ref, w_other))
-        grad = nn(ain_t[...], g).astype(BF)
+        grad = nn(ain_t[...], g_ref[...])
+        product_ref[...] += grad * merged(place_ref, w_ref, w_other).astype(F32)
         rows = grad.shape[0] // groups
-        pack_ref[:, at : at + rows] = grad.reshape(groups, rows, lanes)
+        pack_ref[:, at : at + rows] = grad.astype(BF).reshape(groups, rows, lanes)
         at += rows
     for g_ref in (gsq_ref, ginit_ref):
         rows = g_ref.shape[0] // groups
@@ -1137,14 +1139,32 @@
 
     @pl.when(t == pl.num_programs(0) - 1)
     def _():
+        ggain_ref[...] = jnp.sum(product_ref[...], axis=1, keepdims=True)
+
+
+def project_back_kernel(
+    place_ref, tok_ref, gmid_ref, gain_ref, gq_ref, gk_ref, gv_ref,
+    wq_ref, wqo_ref, wk_ref, wko_ref, wv_ref, wvo_ref, gtok_ref, acc_ref,
+):
+    t = pl.program_id(0)
+
+    @pl.when(t == 0)
+    def _():
+        acc_ref[...] = jnp.zeros_like(acc_ref)
+
+    total = nt(gq_ref[...], merged(place_ref, wq_ref, wqo_ref))
+    total = total + nt(gk_ref[...], merged(place_ref, wk_ref, wko_ref))
+    acc_ref[...] += total + nt(gv_ref[...], merged(place_ref, wv_ref, wvo_ref))
+
+    @pl.when(t == pl.num_programs(0) - 1)
+    def _():
         x = joined(tok_ref)
         inverse = inverse_rms(x)
         normed = x * inverse
-        ga = acc_ref[...]
-        ggain_ref[...] = jnp.sum(ga * normed, axis=0, keepdims=True)
-        scaled = ga * gain_ref[...]
+        scaled = acc_ref[...] * gain_ref[...]
         back = inverse * (scaled - normed * jnp.mean(scaled * normed, axis=-1, keepdims=True))
         grad = (gmid_ref[...].astype(F32) + back).astype(BF)
+        lanes = gtok_ref.shape[2]
         for part in range(gtok_ref.shape[0]):
             gtok_ref[part] = grad[:, part * lanes : (part + 1) * lanes]
 
@@ -1501,18 +1521,24 @@
     )
     output = lax.all_to_all(output, "tp", 0, 0, tiled=True)
 
-    grad_attended, late_grad = pl.pallas_call(
+    late_grad = pl.pallas_call(
+        out_gradient_kernel,
+        grid=(shards,),
+        in_specs=[whole((rows, width)), column, pl.BlockSpec(memory_space=pl.ANY)],
+        out_specs=out_weight,
+        out_shape=jax.ShapeDtypeStruct(late_grad.shape, BF),
+        scratch_shapes=[pltpu.VMEM((width, rows), BF)],
+        compiler_params=params(),
+        input_output_aliases={2: 0},
+    )(middle_grad, attended, late_grad)
+    grad_attended = pl.pallas_call(
         out_back_kernel,
         grid=(shards,),
-        in_specs=[
-            whole((rows, width)), out_weight, column, pl.BlockSpec(memory_space=pl.ANY)
-        ],
-        out_specs=[column, out_weight],
-        out_shape=[wide, jax.ShapeDtypeStruct(late_grad.shape, BF)],
-        scratch_shapes=[pltpu.VMEM((width, rows), BF)],
+        in_specs=[whole((rows, width)), out_weight],
+        out_specs=column,
+        out_shape=wide,
         compiler_params=params(),
-        input_output_aliases={3: 1},
-    )(middle_grad, late, attended, late_grad)
+    )(middle_grad, late)
     late_grad = lax.psum_scatter(
         late_grad.reshape(shards * groups * own_rows, late_width), everywhere,
         scatter_dimension=0, tiled=True,
@@ -1572,22 +1598,33 @@
     slots_of = pl.BlockSpec((slots, shard_width), lambda t, *_: (0, t))
     piece = pl.BlockSpec((1, pairs, full_rows, shard_width), lambda t, *_: (t, 0, 0, 0))
     pieces = jax.ShapeDtypeStruct((shards, pairs, full_rows, shard_width), BF)
-    token_grad, gain_one_grad, grad_own, grad_other = call(
+    token_shards = whole((shards, rows, shard_width))
+    weights = weight(0) + weight(1) + weight(2)
+    weight_args = [first_own, first_other] * 3
+    grad_own, grad_other, gain_one_grad = call(
+        weight_back_kernel,
+        (shards,),
+        [token_shards, whole((1, width)), column, column, column]
+        + weights + [slots_of, slots_of, maps_of, maps_of],
+        [piece, piece, whole((width, 1))],
+        [pieces, pieces, jax.ShapeDtypeStruct((width, 1), F32)],
+        [
+            pltpu.VMEM((width, rows), BF), pltpu.VMEM((groups, full_rows, shard_width), BF),
+            pltpu.VMEM((width, shard_width), F32),
+        ],
+    )(
+        place, x, gain_one, grad_queries, grad_keys, grad_values, *weight_args,
+        slot_query_grad, init_grad, key_map_grad, value_map_grad,
+    )
+    gain_one_grad = gain_one_grad.reshape(1, width) / gain_one
+    token_grad = call(
         project_back_kernel,
         (shards,),
-        [whole((shards, rows, shard_width)), whole((rows, width)), whole((1, width))]
-        + [column, column, column]
-        + weight(0) + weight(1) + weight(2) + [slots_of, slots_of, maps_of, maps_of],
-        [whole((shards, rows, shard_width)), whole((1, width)), piece, piece],
-        [split, jax.ShapeDtypeStruct((1, width), F32), pieces, pieces],
-        [
-            pltpu.VMEM((width, rows), BF), pltpu.VMEM((rows, width), F32),
-            pltpu.VMEM((groups, full_rows, shard_width), BF),
-        ],
-    )(
-        place, x, middle_grad, gain_one, grad_queries, grad_keys, grad_values,
-        *([first_own, first_other] * 3), slot_query_grad, init_grad, key_map_grad, value_map_grad,
-    )
+        [token_shards, whole((rows, width)), whole((1, width)), column, column, column] + weights,
+        token_shards,
+        split,
+        [pltpu.VMEM((rows, width), F32)],
+    )(place, x, middle_grad, gain_one, grad_queries, grad_keys, grad_values, *weight_args)
     token_grad = lax.all_to_all(token_grad, "tp", 0, 0, tiled=True)
 
     vector_sums = [gain_one_grad, gain_two_grad, gate_grad.reshape(1, width), bias_grad]

time: 575 us -> 572 us (level)
  waiting for transfers between devices: 170 us -> 158 us
  Pallas kernels: 299 us -> 310 us
    pallas_call x1 -> x3, Pallas kernels: 24.8 us -> 38.1 us  [the longest x1 16.4 us: sequence_body(): call(weight_back_kernel, (shards,), [token_shards, whole((1, width)), col...]
    ppermute x16, waiting for transfers between devices: 137 us -> 125 us  [across(): lax.ppermute(value, axis, [(source, source ^ bit) for source in range(cou...]
  transfers between devices with their start and end apart: 26 -> 26, of which waited for: 16 -> 17; matrix products, arithmetic and copies ran while one was open for 5% -> 5% of each run, Pallas kernels for 37% -> 39%
where the time goes in v5:
time: 572 us; the launch traced here: 565 us
  Pallas kernels  310 us (54%)
  waiting for transfers between devices  158 us (28%)
  starting transfers between devices  46 us (8%)
  local copies, waits for them, and re-layouts  16.4 us (3%)
  other arithmetic  15.4 us (3%)
  between operations  14.7 us (3%)
    ppermute x16, waiting for transfers between devices, across(): lax.ppermute(value, axis, [(source, source ^ bit) for source in range(cou...  125 us
    pallas_call x1, Pallas kernels, sequence_body(): call(functools.partial(attend_back_kernel, blocks=blocks), (heads, units)...  68.7 us
    pallas_call x1, Pallas kernels, sequence_body(): call(mlp_kernel, (shards * per_shard, 2), [whole((rows, width)), pl.Block...  68.6 us
    pallas_call x1, Pallas kernels, sequence_body(): call(functools.partial(attend_kernel, blocks=blocks), (heads, units), att...  42.2 us
    pallas_call x1, Pallas kernels, sequence_body(): call(functools.partial(read_back_kernel, blocks=blocks), (heads, units),...  29.2 us
    ppermute x16, starting transfers between devices, across(): lax.ppermute(value, axis, [(source, source ^ bit) for source in range(cou...  20.9 us
    pallas_call x1, Pallas kernels, sequence_body(): call(functools.partial(read_kernel, blocks=blocks), (heads, units), query...  18.5 us
    pallas_call x1, Pallas kernels, sequence_body(): call(weight_back_kernel, (shards,), [token_shards, whole((1, width)), col...  16.4 us
  transfers between devices with their start and end apart: 26, of which 17 were waited for; matrix products, arithmetic and copies ran while one was open for 5% of the time, Pallas kernels for 39%

profile of v5, /device:TPU:0, one launch (start us, length us, event | category | flops | bytes accessed | tf_op | source)
XLA Modules:
  0.0 565.5 jit_solution(8646388624712437181)
XLA Ops:
  10.3 3.1 collective-permute-start.2
  17.9 7.8 %collective-permute-done.2 = bf16[560,256]{1,0:T(8,128)(2,1)S(1)} collective-permute-done((bf16[560,256]{1,0:T(8,128)(2,1)}, bf16[560,256]{1,0:T(8,128)(2,1)S(1)}, u32[]{:S(2)}, u32[]{:S(2)}) %collective-permute-start.2) | collective-permute-done | bytes 286752 | tf_op jit(solution)/shard_map/ppermute | solution.py:1201
  25.8 10.7 %collective-permute-done.1 = bf16[560,256]{1,0:T(8,128)(2,1)S(1)} collective-permute-done((bf16[560,256]{1,0:T(8,128)(2,1)}, bf16[560,256]{1,0:T(8,128)(2,1)S(1)}, u32[]{:S(2)}, u32[]{:S(2)}) %collective-permute-start.1) | collective-permute-done | bytes 286752 | tf_op jit(solution)/shard_map/ppermute | solution.py:1201
  38.4 7.6 %all-to-all-start = ((bf16[4,1024,256]{2,1,0:T(8,128)(2,1)}), bf16[4,1024,256]{2,1,0:T(8,128)(2,1)S(1)}, u32[]{:S(2)}, u32[]{:S(2)}) async-start(bf16[4,1024,256]{2,1,0:T(8,128)(2,1)} %param.20), calls=%async_computation | async-start | bytes 4194304 | tf_op jit(solution)/shard_map/all_to_all | solution.py:1334
  49.1 14.5 %collective-permute-done.5 = bf16[2,560,256]{2,1,0:T(8,128)(2,1)S(1)} collective-permute-done((bf16[2,560,256]{2,1,0:T(8,128)(2,1)S(1)}, bf16[2,560,256]{2,1,0:T(8,128)(2,1)S(1)}, u32[]{:S(2)}, u32[]{:S(2)}) %collective-permute-start.5) | collective-permute-done | bytes 573472 | tf_op jit(solution)/shard_map/ppermute | solution.py:1201
  70.4 19.3 %collective-permute-done.6.highx_ref = bf16[2,2,560,256]{3,2,1,0:T(8,128)(2,1)} collective-permute-done((bf16[2,2,560,256]{3,2,1,0:T(8,128)(2,1)S(1)}, bf16[2,2,560,256]{3,2,1,0:T(8,128)(2,1)}, u32[]{:S(2)}, u32[]{:S(2)}) %collective-permute-start.6) | collective-permute-done | bytes 1146912 | tf_op jit(solution)/shard_map/ppermute | solution.py:1201
  92.4 4.5 shard_map.317.wq_ref.wk_ref.wv_ref.sq_ref.init_ref
  96.9 14.3 %all-to-all-done.tok_ref = bf16[4,1024,256]{2,1,0:T(8,128)(2,1)S(1)} async-done(((bf16[4,1024,256]{2,1,0:T(8,128)(2,1)}), bf16[4,1024,256]{2,1,0:T(8,128)(2,1)S(1)}, u32[]{:S(2)}, u32[]{:S(2)}) %all-to-all-start) | async-done | bytes 2097184 | tf_op jit(solution)/shard_map/all_to_all | solution.py:1334
  111.2 8.1 %collective-permute-done.7.wqo_ref.wko_ref.wvo_ref.sqo_ref.inito_ref = bf16[2,4,2,560,256]{4,3,2,1,0:T(8,128)(2,1)} collective-permute-done((bf16[2,4,2,560,256]{4,3,2,1,0:T(8,128)(2,1)}, bf16[2,4,2,560,256]{4,3,2,1,0:T(8,128)(2,1)}, u32[]{:S(2)}, u32[]{:S(2)}) %collective-permute-start.7) | collective-permute-done | bytes 4587552 | tf_op jit(solution)/shard_map/ppermute | solution.py:1201
  121.0 12.4 %shard_map.318 = (bf16[1024,1024]{1,0:T(8,128)(2,1)}, bf16[1024,1024]{1,0:T(8,128)(2,1)}, bf16[1024,1024]{1,0:T(8,128)(2,1)}, bf16[1024,1024]{1,0:T(8,128)(2,1)}, bf16[2,512,1024]{2,1,0:T(8,128)(2,1)}) custom-call(s32[5]{0:T(128)} %stack.72.place_ref.refs_0_, bf16[4,1024,256]{2,1,0:T(8,128)(2,1)} %copy-done, f32[1,1024]{1,0:T(1,128)} %reshape.200.gain_ref, ...), custom_call_target="tpu_custom_call" | custom-call | tf_op jit(solution)/shard_map/pallas_call | solution.py:1381
  136.5 18.5 %shard_map.319 = (f32[1024,1024]{1,0:T(8,128)}, bf16[512,1024]{1,0:T(8,128)(2,1)}) custom-call(s32[5]{0:T(128)} %stack.72.place_ref.refs_0_, bf16[2,4,2,560,256]{4,3,2,1,0:T(8,128)(2,1)} %shard_map.317.wq_ref.wk_ref.wv_ref.sq_ref.init_ref, bf16[2,4,2,560,256]{4,3,2,1,0:T(8,128)(2,1)} %collective-permute-done.7.wqo_ref.wko_ref.wvo_ref.sqo_ref.inito_ref, ...), custom_call_target="tpu_custom_call" | custom-call | tf_op jit(solution)/shard_map/pallas_call | solution.py:1410
  163.9 42.2 %shard_map.320 = (bf16[1024,1024]{1,0:T(8,128)(2,1)}, f32[2,8,1,512]{3,2,1,0:T(1,128)}, bf16[1024,1024]{1,0:T(8,128)(2,1)}, bf16[1024,1024]{1,0:T(8,128)(2,1)}) custom-call(s32[5]{0:T(128)} %stack.72.place_ref.refs_0_, s32[2,2]{1,0:T(2,128)} %add_bitcast_fusion.info_ref, bf16[1024,1024]{1,0:T(8,128)(2,1)} %get-tuple-element.95.q_ref, ...), custom_call_target="tpu_custom_call" | custom-call | tf_op jit(solution)/shard_map/pallas_call | solution.py:1466
  206.1 10.0 %shard_map.321 = (f32[1024,1024]{1,0:T(8,128)}, bf16[1024,1024]{1,0:T(8,128)(2,1)}) custom-call(bf16[1024,1024]{1,0:T(8,128)(2,1)} %get-tuple-element.103.att_ref.o_ref, bf16[4,8,128,2304]{3,2,1,0:T(8,128)(2,1)} %bitcast.84, bf16[4,1024,256]{2,1,0:T(8,128)(2,1)} %copy-done, f32[1,1024]{1,0:T(1,128)} %reshape.203.gain_ref), custom_call_target="tpu_custom_call" | custom-call | tf_op jit(solution)/shard_map/pallas_call | solution.py:1480
  216.1 68.6 %shard_map.322 = (bf16[4,1024,256]{2,1,0:T(8,128)(2,1)}, bf16[1024,1024]{1,0:T(8,128)(2,1)}, f32[1,1024]{1,0:T(1,128)}, bf16[4,8,128,2304]{3,2,1,0:T(8,128)(2,1)}) custom-call(s32[5]{0:T(128)} %stack.72.place_ref.refs_0_, bf16[1024,1024]{1,0:T(8,128)(2,1)} %get-tuple-element.105.min_ref, bf16[4096,1024]{1,0:T(8,128)(2,1)} %bitcast.93, ...), custom_call_target="tpu_custom_call" | custom-call | tf_op jit(solution)/shard_map/pallas_call | solution.py:1492
  284.7 6.8 %shard_map.323 = bf16[4,8,128,2304]{3,2,1,0:T(8,128)(2,1)} custom-call(bf16[1024,1024]{1,0:T(8,128)(2,1)} %get-tuple-element.107.gmid_ref, bf16[1024,1024]{1,0:T(8,128)(2,1)} %get-tuple-element.103.att_ref.o_ref, bf16[4,8,128,2304]{3,2,1,0:T(8,128)(2,1)} %get-tuple-element.108.late_ref), custom_call_target="tpu_custom_call", output_to_operand_aliasing={{}: (2, {})} | custom-call | tf_op jit(solution)/shard_map/pallas_call | solution.py:1524
  291.5 4.7 all-to-all-start.1
  297.7 6.4 %shard_map.324.do_ref = bf16[1024,1024]{1,0:T(8,128)(2,1)} custom-call(bf16[1024,1024]{1,0:T(8,128)(2,1)} %get-tuple-element.107.gmid_ref, bf16[4,8,128,2304]{3,2,1,0:T(8,128)(2,1)} %bitcast.87), custom_call_target="tpu_custom_call" | custom-call | tf_op jit(solution)/shard_map/pallas_call | solution.py:1534
  304.1 68.7 %shard_map.325 = (bf16[1024,1024]{1,0:T(8,128)(2,1)}, f32[1024,1024]{1,0:T(8,128)}, f32[1024,1024]{1,0:T(8,128)}, bf16[1024,1024]{1,0:T(8,128)(2,1)}, bf16[1024,...) custom-call(s32[5]{0:T(128)} %stack.72.place_ref.refs_0_, ...), custom_call_target="tpu_custom_call" | custom-call | tf_op jit(solution)/shard_map/pallas_call | solution.py:1555
  378.6 8.2 %collective-permute-done.10.later_ref = bf16[512,1024]{1,0:T(8,128)(2,1)S(1)} collective-permute-done((bf16[512,1024]{1,0:T(8,128)(2,1)}, bf16[512,1024]{1,0:T(8,128)(2,1)S(1)}, u32[]{:S(2)}, u32[]{:S(2)}) %collective-permute-start.10) | collective-permute-done | bytes 1048608 | tf_op jit(solution)/shard_map/ppermute | solution.py:24
  390.5 29.2 %shard_map.326 = (bf16[1024,1024]{1,0:T(8,128)(2,1)}, bf16[1024,1024]{1,0:T(8,128)(2,1)}, f32[512,1024]{1,0:T(8,128)}, f32[512,1024]{1,0:T(8,128)}, f32[8,1,128]{2,1,0:T(1,128)}) custom-call(s32[5]{0:T(128)} %stack.72.place_ref.refs_0_, bf16[2,4,2,560,256]{4,3,2,1,0:T(8,128)(2,1)} %shard_map.317.wq_ref.wk_ref.wv_ref.sq_ref.init_ref, ...), custom_call_target="tpu_custom_call" | custom-call | tf_op jit(solution)/shard_map/pallas_call | solution.py:1583
  419.8 16.4 %shard_map.328 = (bf16[4,4,560,256]{3,2,1,0:T(8,128)(2,1)}, bf16[4,4,560,256]{3,2,1,0:T(8,128)(2,1)}, f32[1024,1]{1,0:T(8,128)}) custom-call(s32[5]{0:T(128)} %stack.72.place_ref.refs_0_, bf16[4,1024,256]{2,1,0:T(8,128)(2,1)} %copy-done, f32[1,1024]{1,0:T(1,128)} %reshape.200.gain_ref, bf16[1024,1024]{1,0:T(8,128)(2,1)} %get-tuple-element.114.gq_ref, ...), custom_call_target="tpu_custom_call" | custom-call | tf_op jit(solution)/shard_map/pallas_call | solution.py:1604
  439.4 14.9 %shard_map.327 = bf16[4,1024,256]{2,1,0:T(8,128)(2,1)} custom-call(s32[5]{0:T(128)} %stack.72.place_ref.refs_0_, bf16[4,1024,256]{2,1,0:T(8,128)(2,1)} %copy-done, bf16[1024,1024]{1,0:T(8,128)(2,1)} %get-tuple-element.107.gmid_ref, f32[1,1024]{1,0:T(1,128)} %reshape.200.gain_ref, bf16[1024,1024]{1,0:T(8,128)(2,1)} %get-tuple-element.114.gq_ref, ...), custom_call_target="tpu_custom_call" | custom-call | tf_op jit(solution)/shard_map/pallas_call | solution.py:1620
  454.4 5.1 all-to-all-start.2
  459.5 2.7 fusion.40
  462.5 2.7 fusion.41
  469.2 28.7 %collective-permute-done.16 = bf16[2,2,560,256]{3,2,0,1:T(8,128)(2,1)S(1)} collective-permute-done((bf16[2,2,560,256]{3,2,0,1:T(8,128)(2,1)S(1)}, bf16[2,2,560,256]{3,2,0,1:T(8,128)(2,1)S(1)}, u32[]{:S(2)}, u32[]{:S(2)}) %collective-permute-start.16) | collective-permute-done | bytes 1146912 | tf_op jit(solution)/shard_map/ppermute | solution.py:1201
  503.6 12.9 %collective-permute-done.17 = bf16[2,560,256]{2,1,0:T(8,128)(2,1)} collective-permute-done((bf16[2,560,256]{2,1,0:T(8,128)(2,1)}, bf16[2,560,256]{2,1,0:T(8,128)(2,1)}, u32[]{:S(2)}, u32[]{:S(2)}) %collective-permute-start.17) | collective-permute-done | bytes 573472 | tf_op jit(solution)/shard_map/ppermute | solution.py:1201
  520.2 3.3 collective-permute-start.20
  524.6 6.9 %all-to-all-done.2.refs_2_ = bf16[4,1024,256]{2,1,0:T(8,128)(2,1)S(1)} async-done(((bf16[4,1024,256]{2,1,0:T(8,128)(2,1)}), bf16[4,1024,256]{2,1,0:T(8,128)(2,1)S(1)}, u32[]{:S(2)}, u32[]{:S(2)}) %all-to-all-start.2) | async-done | bytes 2097184 | tf_op jit(solution)/shard_map/all_to_all | solution.py:1628
  532.0 5.7 %collective-permute-done.18.refs_4_ = bf16[560,256]{1,0:T(8,128)(2,1)S(1)} collective-permute-done((bf16[560,256]{1,0:T(8,128)(2,1)S(1)}, bf16[560,256]{1,0:T(8,128)(2,1)S(1)}, u32[]{:S(2)}, u32[]{:S(2)}) %collective-permute-start.18) | collective-permute-done | bytes 286752 | tf_op jit(solution)/shard_map/ppermute | solution.py:1201
  537.7 12.3 %collective-permute-done.19.refs_5_ = bf16[560,256]{1,0:T(8,128)(2,1)S(1)} collective-permute-done((bf16[560,256]{1,0:T(8,128)(2,1)S(1)}, bf16[560,256]{1,0:T(8,128)(2,1)S(1)}, u32[]{:S(2)}, u32[]{:S(2)}) %collective-permute-start.19) | collective-permute-done | bytes 286752 | tf_op jit(solution)/shard_map/ppermute | solution.py:1201
  550.7 5.5 shard_map.329
  (125 shorter events, 67.9 us)
Async XLA Ops:
  7.2 198.9 %all-gather.2.cloned.1.call-start = ((), (), s32[]{:S(2)}) async-start(), calls=%async_computation.4 | async-start | bytes 19464192 | tf_op jit(solution)/shard_map/all_gather | solution.py:1341
  10.3 15.5 %collective-permute-start.2 = (bf16[560,256]{1,0:T(8,128)(2,1)}, bf16[560,256]{1,0:T(8,128)(2,1)S(1)}, u32[]{:S(2)}, u32[]{:S(2)}) collective-permute-start(bf16[560,256]{1,0:T(8,128)(2,1)} %shard_map.315), channel_id=1, source_target_pairs={{0,1},{1,0},{2,3},{3,2},{4,5},{5,4},{6,7},{7,6},{8,9},{9,8},{10,11... | collective-permute-start | bytes 860168 | tf_op jit(solution)/shard_map/ppermute | solution.py:1201
  13.3 23.1 %collective-permute-start.1 = (bf16[560,256]{1,0:T(8,128)(2,1)}, bf16[560,256]{1,0:T(8,128)(2,1)S(1)}, u32[]{:S(2)}, u32[]{:S(2)}) collective-permute-start(bf16[560,256]{1,0:T(8,128)(2,1)} %shard_map.315), channel_id=1, source_target_pairs={{0,2},{1,3},{2,0},{3,1},{4,6},{5,7},{6,4},{7,5},{8,10},{9,11},{10,... | collective-permute-start | bytes 860168 | tf_op jit(solution)/shard_map/ppermute | solution.py:1201
  15.9 20.5 %collective-permute-start = (bf16[560,256]{1,0:T(8,128)(2,1)}, bf16[560,256]{1,0:T(8,128)(2,1)S(1)}, u32[]{:S(2)}, u32[]{:S(2)}) collective-permute-start(bf16[560,256]{1,0:T(8,128)(2,1)} %shard_map.315), channel_id=1, source_target_pairs={{0,3},{1,2},{2,1},{3,0},{4,7},{5,6},{6,5},{7,4},{8,11},{9,10},{10,... | collective-permute-start | bytes 860168 | tf_op jit(solution)/shard_map/ppermute | solution.py:1201
  38.4 72.7 %all-to-all-start = ((bf16[4,1024,256]{2,1,0:T(8,128)(2,1)}), bf16[4,1024,256]{2,1,0:T(8,128)(2,1)S(1)}, u32[]{:S(2)}, u32[]{:S(2)}) async-start(bf16[4,1024,256]{2,1,0:T(8,128)(2,1)} %param.20), calls=%async_computation | async-start | bytes 4194304 | tf_op jit(solution)/shard_map/all_to_all | solution.py:1334
  46.1 510.1 %reduce-scatter.2.cloned.1.call-start = ((), (), s32[]{:S(2)}) async-start(), calls=%async_computation.5 | async-start | bytes 19464192 | tf_op jit(solution)/shard_map/reduce_scatter | solution.py:1542
  46.1 17.6 %collective-permute-start.5 = (bf16[2,560,256]{2,1,0:T(8,128)(2,1)S(1)}, bf16[2,560,256]{2,1,0:T(8,128)(2,1)S(1)}, u32[]{:S(2)}, u32[]{:S(2)}) collective-permute-start(bf16[2,560,256]{2,1,0:T(8,128)(2,1)S(1)} %get-tuple-element.92), channel_id=1, source_target_pairs={{0,16},{8,24},{16,0},{24,8},{1,17},{9,25},{17,1},{25,9},{2,18},{10... | collective-permute-start | bytes 1720328 | tf_op jit(solution)/shard_map/ppermute | solution.py:1201
  47.6 19.8 %collective-permute-start.3 = (bf16[2,560,256]{2,1,0:T(8,128)(2,1)}, bf16[2,560,256]{2,1,0:T(8,128)(2,1)}, u32[]{:S(2)}, u32[]{:S(2)}) collective-permute-start(bf16[2,560,256]{2,1,0:T(8,128)(2,1)} %get-tuple-element.91), channel_id=1, source_target_pairs={{0,8},{8,0},{16,24},{24,16},{1,9},{9,1},{17,25},{25,17},{2,10},{10... | collective-permute-start | bytes 1720328 | tf_op jit(solution)/shard_map/ppermute | solution.py:1201
  63.8 25.9 %collective-permute-start.6 = (bf16[2,2,560,256]{3,2,1,0:T(8,128)(2,1)S(1)}, bf16[2,2,560,256]{3,2,1,0:T(8,128)(2,1)}, u32[]{:S(2)}, u32[]{:S(2)}) collective-permute-start(bf16[2,2,560,256]{3,2,1,0:T(8,128)(2,1)S(1)} %pad_maximum_fusion.1.high_ref), channel_id=1, source_target_pairs={{0,8},{8,0},{16,24},{24,16},{1,9},{9,1},{17,25},{25,17},{2,10},{10... | collective-permute-start | bytes 3440648 | tf_op jit(solution)/shard_map/ppermute | solution.py:1201
  69.8 22.6 %collective-permute-start.4 = (bf16[2,2,560,256]{3,2,1,0:T(8,128)(2,1)}, bf16[2,2,560,256]{3,2,1,0:T(8,128)(2,1)}, u32[]{:S(2)}, u32[]{:S(2)}) collective-permute-start(bf16[2,2,560,256]{3,2,1,0:T(8,128)(2,1)} %pad_maximum_fusion.low_ref), channel_id=1, source_target_pairs={{0,16},{8,24},{16,0},{24,8},{1,17},{9,25},{17,1},{25,9},{2,18},{10... | collective-permute-start | bytes 3440648 | tf_op jit(solution)/shard_map/ppermute | solution.py:1201
  111.2 8.1 %collective-permute-start.7 = (bf16[2,4,2,560,256]{4,3,2,1,0:T(8,128)(2,1)}, bf16[2,4,2,560,256]{4,3,2,1,0:T(8,128)(2,1)}, u32[]{:S(2)}, u32[]{:S(2)}) collective-permute-start(bf16[2,4,2,560,256]{4,3,2,1,0:T(8,128)(2,1)} %shard_map.317.wq_ref.wk_ref.wv_ref.sq_ref.init_ref), channel_id=1, source_target_pairs={{0,4},{4,0},{1,5},{5,1},{2,6},{6,2},{3,7},{7,3},{8,12},{12,8},{9,1... | collective-permute-start | bytes 13762568 | tf_op jit(solution)/shard_map/ppermute | solution.py:1201
  133.4 21.5 %collective-permute-start.8 = (bf16[2,512,1024]{2,1,0:T(8,128)(2,1)}, bf16[2,512,1024]{2,1,0:T(8,128)(2,1)S(1)}, u32[]{:S(2)}, u32[]{:S(2)}) collective-permute-start(bf16[2,512,1024]{2,1,0:T(8,128)(2,1)} %get-tuple-element.98), channel_id=1, source_target_pairs={{0,4},{1,5},{2,6},{3,7},{8,12},{9,13},{10,14},{11,15},{16,20},{17,... | collective-permute-start | bytes 6291464 | tf_op jit(solution)/shard_map/ppermute | solution.py:24
  136.4 20.1 %copy-start.16 = (s32[4]{0:T(128)S(1)}, s32[4]{0:T(128)}, u32[]{:S(2)}) copy-start(s32[4]{0:T(128)} %param.22) | copy-start | bytes 52
  136.4 25.8 %copy-start.13 = (f32[1,1024]{1,0:T(1,128)S(1)}, f32[1,1024]{1,0:T(1,128)}, u32[]{:S(2)}) copy-start(f32[1,1024]{1,0:T(1,128)} %reshape.202.gate_ref) | copy-start | bytes 12292
  155.0 7.9 %collective-permute-start.9 = (bf16[512,1024]{1,0:T(8,128)(2,1)}, bf16[512,1024]{1,0:T(8,128)(2,1)S(1)}, u32[]{:S(2)}, u32[]{:S(2)}) collective-permute-start(bf16[512,1024]{1,0:T(8,128)(2,1)} %get-tuple-element.102), channel_id=1, source_target_pairs={{0,4},{1,5},{2,6},{3,7},{8,12},{9,13},{10,14},{11,15},{16,20},{17,... | collective-permute-start | bytes 3145736 | tf_op jit(solution)/shard_map/ppermute | solution.py:24
  291.5 87.0 %all-to-all-start.1 = ((bf16[4,1024,256]{2,1,0:T(8,128)(2,1)}), bf16[4,1024,256]{2,1,0:T(8,128)(2,1)S(1)}, u32[]{:S(2)}, u32[]{:S(2)}) async-start(bf16[4,1024,256]{2,1,0:T(8,128)(2,1)} %get-tuple-element.112), calls=%async_computation.2 | async-start | bytes 4194304 | tf_op jit(solution)/shard_map/all_to_all | solution.py:1522
  304.0 74.4 %copy-start.14 = (f32[1,1024]{1,0:T(1,128)S(1)}, f32[1,1024]{1,0:T(1,128)}, u32[]{:S(2)}) copy-start(f32[1,1024]{1,0:T(1,128)} %get-tuple-element.132) | copy-start | bytes 12292
  372.7 14.0 %collective-permute-start.10 = (bf16[512,1024]{1,0:T(8,128)(2,1)}, bf16[512,1024]{1,0:T(8,128)(2,1)S(1)}, u32[]{:S(2)}, u32[]{:S(2)}) collective-permute-start(bf16[512,1024]{1,0:T(8,128)(2,1)} %get-tuple-element.117), channel_id=1, source_target_pairs={{4,0},{5,1},{6,2},{7,3},{12,8},{13,9},{14,10},{15,11},{20,16},{21,... | collective-permute-start | bytes 3145736 | tf_op jit(solution)/shard_map/ppermute | solution.py:24
  374.0 14.3 %collective-permute-start.11 = (bf16[512,1024]{1,0:T(8,128)(2,1)}, bf16[512,1024]{1,0:T(8,128)(2,1)}, u32[]{:S(2)}, u32[]{:S(2)}) collective-permute-start(bf16[512,1024]{1,0:T(8,128)(2,1)} %get-tuple-element.122), channel_id=1, source_target_pairs={{4,0},{5,1},{6,2},{7,3},{12,8},{13,9},{14,10},{15,11},{20,16},{21,... | collective-permute-start | bytes 3145736 | tf_op jit(solution)/shard_map/ppermute | solution.py:24
  375.3 15.2 %collective-permute-start.12 = (bf16[512,1024]{1,0:T(8,128)(2,1)}, bf16[512,1024]{1,0:T(8,128)(2,1)}, u32[]{:S(2)}, u32[]{:S(2)}) collective-permute-start(bf16[512,1024]{1,0:T(8,128)(2,1)} %get-tuple-element.123), channel_id=1, source_target_pairs={{4,0},{5,1},{6,2},{7,3},{12,8},{13,9},{14,10},{15,11},{20,16},{21,... | collective-permute-start | bytes 3145736 | tf_op jit(solution)/shard_map/ppermute | solution.py:24
  378.5 41.2 %copy-start.2 = (bf16[4,1024,256]{2,1,0:T(8,128)(2,1)}, bf16[4,1024,256]{2,1,0:T(8,128)(2,1)S(1)}, u32[]{:S(2)}) copy-start(bf16[4,1024,256]{2,1,0:T(8,128)(2,1)S(1)} %all-to-all-done.1.refs_1_) | copy-start | bytes 6291460
  438.3 24.2 %collective-permute-start.13 = (bf16[4,4,560,256]{3,2,1,0:T(8,128)(2,1)}, bf16[4,4,560,256]{3,2,1,0:T(8,128)(2,1)}, u32[]{:S(2)}, u32[]{:S(2)}) collective-permute-start(bf16[4,4,560,256]{3,2,1,0:T(8,128)(2,1)} %get-tuple-element.195), channel_id=1, source_target_pairs={{0,4},{4,0},{1,5},{5,1},{2,6},{6,2},{3,7},{7,3},{8,12},{12,8},{9,1... | collective-permute-start | bytes 13762568 | tf_op jit(solution)/shard_map/ppermute | solution.py:1201
  454.4 77.1 %all-to-all-start.2 = ((bf16[4,1024,256]{2,1,0:T(8,128)(2,1)}), bf16[4,1024,256]{2,1,0:T(8,128)(2,1)S(1)}, u32[]{:S(2)}, u32[]{:S(2)}) async-start(bf16[4,1024,256]{2,1,0:T(8,128)(2,1)} %shard_map.327), calls=%async_computation.3 | async-start | bytes 4194304 | tf_op jit(solution)/shard_map/all_to_all | solution.py:1628
  465.7 32.2 %collective-permute-start.16 = (bf16[2,2,560,256]{3,2,0,1:T(8,128)(2,1)S(1)}, bf16[2,2,560,256]{3,2,0,1:T(8,128)(2,1)S(1)}, u32[]{:S(2)}, u32[]{:S(2)}) collective-permute-start(bf16[2,2,560,256]{3,2,0,1:T(8,128)(2,1)S(1)} %fusion.5), channel_id=1, source_target_pairs={{0,16},{8,24},{16,0},{24,8},{1,17},{9,25},{17,1},{25,9},{2,18},{10... | collective-permute-start | bytes 3440648 | tf_op jit(solution)/shard_map/ppermute | solution.py:1201
  467.6 32.9 %collective-permute-start.14 = (bf16[2,2,560,256]{3,2,0,1:T(8,128)(2,1)S(1)}, bf16[2,2,560,256]{3,2,0,1:T(8,128)(2,1)S(1)}, u32[]{:S(2)}, u32[]{:S(2)}) collective-permute-start(bf16[2,2,560,256]{3,2,0,1:T(8,128)(2,1)S(1)} %fusion.3), channel_id=1, source_target_pairs={{0,8},{8,0},{16,24},{24,16},{1,9},{9,1},{17,25},{25,17},{2,10},{10... | collective-permute-start | bytes 3440648 | tf_op jit(solution)/shard_map/ppermute | solution.py:1201
  499.2 17.4 %collective-permute-start.17 = (bf16[2,560,256]{2,1,0:T(8,128)(2,1)}, bf16[2,560,256]{2,1,0:T(8,128)(2,1)}, u32[]{:S(2)}, u32[]{:S(2)}) collective-permute-start(bf16[2,560,256]{2,1,0:T(8,128)(2,1)} %dynamic-slice_bitcast_fusion), channel_id=1, source_target_pairs={{0,8},{8,0},{16,24},{24,16},{1,9},{9,1},{17,25},{25,17},{2,10},{10... | collective-permute-start | bytes 1720328 | tf_op jit(solution)/shard_map/ppermute | solution.py:1201
  502.7 15.0 %collective-permute-start.15 = (bf16[2,560,256]{2,1,0:T(8,128)(2,1)}, bf16[2,560,256]{2,1,0:T(8,128)(2,1)}, u32[]{:S(2)}, u32[]{:S(2)}) collective-permute-start(bf16[2,560,256]{2,1,0:T(8,128)(2,1)} %dynamic-slice_bitcast_fusion.1), channel_id=1, source_target_pairs={{0,16},{8,24},{16,0},{24,8},{1,17},{9,25},{17,1},{25,9},{2,18},{10... | collective-permute-start | bytes 1720328 | tf_op jit(solution)/shard_map/ppermute | solution.py:1201
  520.2 11.8 %collective-permute-start.20 = (bf16[560,256]{1,0:T(8,128)(2,1)}, bf16[560,256]{1,0:T(8,128)(2,1)S(1)}, u32[]{:S(2)}, u32[]{:S(2)}) collective-permute-start(bf16[560,256]{1,0:T(8,128)(2,1)} %get-tuple-element.180), channel_id=1, source_target_pairs={{0,3},{1,2},{2,1},{3,0},{4,7},{5,6},{6,5},{7,4},{8,11},{9,10},{10,... | collective-permute-start | bytes 860168 | tf_op jit(solution)/shard_map/ppermute | solution.py:1201
  523.5 14.1 %collective-permute-start.18 = (bf16[560,256]{1,0:T(8,128)(2,1)S(1)}, bf16[560,256]{1,0:T(8,128)(2,1)S(1)}, u32[]{:S(2)}, u32[]{:S(2)}) collective-permute-start(bf16[560,256]{1,0:T(8,128)(2,1)S(1)} %get-tuple-element.182), channel_id=1, source_target_pairs={{0,1},{1,0},{2,3},{3,2},{4,5},{5,4},{6,7},{7,6},{8,9},{9,8},{10,11... | collective-permute-start | bytes 860168 | tf_op jit(solution)/shard_map/ppermute | solution.py:1201
  523.5 26.5 %collective-permute-start.19 = (bf16[560,256]{1,0:T(8,128)(2,1)S(1)}, bf16[560,256]{1,0:T(8,128)(2,1)S(1)}, u32[]{:S(2)}, u32[]{:S(2)}) collective-permute-start(bf16[560,256]{1,0:T(8,128)(2,1)S(1)} %get-tuple-element.183), channel_id=1, source_target_pairs={{0,2},{1,3},{2,0},{3,1},{4,6},{5,7},{6,4},{7,5},{8,10},{9,11},{10,... | collective-permute-start | bytes 860168 | tf_op jit(solution)/shard_map/ppermute | solution.py:1201
  531.5 18.5 %copy-start.3 = (bf16[4,1024,256]{2,1,0:T(8,128)(2,1)}, bf16[4,1024,256]{2,1,0:T(8,128)(2,1)S(1)}, u32[]{:S(2)}) copy-start(bf16[4,1024,256]{2,1,0:T(8,128)(2,1)S(1)} %all-to-all-done.2.refs_2_) | copy-start | bytes 6291460
  532.0 18.0 %copy-start.10 = (bf16[560,256]{1,0:T(8,128)(2,1)}, bf16[560,256]{1,0:T(8,128)(2,1)S(1)}, u32[]{:S(2)}) copy-start(bf16[560,256]{1,0:T(8,128)(2,1)S(1)} %collective-permute-done.20.refs_6_) | copy-start | bytes 860164
  (11 other events, 79.1 us)
Sparse Core Ops, SparseCore 0:
  38.6 156.6 all-gather.1
  291.6 230.9 reduce-scatter.1

commit v6 on v5

--- a/solution.py
+++ b/solution.py
@@ -975,7 +975,9 @@
     packed_ref[:, 2 * hidden :] = out_ref[...].T
 
 
-def unpack_kernel(packed_ref, up_ref, down_ref, out_ref):
+def unpack_kernel(packed_ref, from_a, from_b, up_ref, down_ref, out_ref, to_a, to_b):
+    to_a[...] = from_a[...]
+    to_b[...] = from_b[...]
     hidden = up_ref.shape[1]
     up_ref[...] = packed_ref[:, :hidden].astype(F32)
     down_ref[...] = packed_ref[:, hidden : 2 * hidden].astype(F32).T
@@ -984,9 +986,7 @@
 
 def finish_kernel(*refs):
     place_ref, refs = refs[0], refs[1:]
-    for from_ref, to_ref in zip(refs[:2], refs[-3:-1]):
-        to_ref[...] = from_ref[...]
-    terms, outs = refs[2:-14], refs[-14:-3]
+    terms, outs = refs[:-12], refs[-12:-1]
     sum_ref = refs[-1]
     total = terms[0][...].astype(F32)
     for term in terms[1:]:
@@ -1636,6 +1636,17 @@
     grad_own = lax.dynamic_update_slice(grad_own, vector_rows, (0, 0, at_vectors, 0))
     grad_other = lax.dynamic_update_slice(grad_other, vector_rows, (0, 0, at_vectors, 0))
     terms = scatter_pairs(grad_own, grad_other)
+    activation = jax.ShapeDtypeStruct(output.shape, BF)
+    late_parts = pl.pallas_call(
+        unpack_kernel,
+        out_shape=[
+            jax.ShapeDtypeStruct(w_up.shape, F32), jax.ShapeDtypeStruct(w_down.shape, F32),
+            jax.ShapeDtypeStruct(w_out.shape, F32), activation, activation,
+        ],
+        compiler_params=params(),
+    )(late_grad, output, token_grad)
+    terms, late_parts = lax.optimization_barrier((terms, late_parts))
+    up_grad, down_grad, out_grad, output, token_grad = late_parts
     parts = (
         w_query, w_key, w_value, state_query, state_init, state_key, state_value,
         gain_attn, gain_mlp, gate_bias, bias_table,
@@ -1643,23 +1654,14 @@
     sums = call(
         finish_kernel,
         (1,),
-        [whole(output.shape)] * 2 + [whole((full_rows, shard_width))] * shards,
-        [whole(item.shape) for item in parts] + [whole(output.shape)] * 2,
-        [jax.ShapeDtypeStruct(item.shape, F32) for item in parts]
-        + [jax.ShapeDtypeStruct(output.shape, BF)] * 2,
+        [whole((full_rows, shard_width))] * shards,
+        [whole(item.shape) for item in parts],
+        [jax.ShapeDtypeStruct(item.shape, F32) for item in parts],
         [pltpu.VMEM((16, shard_width), F32)],
-    )(place, output, token_grad, *terms)
-    late_grad, sums = lax.optimization_barrier((late_grad, sums))
-    up_grad, down_grad, out_grad = pl.pallas_call(
-        unpack_kernel,
-        out_shape=[
-            jax.ShapeDtypeStruct(w_up.shape, F32), jax.ShapeDtypeStruct(w_down.shape, F32),
-            jax.ShapeDtypeStruct(w_out.shape, F32),
-        ],
-    )(late_grad)
+    )(place, *terms)
     return (
-        sums[11].reshape(seq_count, length, shard_width),
-        sums[12].reshape(seq_count, length, shard_width),
+        output.reshape(seq_count, length, shard_width),
+        token_grad.reshape(seq_count, length, shard_width),
         *sums[:3],
         out_grad,
         up_grad,

time: 572 us -> 567 us (level)
  waiting for transfers between devices: 158 us -> 151 us
    all_to_all x1, waiting for transfers between devices: 6.89 us -> 0.92 us  [sequence_body(): token_grad = lax.all_to_all(token_grad, 'tp', 0, 0, tiled=True)]
  transfers between devices with their start and end apart: 26 -> 26, of which waited for: 17 -> 15; matrix products, arithmetic and copies ran while one was open for 5% -> 5% of each run, Pallas kernels for 39% -> 39%
where the time goes in v6:
time: 567 us; the launch traced here: 558 us
  Pallas kernels  310 us (55%)
  waiting for transfers between devices  151 us (27%)
  starting transfers between devices  44.9 us (8%)
  local copies, waits for them, and re-layouts  17.8 us (3%)
  other arithmetic  15.5 us (3%)
  between operations  14.7 us (3%)
    ppermute x16, waiting for transfers between devices, across(): lax.ppermute(value, axis, [(source, source ^ bit) for source in range(cou...  123 us
    pallas_call x1, Pallas kernels, sequence_body(): call(functools.partial(attend_back_kernel, blocks=blocks), (heads, units)...  68.7 us
    pallas_call x1, Pallas kernels, sequence_body(): call(mlp_kernel, (shards * per_shard, 2), [whole((rows, width)), pl.Block...  68.6 us
    pallas_call x1, Pallas kernels, sequence_body(): call(functools.partial(attend_kernel, blocks=blocks), (heads, units), att...  42.1 us
    pallas_call x1, Pallas kernels, sequence_body(): call(functools.partial(read_back_kernel, blocks=blocks), (heads, units),...  29.2 us
    ppermute x16, starting transfers between devices, across(): lax.ppermute(value, axis, [(source, source ^ bit) for source in range(cou...  22.2 us
    pallas_call x1, Pallas kernels, sequence_body(): call(functools.partial(read_kernel, blocks=blocks), (heads, units), query...  18.4 us
    pallas_call x1, Pallas kernels, sequence_body(): call(weight_back_kernel, (shards,), [token_shards, whole((1, width)), col...  16.4 us
  transfers between devices with their start and end apart: 26, of which 15 were waited for; matrix products, arithmetic and copies ran while one was open for 5% of the time, Pallas kernels for 39%

profile of v6, /device:TPU:0, one launch (start us, length us, event | category | flops | bytes accessed | tf_op | source)
XLA Modules:
  0.0 558.0 jit_solution(507780515082812061)
XLA Ops:
  10.3 5.1 collective-permute-start
  17.9 5.5 collective-permute-done
  23.4 16.6 %collective-permute-done.1 = bf16[560,256]{1,0:T(8,128)(2,1)S(1)} collective-permute-done((bf16[560,256]{1,0:T(8,128)(2,1)}, bf16[560,256]{1,0:T(8,128)(2,1)S(1)}, u32[]{:S(2)}, u32[]{:S(2)}) %collective-permute-start.1) | collective-permute-done | bytes 286752 | tf_op jit(solution)/shard_map/ppermute | solution.py:1201
  42.0 3.8 all-to-all-start
  48.8 15.2 %collective-permute-done.5 = bf16[2,560,256]{2,1,0:T(8,128)(2,1)S(1)} collective-permute-done((bf16[2,560,256]{2,1,0:T(8,128)(2,1)S(1)}, bf16[2,560,256]{2,1,0:T(8,128)(2,1)S(1)}, u32[]{:S(2)}, u32[]{:S(2)}) %collective-permute-start.5) | collective-permute-done | bytes 573472 | tf_op jit(solution)/shard_map/ppermute | solution.py:1201
  70.4 19.7 %collective-permute-done.6.highx_ref = bf16[2,2,560,256]{3,2,1,0:T(8,128)(2,1)} collective-permute-done((bf16[2,2,560,256]{3,2,1,0:T(8,128)(2,1)S(1)}, bf16[2,2,560,256]{3,2,1,0:T(8,128)(2,1)}, u32[]{:S(2)}, u32[]{:S(2)}) %collective-permute-start.6) | collective-permute-done | bytes 1146912 | tf_op jit(solution)/shard_map/ppermute | solution.py:1201
  90.1 3.6 collective-permute-done.4.lowy_ref
  93.8 4.5 shard_map.317.wq_ref.wk_ref.wv_ref.sq_ref.init_ref
  98.3 14.7 %all-to-all-done.tok_ref = bf16[4,1024,256]{2,1,0:T(8,128)(2,1)S(1)} async-done(((bf16[4,1024,256]{2,1,0:T(8,128)(2,1)}), bf16[4,1024,256]{2,1,0:T(8,128)(2,1)S(1)}, u32[]{:S(2)}, u32[]{:S(2)}) %all-to-all-start) | async-done | bytes 2097184 | tf_op jit(solution)/shard_map/all_to_all | solution.py:1334
  113.0 8.1 %collective-permute-done.7.wqo_ref.wko_ref.wvo_ref.sqo_ref.inito_ref = bf16[2,4,2,560,256]{4,3,2,1,0:T(8,128)(2,1)} collective-permute-done((bf16[2,4,2,560,256]{4,3,2,1,0:T(8,128)(2,1)}, bf16[2,4,2,560,256]{4,3,2,1,0:T(8,128)(2,1)}, u32[]{:S(2)}, u32[]{:S(2)}) %collective-permute-start.7) | collective-permute-done | bytes 4587552 | tf_op jit(solution)/shard_map/ppermute | solution.py:1201
  122.8 12.4 %shard_map.318 = (bf16[1024,1024]{1,0:T(8,128)(2,1)}, bf16[1024,1024]{1,0:T(8,128)(2,1)}, bf16[1024,1024]{1,0:T(8,128)(2,1)}, bf16[1024,1024]{1,0:T(8,128)(2,1)}, bf16[2,512,1024]{2,1,0:T(8,128)(2,1)}) custom-call(s32[5]{0:T(128)} %stack.72.place_ref.refs_0_, bf16[4,1024,256]{2,1,0:T(8,128)(2,1)} %copy-done, f32[1,1024]{1,0:T(1,128)} %reshape.200.gain_ref, ...), custom_call_target="tpu_custom_call" | custom-call | tf_op jit(solution)/shard_map/pallas_call | solution.py:1381
  138.2 18.4 %shard_map.319 = (f32[1024,1024]{1,0:T(8,128)}, bf16[512,1024]{1,0:T(8,128)(2,1)}) custom-call(s32[5]{0:T(128)} %stack.72.place_ref.refs_0_, bf16[2,4,2,560,256]{4,3,2,1,0:T(8,128)(2,1)} %shard_map.317.wq_ref.wk_ref.wv_ref.sq_ref.init_ref, bf16[2,4,2,560,256]{4,3,2,1,0:T(8,128)(2,1)} %collective-permute-done.7.wqo_ref.wko_ref.wvo_ref.sqo_ref.inito_ref, ...), custom_call_target="tpu_custom_call" | custom-call | tf_op jit(solution)/shard_map/pallas_call | solution.py:1410
  165.5 42.1 %shard_map.320 = (bf16[1024,1024]{1,0:T(8,128)(2,1)}, f32[2,8,1,512]{3,2,1,0:T(1,128)}, bf16[1024,1024]{1,0:T(8,128)(2,1)}, bf16[1024,1024]{1,0:T(8,128)(2,1)}) custom-call(s32[5]{0:T(128)} %stack.72.place_ref.refs_0_, s32[2,2]{1,0:T(2,128)} %add_bitcast_fusion.info_ref, bf16[1024,1024]{1,0:T(8,128)(2,1)} %get-tuple-element.90.q_ref, ...), custom_call_target="tpu_custom_call" | custom-call | tf_op jit(solution)/shard_map/pallas_call | solution.py:1466
  207.7 10.0 %shard_map.321 = (f32[1024,1024]{1,0:T(8,128)}, bf16[1024,1024]{1,0:T(8,128)(2,1)}) custom-call(bf16[1024,1024]{1,0:T(8,128)(2,1)} %get-tuple-element.99.att_ref.o_ref, bf16[4,8,128,2304]{3,2,1,0:T(8,128)(2,1)} %bitcast.84, bf16[4,1024,256]{2,1,0:T(8,128)(2,1)} %copy-done, f32[1,1024]{1,0:T(1,128)} %reshape.203.gain_ref), custom_call_target="tpu_custom_call" | custom-call | tf_op jit(solution)/shard_map/pallas_call | solution.py:1480
  217.7 68.6 %shard_map.322 = (bf16[4,1024,256]{2,1,0:T(8,128)(2,1)}, bf16[1024,1024]{1,0:T(8,128)(2,1)}, f32[1,1024]{1,0:T(1,128)}, bf16[4,8,128,2304]{3,2,1,0:T(8,128)(2,1)}) custom-call(s32[5]{0:T(128)} %stack.72.place_ref.refs_0_, bf16[1024,1024]{1,0:T(8,128)(2,1)} %get-tuple-element.101.min_ref, bf16[4096,1024]{1,0:T(8,128)(2,1)} %bitcast.93, ...), custom_call_target="tpu_custom_call" | custom-call | tf_op jit(solution)/shard_map/pallas_call | solution.py:1492
  286.3 6.7 %shard_map.327 = bf16[4,8,128,2304]{3,2,1,0:T(8,128)(2,1)} custom-call(bf16[1024,1024]{1,0:T(8,128)(2,1)} %get-tuple-element.103.gmid_ref, bf16[1024,1024]{1,0:T(8,128)(2,1)} %get-tuple-element.99.att_ref.o_ref, bf16[4,8,128,2304]{3,2,1,0:T(8,128)(2,1)} %get-tuple-element.129.late_ref), custom_call_target="tpu_custom_call", output_to_operand_aliasing={{}: (2, {})} | custom-call | tf_op jit(solution)/shard_map/pallas_call | solution.py:1524
  293.1 6.2 %all-to-all-start.1 = ((bf16[4,1024,256]{2,1,0:T(8,128)(2,1)}), bf16[4,1024,256]{2,1,0:T(8,128)(2,1)S(1)}, u32[]{:S(2)}, u32[]{:S(2)}) async-start(bf16[4,1024,256]{2,1,0:T(8,128)(2,1)} %get-tuple-element.110), calls=%async_computation.1 | async-start | bytes 4194304 | tf_op jit(solution)/shard_map/all_to_all | solution.py:1522
  300.7 6.5 %shard_map.323.do_ref = bf16[1024,1024]{1,0:T(8,128)(2,1)} custom-call(bf16[1024,1024]{1,0:T(8,128)(2,1)} %get-tuple-element.103.gmid_ref, bf16[4,8,128,2304]{3,2,1,0:T(8,128)(2,1)} %bitcast.87), custom_call_target="tpu_custom_call" | custom-call | tf_op jit(solution)/shard_map/pallas_call | solution.py:1534
  307.2 68.7 %shard_map.324 = (bf16[1024,1024]{1,0:T(8,128)(2,1)}, f32[1024,1024]{1,0:T(8,128)}, f32[1024,1024]{1,0:T(8,128)}, bf16[1024,1024]{1,0:T(8,128)(2,1)}, bf16[1024,...) custom-call(s32[5]{0:T(128)} %stack.72.place_ref.refs_0_, ...), custom_call_target="tpu_custom_call" | custom-call | tf_op jit(solution)/shard_map/pallas_call | solution.py:1555
  381.8 7.8 %collective-permute-done.10.later_ref = bf16[512,1024]{1,0:T(8,128)(2,1)S(1)} collective-permute-done((bf16[512,1024]{1,0:T(8,128)(2,1)}, bf16[512,1024]{1,0:T(8,128)(2,1)S(1)}, u32[]{:S(2)}, u32[]{:S(2)}) %collective-permute-start.10) | collective-permute-done | bytes 1048608 | tf_op jit(solution)/shard_map/ppermute | solution.py:24
  393.3 29.2 %shard_map.325 = (bf16[1024,1024]{1,0:T(8,128)(2,1)}, bf16[1024,1024]{1,0:T(8,128)(2,1)}, f32[512,1024]{1,0:T(8,128)}, f32[512,1024]{1,0:T(8,128)}, f32[8,1,128]{2,1,0:T(1,128)}) custom-call(s32[5]{0:T(128)} %stack.72.place_ref.refs_0_, bf16[2,4,2,560,256]{4,3,2,1,0:T(8,128)(2,1)} %shard_map.317.wq_ref.wk_ref.wv_ref.sq_ref.init_ref, ...), custom_call_target="tpu_custom_call" | custom-call | tf_op jit(solution)/shard_map/pallas_call | solution.py:1583
  422.6 16.4 %shard_map.326 = (bf16[4,4,560,256]{3,2,1,0:T(8,128)(2,1)}, bf16[4,4,560,256]{3,2,1,0:T(8,128)(2,1)}, f32[1024,1]{1,0:T(8,128)}) custom-call(s32[5]{0:T(128)} %stack.72.place_ref.refs_0_, bf16[4,1024,256]{2,1,0:T(8,128)(2,1)} %copy-done, f32[1,1024]{1,0:T(1,128)} %reshape.200.gain_ref, bf16[1024,1024]{1,0:T(8,128)(2,1)} %get-tuple-element.105.gq_ref, ...), custom_call_target="tpu_custom_call" | custom-call | tf_op jit(solution)/shard_map/pallas_call | solution.py:1604
  442.3 14.9 %shard_map.328 = bf16[4,1024,256]{2,1,0:T(8,128)(2,1)} custom-call(s32[5]{0:T(128)} %stack.72.place_ref.refs_0_, bf16[4,1024,256]{2,1,0:T(8,128)(2,1)} %copy-done, bf16[1024,1024]{1,0:T(8,128)(2,1)} %get-tuple-element.103.gmid_ref, f32[1,1024]{1,0:T(1,128)} %reshape.200.gain_ref, bf16[1024,1024]{1,0:T(8,128)(2,1)} %get-tuple-element.105.gq_ref, ...), custom_call_target="tpu_custom_call" | custom-call | tf_op jit(solution)/shard_map/pallas_call | solution.py:1620
  457.2 5.1 all-to-all-start.2
  462.3 2.7 fusion.40
  465.3 2.7 fusion.41
  471.9 28.8 %collective-permute-done.16 = bf16[2,2,560,256]{3,2,0,1:T(8,128)(2,1)S(1)} collective-permute-done((bf16[2,2,560,256]{3,2,0,1:T(8,128)(2,1)S(1)}, bf16[2,2,560,256]{3,2,0,1:T(8,128)(2,1)S(1)}, u32[]{:S(2)}, u32[]{:S(2)}) %collective-permute-start.16) | collective-permute-done | bytes 1146912 | tf_op jit(solution)/shard_map/ppermute | solution.py:1201
  506.2 12.9 %collective-permute-done.17 = bf16[2,560,256]{2,1,0:T(8,128)(2,1)} collective-permute-done((bf16[2,560,256]{2,1,0:T(8,128)(2,1)}, bf16[2,560,256]{2,1,0:T(8,128)(2,1)}, u32[]{:S(2)}, u32[]{:S(2)}) %collective-permute-start.17) | collective-permute-done | bytes 573472 | tf_op jit(solution)/shard_map/ppermute | solution.py:1201
  529.5 5.0 shard_map.329
  534.5 6.4 %collective-permute-done.18.refs_2_ = bf16[560,256]{1,0:T(8,128)(2,1)S(1)} collective-permute-done((bf16[560,256]{1,0:T(8,128)(2,1)}, bf16[560,256]{1,0:T(8,128)(2,1)S(1)}, u32[]{:S(2)}, u32[]{:S(2)}) %collective-permute-start.18) | collective-permute-done | bytes 286752 | tf_op jit(solution)/shard_map/ppermute | solution.py:1201
  540.9 6.4 %collective-permute-done.19.refs_3_ = bf16[560,256]{1,0:T(8,128)(2,1)S(1)} collective-permute-done((bf16[560,256]{1,0:T(8,128)(2,1)S(1)}, bf16[560,256]{1,0:T(8,128)(2,1)S(1)}, u32[]{:S(2)}, u32[]{:S(2)}) %collective-permute-start.19) | collective-permute-done | bytes 286752 | tf_op jit(solution)/shard_map/ppermute | solution.py:1201
  548.1 2.8 shard_map.330
  (125 shorter events, 65.7 us)
Async XLA Ops:
  7.2 200.5 %all-gather.2.cloned.1.call-start = ((), (), s32[]{:S(2)}) async-start(), calls=%async_computation.4 | async-start | bytes 19464192 | tf_op jit(solution)/shard_map/all_gather | solution.py:1341
  10.3 13.1 %collective-permute-start = (bf16[560,256]{1,0:T(8,128)(2,1)}, bf16[560,256]{1,0:T(8,128)(2,1)S(1)}, u32[]{:S(2)}, u32[]{:S(2)}) collective-permute-start(bf16[560,256]{1,0:T(8,128)(2,1)} %shard_map.315), channel_id=1, source_target_pairs={{0,3},{1,2},{2,1},{3,0},{4,7},{5,6},{6,5},{7,4},{8,11},{9,10},{10,... | collective-permute-start | bytes 860168 | tf_op jit(solution)/shard_map/ppermute | solution.py:1201
  15.4 24.6 %collective-permute-start.1 = (bf16[560,256]{1,0:T(8,128)(2,1)}, bf16[560,256]{1,0:T(8,128)(2,1)S(1)}, u32[]{:S(2)}, u32[]{:S(2)}) collective-permute-start(bf16[560,256]{1,0:T(8,128)(2,1)} %shard_map.315), channel_id=1, source_target_pairs={{0,2},{1,3},{2,0},{3,1},{4,6},{5,7},{6,4},{7,5},{8,10},{9,11},{10,... | collective-permute-start | bytes 860168 | tf_op jit(solution)/shard_map/ppermute | solution.py:1201
  15.4 24.6 %collective-permute-start.2 = (bf16[560,256]{1,0:T(8,128)(2,1)}, bf16[560,256]{1,0:T(8,128)(2,1)S(1)}, u32[]{:S(2)}, u32[]{:S(2)}) collective-permute-start(bf16[560,256]{1,0:T(8,128)(2,1)} %shard_map.315), channel_id=1, source_target_pairs={{0,1},{1,0},{2,3},{3,2},{4,5},{5,4},{6,7},{7,6},{8,9},{9,8},{10,11... | collective-permute-start | bytes 860168 | tf_op jit(solution)/shard_map/ppermute | solution.py:1201
  42.0 71.0 %all-to-all-start = ((bf16[4,1024,256]{2,1,0:T(8,128)(2,1)}), bf16[4,1024,256]{2,1,0:T(8,128)(2,1)S(1)}, u32[]{:S(2)}, u32[]{:S(2)}) async-start(bf16[4,1024,256]{2,1,0:T(8,128)(2,1)} %param.20), calls=%async_computation | async-start | bytes 4194304 | tf_op jit(solution)/shard_map/all_to_all | solution.py:1334
  45.7 482.5 %reduce-scatter.2.cloned.1.call-start = ((), (), s32[]{:S(2)}) async-start(), calls=%async_computation.5 | async-start | bytes 19464192 | tf_op jit(solution)/shard_map/reduce_scatter | solution.py:1542
  45.7 18.2 %collective-permute-start.5 = (bf16[2,560,256]{2,1,0:T(8,128)(2,1)S(1)}, bf16[2,560,256]{2,1,0:T(8,128)(2,1)S(1)}, u32[]{:S(2)}, u32[]{:S(2)}) collective-permute-start(bf16[2,560,256]{2,1,0:T(8,128)(2,1)S(1)} %get-tuple-element.87), channel_id=1, source_target_pairs={{0,16},{8,24},{16,0},{24,8},{1,17},{9,25},{17,1},{25,9},{2,18},{10... | collective-permute-start | bytes 1720328 | tf_op jit(solution)/shard_map/ppermute | solution.py:1201
  47.3 18.5 %collective-permute-start.3 = (bf16[2,560,256]{2,1,0:T(8,128)(2,1)}, bf16[2,560,256]{2,1,0:T(8,128)(2,1)}, u32[]{:S(2)}, u32[]{:S(2)}) collective-permute-start(bf16[2,560,256]{2,1,0:T(8,128)(2,1)} %get-tuple-element.86), channel_id=1, source_target_pairs={{0,8},{8,0},{16,24},{24,16},{1,9},{9,1},{17,25},{25,17},{2,10},{10... | collective-permute-start | bytes 1720328 | tf_op jit(solution)/shard_map/ppermute | solution.py:1201
  64.2 25.9 %collective-permute-start.6 = (bf16[2,2,560,256]{3,2,1,0:T(8,128)(2,1)S(1)}, bf16[2,2,560,256]{3,2,1,0:T(8,128)(2,1)}, u32[]{:S(2)}, u32[]{:S(2)}) collective-permute-start(bf16[2,2,560,256]{3,2,1,0:T(8,128)(2,1)S(1)} %pad_maximum_fusion.1.high_ref), channel_id=1, source_target_pairs={{0,8},{8,0},{16,24},{24,16},{1,9},{9,1},{17,25},{25,17},{2,10},{10... | collective-permute-start | bytes 3440648 | tf_op jit(solution)/shard_map/ppermute | solution.py:1201
  68.2 25.5 %collective-permute-start.4 = (bf16[2,2,560,256]{3,2,1,0:T(8,128)(2,1)}, bf16[2,2,560,256]{3,2,1,0:T(8,128)(2,1)}, u32[]{:S(2)}, u32[]{:S(2)}) collective-permute-start(bf16[2,2,560,256]{3,2,1,0:T(8,128)(2,1)} %pad_maximum_fusion.low_ref), channel_id=1, source_target_pairs={{0,16},{8,24},{16,0},{24,8},{1,17},{9,25},{17,1},{25,9},{2,18},{10... | collective-permute-start | bytes 3440648 | tf_op jit(solution)/shard_map/ppermute | solution.py:1201
  113.0 8.1 %collective-permute-start.7 = (bf16[2,4,2,560,256]{4,3,2,1,0:T(8,128)(2,1)}, bf16[2,4,2,560,256]{4,3,2,1,0:T(8,128)(2,1)}, u32[]{:S(2)}, u32[]{:S(2)}) collective-permute-start(bf16[2,4,2,560,256]{4,3,2,1,0:T(8,128)(2,1)} %shard_map.317.wq_ref.wk_ref.wv_ref.sq_ref.init_ref), channel_id=1, source_target_pairs={{0,4},{4,0},{1,5},{5,1},{2,6},{6,2},{3,7},{7,3},{8,12},{12,8},{9,1... | collective-permute-start | bytes 13762568 | tf_op jit(solution)/shard_map/ppermute | solution.py:1201
  135.2 21.4 %collective-permute-start.8 = (bf16[2,512,1024]{2,1,0:T(8,128)(2,1)}, bf16[2,512,1024]{2,1,0:T(8,128)(2,1)S(1)}, u32[]{:S(2)}, u32[]{:S(2)}) collective-permute-start(bf16[2,512,1024]{2,1,0:T(8,128)(2,1)} %get-tuple-element.93), channel_id=1, source_target_pairs={{0,4},{1,5},{2,6},{3,7},{8,12},{9,13},{10,14},{11,15},{16,20},{17,... | collective-permute-start | bytes 6291464 | tf_op jit(solution)/shard_map/ppermute | solution.py:24
  138.2 20.0 %copy-start.16 = (s32[4]{0:T(128)S(1)}, s32[4]{0:T(128)}, u32[]{:S(2)}) copy-start(s32[4]{0:T(128)} %param.22) | copy-start | bytes 52
  138.2 25.7 %copy-start.13 = (f32[1,1024]{1,0:T(1,128)S(1)}, f32[1,1024]{1,0:T(1,128)}, u32[]{:S(2)}) copy-start(f32[1,1024]{1,0:T(1,128)} %reshape.202.gate_ref) | copy-start | bytes 12292
  156.6 7.9 %collective-permute-start.9 = (bf16[512,1024]{1,0:T(8,128)(2,1)}, bf16[512,1024]{1,0:T(8,128)(2,1)S(1)}, u32[]{:S(2)}, u32[]{:S(2)}) collective-permute-start(bf16[512,1024]{1,0:T(8,128)(2,1)} %get-tuple-element.97), channel_id=1, source_target_pairs={{0,4},{1,5},{2,6},{3,7},{8,12},{9,13},{10,14},{11,15},{16,20},{17,... | collective-permute-start | bytes 3145736 | tf_op jit(solution)/shard_map/ppermute | solution.py:24
  293.1 88.7 %all-to-all-start.1 = ((bf16[4,1024,256]{2,1,0:T(8,128)(2,1)}), bf16[4,1024,256]{2,1,0:T(8,128)(2,1)S(1)}, u32[]{:S(2)}, u32[]{:S(2)}) async-start(bf16[4,1024,256]{2,1,0:T(8,128)(2,1)} %get-tuple-element.110), calls=%async_computation.1 | async-start | bytes 4194304 | tf_op jit(solution)/shard_map/all_to_all | solution.py:1522
  307.2 74.5 %copy-start.14 = (f32[1,1024]{1,0:T(1,128)S(1)}, f32[1,1024]{1,0:T(1,128)}, u32[]{:S(2)}) copy-start(f32[1,1024]{1,0:T(1,128)} %get-tuple-element.125) | copy-start | bytes 12292
  375.9 13.7 %collective-permute-start.10 = (bf16[512,1024]{1,0:T(8,128)(2,1)}, bf16[512,1024]{1,0:T(8,128)(2,1)S(1)}, u32[]{:S(2)}, u32[]{:S(2)}) collective-permute-start(bf16[512,1024]{1,0:T(8,128)(2,1)} %get-tuple-element.108), channel_id=1, source_target_pairs={{4,0},{5,1},{6,2},{7,3},{12,8},{13,9},{14,10},{15,11},{20,16},{21,... | collective-permute-start | bytes 3145736 | tf_op jit(solution)/shard_map/ppermute | solution.py:24
  377.2 14.0 %collective-permute-start.11 = (bf16[512,1024]{1,0:T(8,128)(2,1)}, bf16[512,1024]{1,0:T(8,128)(2,1)}, u32[]{:S(2)}, u32[]{:S(2)}) collective-permute-start(bf16[512,1024]{1,0:T(8,128)(2,1)} %get-tuple-element.115), channel_id=1, source_target_pairs={{4,0},{5,1},{6,2},{7,3},{12,8},{13,9},{14,10},{15,11},{20,16},{21,... | collective-permute-start | bytes 3145736 | tf_op jit(solution)/shard_map/ppermute | solution.py:24
  378.5 14.9 %collective-permute-start.12 = (bf16[512,1024]{1,0:T(8,128)(2,1)}, bf16[512,1024]{1,0:T(8,128)(2,1)}, u32[]{:S(2)}, u32[]{:S(2)}) collective-permute-start(bf16[512,1024]{1,0:T(8,128)(2,1)} %get-tuple-element.116), channel_id=1, source_target_pairs={{4,0},{5,1},{6,2},{7,3},{12,8},{13,9},{14,10},{15,11},{20,16},{21,... | collective-permute-start | bytes 3145736 | tf_op jit(solution)/shard_map/ppermute | solution.py:24
  381.8 40.8 %copy-start.2 = (bf16[4,1024,256]{2,1,0:T(8,128)(2,1)}, bf16[4,1024,256]{2,1,0:T(8,128)(2,1)S(1)}, u32[]{:S(2)}) copy-start(bf16[4,1024,256]{2,1,0:T(8,128)(2,1)S(1)} %all-to-all-done.1.from_a) | copy-start | bytes 6291460
  422.6 17.7 %copy-start.15 = (f32[8,1,128]{2,1,0:T(1,128)S(1)}, f32[8,1,128]{2,1,0:T(1,128)}, u32[]{:S(2)}) copy-start(f32[8,1,128]{2,1,0:T(1,128)} %get-tuple-element.126) | copy-start | bytes 12292
  441.1 24.2 %collective-permute-start.13 = (bf16[4,4,560,256]{3,2,1,0:T(8,128)(2,1)}, bf16[4,4,560,256]{3,2,1,0:T(8,128)(2,1)}, u32[]{:S(2)}, u32[]{:S(2)}) collective-permute-start(bf16[4,4,560,256]{3,2,1,0:T(8,128)(2,1)} %get-tuple-element.185), channel_id=1, source_target_pairs={{0,4},{4,0},{1,5},{5,1},{2,6},{6,2},{3,7},{7,3},{8,12},{12,8},{9,1... | collective-permute-start | bytes 13762568 | tf_op jit(solution)/shard_map/ppermute | solution.py:1201
  457.2 71.1 %all-to-all-start.2 = ((bf16[4,1024,256]{2,1,0:T(8,128)(2,1)}), bf16[4,1024,256]{2,1,0:T(8,128)(2,1)S(1)}, u32[]{:S(2)}, u32[]{:S(2)}) async-start(bf16[4,1024,256]{2,1,0:T(8,128)(2,1)} %shard_map.328), calls=%async_computation.3 | async-start | bytes 4194304 | tf_op jit(solution)/shard_map/all_to_all | solution.py:1628
  468.5 32.2 %collective-permute-start.16 = (bf16[2,2,560,256]{3,2,0,1:T(8,128)(2,1)S(1)}, bf16[2,2,560,256]{3,2,0,1:T(8,128)(2,1)S(1)}, u32[]{:S(2)}, u32[]{:S(2)}) collective-permute-start(bf16[2,2,560,256]{3,2,0,1:T(8,128)(2,1)S(1)} %fusion.5), channel_id=1, source_target_pairs={{0,16},{8,24},{16,0},{24,8},{1,17},{9,25},{17,1},{25,9},{2,18},{10... | collective-permute-start | bytes 3440648 | tf_op jit(solution)/shard_map/ppermute | solution.py:1201
  470.3 32.9 %collective-permute-start.14 = (bf16[2,2,560,256]{3,2,0,1:T(8,128)(2,1)S(1)}, bf16[2,2,560,256]{3,2,0,1:T(8,128)(2,1)S(1)}, u32[]{:S(2)}, u32[]{:S(2)}) collective-permute-start(bf16[2,2,560,256]{3,2,0,1:T(8,128)(2,1)S(1)} %fusion.3), channel_id=1, source_target_pairs={{0,8},{8,0},{16,24},{24,16},{1,9},{9,1},{17,25},{25,17},{2,10},{10... | collective-permute-start | bytes 3440648 | tf_op jit(solution)/shard_map/ppermute | solution.py:1201
  501.9 17.3 %collective-permute-start.17 = (bf16[2,560,256]{2,1,0:T(8,128)(2,1)}, bf16[2,560,256]{2,1,0:T(8,128)(2,1)}, u32[]{:S(2)}, u32[]{:S(2)}) collective-permute-start(bf16[2,560,256]{2,1,0:T(8,128)(2,1)} %dynamic-slice_bitcast_fusion), channel_id=1, source_target_pairs={{0,8},{8,0},{16,24},{24,16},{1,9},{9,1},{17,25},{25,17},{2,10},{10... | collective-permute-start | bytes 1720328 | tf_op jit(solution)/shard_map/ppermute | solution.py:1201
  505.4 15.0 %collective-permute-start.15 = (bf16[2,560,256]{2,1,0:T(8,128)(2,1)}, bf16[2,560,256]{2,1,0:T(8,128)(2,1)}, u32[]{:S(2)}, u32[]{:S(2)}) collective-permute-start(bf16[2,560,256]{2,1,0:T(8,128)(2,1)} %dynamic-slice_bitcast_fusion.1), channel_id=1, source_target_pairs={{0,16},{8,24},{16,0},{24,8},{1,17},{9,25},{17,1},{25,9},{2,18},{10... | collective-permute-start | bytes 1720328 | tf_op jit(solution)/shard_map/ppermute | solution.py:1201
  506.2 14.2 %copy-start.6 = (bf16[2,2,560,256]{3,2,0,1:T(8,128)(2,1)S(1)}, bf16[2,2,560,256]{3,2,0,1:T(8,128)(2,1)}, u32[]{:S(2)}) copy-start(bf16[2,2,560,256]{3,2,0,1:T(8,128)(2,1)} %copy-done.5) | copy-start | bytes 3440644
  522.9 18.0 %collective-permute-start.18 = (bf16[560,256]{1,0:T(8,128)(2,1)}, bf16[560,256]{1,0:T(8,128)(2,1)S(1)}, u32[]{:S(2)}, u32[]{:S(2)}) collective-permute-start(bf16[560,256]{1,0:T(8,128)(2,1)} %get-tuple-element.172), channel_id=1, source_target_pairs={{0,1},{1,0},{2,3},{3,2},{4,5},{5,4},{6,7},{7,6},{8,9},{9,8},{10,11... | collective-permute-start | bytes 860168 | tf_op jit(solution)/shard_map/ppermute | solution.py:1201
  524.4 22.9 %collective-permute-start.19 = (bf16[560,256]{1,0:T(8,128)(2,1)S(1)}, bf16[560,256]{1,0:T(8,128)(2,1)S(1)}, u32[]{:S(2)}, u32[]{:S(2)}) collective-permute-start(bf16[560,256]{1,0:T(8,128)(2,1)S(1)} %get-tuple-element.173), channel_id=1, source_target_pairs={{0,2},{1,3},{2,0},{3,1},{4,6},{5,7},{6,4},{7,5},{8,10},{9,11},{10,... | collective-permute-start | bytes 860168 | tf_op jit(solution)/shard_map/ppermute | solution.py:1201
  526.8 20.5 %collective-permute-start.20 = (bf16[560,256]{1,0:T(8,128)(2,1)S(1)}, bf16[560,256]{1,0:T(8,128)(2,1)S(1)}, u32[]{:S(2)}, u32[]{:S(2)}) collective-permute-start(bf16[560,256]{1,0:T(8,128)(2,1)S(1)} %get-tuple-element.170), channel_id=1, source_target_pairs={{0,3},{1,2},{2,1},{3,0},{4,7},{5,6},{6,5},{7,4},{8,11},{9,10},{10,... | collective-permute-start | bytes 860168 | tf_op jit(solution)/shard_map/ppermute | solution.py:1201
  (11 other events, 43.0 us)
Sparse Core Ops, SparseCore 0:
  42.1 153.0 all-gather.1
  293.2 232.1 reduce-scatter.1
